TPU v7x, 128 devices: a whole 4x4x4 slice. The times are simulated.
128 devices in a mesh: outer: 16 (over x, z), inner: 8 (over y, core).
Axes of the slice: x: 4, y: 4, z: 4, core: 2. Of those that a mesh axis runs over, the one named last changes fastest.
Arguments:
- queries: bfloat16 [16384, 4096], P(('outer', 'inner')), may hold values from -170 to 170
- keys: bfloat16 [16384, 4096], P(('outer', 'inner')), may hold values from -170 to 170
- values: bfloat16 [16384, 4096], P(('outer', 'inner')), may hold values from -5 to 5
- teacher: bfloat16 [16384, 4096], P(('outer', 'inner')), may hold values from -12 to 12
- query_map: bfloat16 [32, 64, 128], replicated, may hold values from -0.5 to 0.5
- key_map: bfloat16 [32, 64, 128], replicated, may hold values from -0.5 to 0.5
Outputs:
- attn_out: bfloat16 [16384, 4096], P(('outer', 'inner'))
- loss: float32 [], replicated
- grad_query_map: float32 [32, 64, 128], replicated
- grad_key_map: float32 [32, 64, 128], replicated
All inputs are finite; a program needn't handle non-finite values.
Results may differ from a plain program's by a relative error of at most 0.011.
Values sent between devices are 32-bit elements; how exact they have to be, the bound alone decides.
No kernel may reach another device: no remote copies, remote signals or barrier semaphores. Data moves between devices by JAX's collectives and lax.ppermute only.
A program may use at most 512 MiB of HBM per device.

v0:
```python
import jax
import jax.numpy as jnp
from jax import lax
from jax.sharding import PartitionSpec as P

hp = lax.Precision.HIGHEST


def carried_in(part, axis, combine, identity, reverse):
    count = lax.axis_size(axis)
    place = lax.axis_index(axis)
    ahead = count - 1 - place if reverse else place
    gathered = jax.tree.map(lambda a: lax.all_gather(a, axis), part)
    state = jax.tree.map(lambda a, e: jnp.zeros_like(a) + jnp.asarray(e, a.dtype), part, identity)

    def one(turn, state):
        source = count - 1 - turn if reverse else turn
        return combine(
            state, jax.tree.map(lambda a: lax.dynamic_index_in_dim(a, source, 0, False), gathered)
        )

    return lax.fori_loop(0, ahead, one, state)


def from_root(x, axis, root):
    mine = lax.axis_index(axis) == root
    return lax.psum(jnp.where(mine, x, jnp.zeros_like(x)), axis)


def feature_map(x, w):
    logits = jnp.einsum("thd,hfd->thf", x, w, preferred_element_type=jnp.float32)
    first = jax.nn.softmax(logits, axis=-1)
    second = jax.nn.softmax(-logits, axis=-1)
    return (jnp.concatenate([first, second], axis=-1), first, second)


def soft_back(dphi, first, second, x):
    half = first.shape[-1]
    part_one = dphi[..., :half]
    part_two = dphi[..., half:]
    grad_logit = first * (part_one - jnp.sum(first * part_one, -1, keepdims=True))
    grad_logit = grad_logit - second * (part_two - jnp.sum(second * part_two, -1, keepdims=True))
    return jnp.einsum(
        "thf,thd->hfd", grad_logit.astype(jnp.bfloat16), x, preferred_element_type=jnp.float32
    )


def pair_add(left, right):
    return (left[0] + right[0], left[1] + right[1])


def forward_prefix(states):
    zeros = (jnp.zeros_like(states[0]), jnp.zeros_like(states[1]))
    within = carried_in(states, "inner", pair_add, zeros, False)
    inclusive = pair_add(within, states)
    block_total = (
        from_root(inclusive[0], "inner", lax.axis_size("inner") - 1),
        from_root(inclusive[1], "inner", lax.axis_size("inner") - 1),
    )
    before = carried_in(block_total, "outer", pair_add, zeros, False)
    return pair_add(before, within)


def backward_suffix(states):
    zeros = (jnp.zeros_like(states[0]), jnp.zeros_like(states[1]))
    within = carried_in(states, "inner", pair_add, zeros, True)
    inclusive = pair_add(within, states)
    block_total = (from_root(inclusive[0], "inner", 0), from_root(inclusive[1], "inner", 0))
    after = carried_in(block_total, "outer", pair_add, zeros, True)
    return pair_add(after, within)


def shards(queries, keys, values, teacher, query_map, key_map):
    rows = queries.shape[0]
    heads = query_map.shape[0]
    width = query_map.shape[2]
    x_query = queries.reshape(rows, heads, width)
    x_key = keys.reshape(rows, heads, width)
    val_rows = values.reshape(rows, heads, width)
    phiq, aq, bq = feature_map(x_query, query_map)
    phik, ak, bk = feature_map(x_key, key_map)
    phiqb = phiq.astype(jnp.bfloat16)
    phikb = phik.astype(jnp.bfloat16)
    state_loc = jnp.einsum("thf,thd->hfd", phikb, val_rows, preferred_element_type=jnp.float32)
    norm_loc = jnp.sum(phik, axis=0)
    state_pre, norm_pre = forward_prefix((state_loc, norm_loc))
    mask = lax.broadcasted_iota(jnp.int32, (rows, rows), 0) >= lax.broadcasted_iota(
        jnp.int32, (rows, rows), 1
    )
    scores = jnp.einsum("thf,shf->hts", phiqb, phikb, preferred_element_type=jnp.float32)
    scores = jnp.where(mask[None], scores, 0.0)
    scoresb = scores.astype(jnp.bfloat16)
    state_preb = state_pre.astype(jnp.bfloat16)
    num = jnp.einsum("hts,shd->thd", scoresb, val_rows, preferred_element_type=jnp.float32)
    num = num + jnp.einsum("thf,hfd->thd", phiqb, state_preb, preferred_element_type=jnp.float32)
    den = jnp.sum(scores, axis=2).T + jnp.einsum("thf,hf->th", phiq, norm_pre, precision=hp)
    y_full = num / den[..., None]
    attn_out = y_full.astype(jnp.bfloat16).reshape(rows, heads * width)
    err = y_full - teacher.reshape(rows, heads, width).astype(jnp.float32)
    grad_out = 2.0 / (heads * width) * err
    dnum = grad_out / den[..., None]
    dnumb = dnum.astype(jnp.bfloat16)
    dden = -jnp.sum(grad_out * y_full, axis=-1) / den
    rev_loc = jnp.einsum("thf,thd->hfd", phiqb, dnumb, preferred_element_type=jnp.float32)
    rnorm_loc = jnp.einsum("thf,th->hf", phiq, dden, precision=hp)
    rev_suf, rnorm_suf = backward_suffix((rev_loc, rnorm_loc))
    rev_sufb = rev_suf.astype(jnp.bfloat16)
    grid = (
        jnp.einsum("thd,shd->hts", dnumb, val_rows, preferred_element_type=jnp.float32)
        + dden.T[:, :, None]
    )
    gridb = jnp.where(mask[None], grid, 0.0).astype(jnp.bfloat16)
    dphiq = jnp.einsum("hts,shf->thf", gridb, phikb, preferred_element_type=jnp.float32)
    dphiq = dphiq + jnp.einsum(
        "thd,hfd->thf", dnumb, state_preb, preferred_element_type=jnp.float32
    )
    dphiq = dphiq + dden[..., None] * norm_pre[None]
    dphik = jnp.einsum("hts,thf->shf", gridb, phiqb, preferred_element_type=jnp.float32)
    dphik = dphik + jnp.einsum(
        "shd,hfd->shf", val_rows, rev_sufb, preferred_element_type=jnp.float32
    )
    dphik = dphik + rnorm_suf[None]
    grad_query = soft_back(dphiq, aq, bq, x_query)
    grad_key = soft_back(dphik, ak, bk, x_key)
    local_error = jnp.sum(err * err) / (heads * width)
    error_total, grad_query_map, grad_key_map = lax.psum(
        (local_error, grad_query, grad_key), ("outer", "inner")
    )
    all_rows = rows * lax.axis_size("outer") * lax.axis_size("inner")
    loss = error_total / all_rows
    return (attn_out, loss, grad_query_map, grad_key_map)


def solution(mesh):
    placed = (
        P(("outer", "inner"), None),
        P(("outer", "inner"), None),
        P(("outer", "inner"), None),
        P(("outer", "inner"), None),
        P(),
        P(),
    )
    return jax.shard_map(
        shards,
        mesh=mesh,
        in_specs=placed,
        out_specs=(P(("outer", "inner"), None), P(), P(), P()),
        check_vma=False,
    )
```

profile of v0, /device:TPU:1, one launch (start us, length us, event | category | flops | bytes accessed | tf_op | source)
XLA Modules:
  0.0 1063.8 jit_solution(6089463339698616725)
XLA Ops:
  19.9 14.6 %all-gather.1 = f32[256,128]{1,0:T(8,128)S(1)} all-gather(f32[32,128]{1,0:T(8,128)S(1)} %fusion.9), channel_id=3, replica_groups=mesh['outer'=16,'inner'=8] {'inner'}, dimensions={0}, use_global_device_ids=true | all-gather | bytes 147456 | tf_op jit(solution)/shard_map/all_gather | solution.py:13
  34.5 70.4 %all-gather.13.cloned.1.call-done = f32[256,128,128]{2,1,0:T(8,128)} async-done(((f32[32,128,128]{2,1,0:T(8,128)}), f32[256,128,128]{2,1,0:T(8,128)}) %all-gather.13.cloned.1.call-update) | async-done | bytes 16777232 | tf_op jit(solution)/shard_map/all_gather | solution.py:13
  109.2 3.9 select_bitcast_fusion.1
  113.2 76.1 %all-reduce.5.cloned.1.call-done = f32[1,32,128,128]{2,3,1,0:T(8,128)} async-done(((f32[1,32,128,128]{2,3,1,0:T(8,128)}), f32[1,32,128,128]{2,3,1,0:T(8,128)}) %all-reduce.5.cloned.1.call-update) | async-done | bytes 2097168 | tf_op jit(solution)/shard_map/psum | solution.py:27
  207.4 25.1 %psum.50 = f32[1,32,128]{2,1,0:T(8,128)S(1)} all-reduce(f32[1,32,128]{2,1,0:T(8,128)S(1)} %select_bitcast_fusion.3), channel_id=1, replica_groups=mesh['outer'=16,'inner'=8] {'inner'}, use_global_device_ids=true, to_apply=%region_12.13 | all-reduce | flops 4096 | bytes 32768 | tf_op jit(solution)/shard_map/psum | solution.py:27
  232.5 20.2 %all_gather.55 = f32[16,32,128]{2,1,0:T(8,128)S(1)} all-gather(f32[1,32,128]{2,1,0:T(8,128)S(1)} %psum.50), channel_id=1, replica_groups=mesh['outer'=16,'inner'=8] {'outer'}, dimensions={0}, use_global_device_ids=true | all-gather | bytes 278528 | tf_op jit(solution)/shard_map/all_gather | solution.py:13
  252.7 138.7 %all-gather.9.cloned.1.call-done = f32[16,32,128,128]{3,2,1,0:T(8,128)} async-done(((f32[1,32,128,128]{3,2,1,0:T(8,128)}), f32[16,32,128,128]{3,2,1,0:T(8,128)}) %all-gather.9.cloned.1.call-update) | async-done | bytes 33554448 | tf_op jit(solution)/shard_map/all_gather | solution.py:13
  412.6 13.4 %all-gather.3 = f32[256,128]{1,0:T(8,128)S(1)} all-gather(f32[32,128]{1,0:T(8,128)S(1)} %bitcast.183), channel_id=5, replica_groups=mesh['outer'=16,'inner'=8] {'inner'}, dimensions={0}, use_global_device_ids=true | all-gather | bytes 147456 | tf_op jit(solution)/shard_map/all_gather | solution.py:13
  426.1 123.0 %all-gather.15.cloned.1.call-done = f32[256,128,128]{2,1,0:T(8,128)} async-done(((f32[32,128,128]{2,1,0:T(8,128)}), f32[256,128,128]{2,1,0:T(8,128)}) %all-gather.15.cloned.1.call-update) | async-done | bytes 16777232 | tf_op jit(solution)/shard_map/all_gather | solution.py:13
  549.3 13.0 %while.54 = (s32[]{:T(128)}, f32[32,128,128]{2,1,0:T(8,128)S(1)}, f32[32,128]{1,0:T(8,128)S(1)}, s32[]{:T(128)}, f32[8,32,128,128]{3,2,1,0:T(8,128)}, /*index=5*...) while((s32[]{:T(128)}, f32[32,128,128]{2,1,0:T(8,128)S(1)}, ...), condition=%wide.region_23.24_spmd, body=%wide.region_22.23_spmd.sunk | while | flops 528390 | bytes 6340771 | solution.py:22
  564.1 3.9 select_bitcast_fusion
  568.1 64.5 %all-reduce.7.cloned.1.call-done = f32[1,32,128,128]{2,3,1,0:T(8,128)} async-done(((f32[1,32,128,128]{2,3,1,0:T(8,128)}), f32[1,32,128,128]{2,3,1,0:T(8,128)}) %all-reduce.7.cloned.1.call-update) | async-done | bytes 2097168 | tf_op jit(solution)/shard_map/psum | solution.py:27
  643.3 4.3 fusion.35
  647.6 4.1 fusion.90
  651.7 25.0 %psum.54 = f32[1,32,128]{2,1,0:T(8,128)S(1)} all-reduce(f32[1,32,128]{2,1,0:T(8,128)S(1)} %select_bitcast_fusion.2), channel_id=1, replica_groups=mesh['outer'=16,'inner'=8] {'inner'}, use_global_device_ids=true, to_apply=%region_25.26 | all-reduce | flops 4096 | bytes 32768 | tf_op jit(solution)/shard_map/psum | solution.py:27
  676.7 19.8 %all_gather.63 = f32[16,32,128]{2,1,0:T(8,128)S(1)} all-gather(f32[1,32,128]{2,1,0:T(8,128)S(1)} %psum.54), channel_id=1, replica_groups=mesh['outer'=16,'inner'=8] {'outer'}, dimensions={0}, use_global_device_ids=true | all-gather | bytes 278528 | tf_op jit(solution)/shard_map/all_gather | solution.py:13
  696.5 138.3 %all-gather.11.cloned.1.call-done = f32[16,32,128,128]{3,2,1,0:T(8,128)} async-done(((f32[1,32,128,128]{3,2,1,0:T(8,128)}), f32[16,32,128,128]{3,2,1,0:T(8,128)}) %all-gather.11.cloned.1.call-update) | async-done | bytes 33554448 | tf_op jit(solution)/shard_map/all_gather | solution.py:13
  836.4 59.0 %while.55 = (s32[]{:T(128)}, f32[32,128,128]{2,1,0:T(8,128)}, f32[32,128]{1,0:T(8,128)S(1)}, s32[]{:T(128)}, f32[16,32,128,128]{3,2,1,0:T(8,128)}, /*index=5*/f3...) while((s32[]{:T(128)}, f32[32,128,128]{2,1,0:T(8,128)}, f32[32,128]{1,0:T(8,128)S(1)}, ...), condition=%wide.region_27.28_spmd, body=%wide.region_26.27_spmd.sunk | while | flops 528390 | bytes 6340771 | solution.py:22
  836.4 3.9 bitcast_add_fusion.24
  840.4 3.9 bitcast_add_fusion.24
  844.3 3.9 bitcast_add_fusion.24
  848.2 3.9 bitcast_add_fusion.24
  852.2 3.9 bitcast_add_fusion.24
  856.1 3.9 bitcast_add_fusion.24
  860.0 3.9 bitcast_add_fusion.24
  864.0 3.9 bitcast_add_fusion.24
  867.9 3.9 bitcast_add_fusion.24
  871.8 3.9 bitcast_add_fusion.24
  879.7 3.9 bitcast_add_fusion.24
  891.5 3.9 bitcast_add_fusion.24
  905.6 64.8 %psum.51 = f32[]{:T(128)} all-reduce(f32[]{:T(128)S(6)} %div.68), channel_id=1, replica_groups=mesh['outer'=16,'inner'=8] {'outer','inner'}, use_global_device_ids=true, to_apply=%region_17.18 | all-reduce | flops 1 | bytes 8 | tf_op jit(solution)/shard_map/psum | solution.py:126
  972.3 80.1 %all-reduce.9.cloned.1.call-done = (f32[32,64,128]{2,1,0:T(8,128)}, f32[32,64,128]{2,1,0:T(8,128)}) async-done(((f32[32,64,128]{2,1,0:T(8,128)}, f32[32,64,128]{2,1,0:T(8,128)}), (f32[32,64,128]{2,1,0:T(8,128)}, f32[32,64,128]{2,1,0:T(8,128)})) %all-reduce.9.cloned.1.call-update) | async-done | bytes 2097168 | tf_op jit(solution)/shard_map/psum | solution.py:126
  (157 shorter events, 111.2 us)
Async XLA Ops:
  7.2 7.1 copy-start
  7.2 3.4 copy-start.28
  7.2 3.4 copy-start.24
  7.2 97.7 %all-gather.13.cloned.1.call-start = ((), (), s32[]{:S(2)}) async-start(), calls=%async_computation.4 | async-start | bytes 18874368 | tf_op jit(solution)/shard_map/all_gather | solution.py:13
  14.3 5.0 copy-start.2
  14.3 5.0 copy-start.9
  16.3 173.0 %all-reduce.5.cloned.1.call-start = ((), (), s32[]{:S(2)}) async-start(), calls=%async_computation | async-start | bytes 4194304 | tf_op jit(solution)/shard_map/psum | solution.py:27
  113.2 278.3 %all-gather.9.cloned.1.call-start = ((), (), s32[]{:S(2)}) async-start(), calls=%async_computation.1 | async-start | bytes 35651584 | tf_op jit(solution)/shard_map/all_gather | solution.py:13
  192.3 356.8 %all-gather.15.cloned.1.call-start = ((), (), s32[]{:S(2)}) async-start(), calls=%async_computation.5 | async-start | bytes 18874368 | tf_op jit(solution)/shard_map/all_gather | solution.py:13
  203.2 1.3 copy-start.12
  203.2 2.1 copy-start.3
  203.2 2.6 copy-start.10
  205.8 1.5 copy-start.14
  393.1 3.5 copy-start.1
  396.6 1.2 copy-start.15
  397.8 2.0 copy-start.23
  397.8 2.2 copy-start.29
  406.1 226.6 %all-reduce.7.cloned.1.call-start = ((), (), s32[]{:S(2)}) async-start(), calls=%async_computation.2 | async-start | bytes 4194304 | tf_op jit(solution)/shard_map/psum | solution.py:27
  406.2 3.1 copy-start.7
  406.2 3.1 copy-start.13
  568.1 266.7 %all-gather.11.cloned.1.call-start = ((), (), s32[]{:S(2)}) async-start(), calls=%async_computation.3 | async-start | bytes 35651584 | tf_op jit(solution)/shard_map/all_gather | solution.py:13
  635.6 416.8 %all-reduce.9.cloned.1.call-start = ((), (), s32[]{:S(2)}) async-start(), calls=%async_computation.6 | async-start | bytes 4194304 | tf_op jit(solution)/shard_map/psum | solution.py:126
  635.7 2.8 copy-start.4
  635.7 2.8 copy-start.11
  638.5 1.2 copy-start.17
  638.5 1.5 copy-start.22
  640.1 2.1 copy-start.8
  640.8 1.3 copy-start.18
  895.4 4.5 copy-start.5
  898.6 1.4 copy-start.19
  904.8 65.5 %copy-start.26 = (bf16[128,32,128]{0,2,1:T(8,128)(2,1)S(1)}, bf16[128,32,128]{0,2,1:T(8,128)(2,1)}, u32[]{:S(2)}) copy-start(bf16[128,32,128]{0,2,1:T(8,128)(2,1)} %get-tuple-element.351) | copy-start | bytes 3145732
  1052.5 2.4 copy-start.27
  (5 other events, 5.1 us)
Sparse Core Ops, SparseCore 0:
  16.4 88.5 all-gather.12
  113.3 75.9 all-reduce.4
  192.4 199.0 all-gather.8
  406.2 142.7 all-gather.14
  568.2 64.4 all-reduce.6
  635.8 199.0 all-gather.10
  905.0 147.4 all-reduce.8
where the time goes:
time: 1060 us
  waiting for transfers between devices  691 us (65%)
  blocking collectives  183 us (17%)
  other arithmetic  88.6 us (8%)
  matrix products  45.7 us (4%)
  local copies, waits for them, and re-layouts  37.7 us (4%)
  between operations  17 us (2%)
    all_gather x4, waiting for transfers between devices, carried_in(): gathered = jax.tree.map(lambda a: lax.all_gather(a, axis), part)  470 us
    psum x2, waiting for transfers between devices, from_root(): return lax.psum(jnp.where(mine, x, jnp.zeros_like(x)), axis)  141 us
    psum x1, waiting for transfers between devices, shards(): lax.psum((local_error, grad_query, grad_key), ('outer', 'inner'))  80.1 us
    add x46, other arithmetic, pair_add(): return (left[0] + right[0], left[1] + right[1])  74 us
    all_gather x4, blocking collectives, carried_in(): gathered = jax.tree.map(lambda a: lax.all_gather(a, axis), part)  68.1 us
    psum x1, blocking collectives, shards(): lax.psum((local_error, grad_query, grad_key), ('outer', 'inner'))  64.8 us
    psum x2, blocking collectives, from_root(): return lax.psum(jnp.where(mine, x, jnp.zeros_like(x)), axis)  50.1 us
  transfers between devices with their start and end apart: 7, of which 7 were waited for; matrix products, arithmetic and copies ran while one was open for 3% of the time, Pallas kernels for 0%

commit v1 on v0

v1 whole, which is shorter than its diff:
```python
import functools

import jax
import jax.numpy as jnp
from jax import lax
from jax.experimental import pallas as pl
from jax.experimental.pallas import tpu as pltpu
from jax.sharding import Mesh
from jax.sharding import PartitionSpec as P

F32 = jnp.float32
BF16 = jnp.bfloat16
CHIPS = ("x", "z", "y")
NCHIP = 64
HEADS = 32
HALF = 16
ROWS = 128
TOK = 256
GRP = 4
STEPS = HALF // GRP
PIECE = 33
GROWS = GRP * 4 * PIECE
ALL_ROWS = HALF * 4 * PIECE
WIDTH = 128


def dot(a, b, dims):
    return lax.dot_general(a, b, (dims, ((), ())), preferred_element_type=F32)


def low_lanes(shape):
    return lax.broadcasted_iota(jnp.int32, shape, 1) < 64


def halves_sum(x, low):
    first = jnp.sum(jnp.where(low, x, 0.0), axis=1, keepdims=True)
    second = jnp.sum(jnp.where(low, 0.0, x), axis=1, keepdims=True)
    return first, second


def feature_map(x, w):
    signed = jnp.concatenate([w, -w], axis=0)
    logits = dot(x, signed, ((1,), (1,)))
    low = low_lanes(logits.shape)
    big = jnp.float32(-3e38)
    top_one = jnp.max(jnp.where(low, logits, big), axis=1, keepdims=True)
    top_two = jnp.max(jnp.where(low, big, logits), axis=1, keepdims=True)
    e = jnp.exp(logits - jnp.where(low, top_one, top_two))
    sum_one, sum_two = halves_sum(e, low)
    return e * jnp.where(low, 1.0 / sum_one, 1.0 / sum_two)


def soft_back(phi, dphi, x):
    low = low_lanes(phi.shape)
    sum_one, sum_two = halves_sum(phi * dphi, low)
    d = phi * (dphi - jnp.where(low, sum_one, sum_two))
    dlogit = (d - pltpu.roll(d, 64, 1)).astype(BF16)
    return dot(dlogit, x, ((0,), (0,)))[:64]


def both_cores(core, own, other, buf):
    buf[pl.ds(pl.multiple_of(core * ROWS, ROWS), ROWS), :] = own
    buf[pl.ds(pl.multiple_of((1 - core) * ROWS, ROWS), ROWS), :] = other.astype(BF16)
    return buf[...]


def put_state(ref, i, state, row):
    for q in range(4):
        at = (4 * i + q) * PIECE
        ref[at : at + 32, :] = state[32 * q : 32 * q + 32]
        ref[at + 32 : at + 33, :] = row


def get_state(ref, i):
    parts = [ref[(4 * i + q) * PIECE : (4 * i + q) * PIECE + 32, :] for q in range(4)]
    at = 4 * i * PIECE + 32
    return jnp.concatenate(parts, axis=0), ref[at : at + 1, :]


def key_kernel(core_ref, k_own, k_other, v_own, v_other, w_ref, kf, vf, phik_ref, send, kbuf, vbuf):
    core = core_ref[0]
    for i in range(GRP):
        cols = slice(WIDTH * i, WIDTH * (i + 1))
        k = both_cores(core, k_own[:, cols], k_other[:, cols], kbuf.at[i])
        v = both_cores(core, v_own[:, cols], v_other[:, cols], vbuf.at[i])
        kf[:, cols] = k
        vf[:, cols] = v
        phik = feature_map(k, w_ref[i])
        phik_ref[:, cols] = phik
        state = dot(phik.astype(BF16), v, ((0,), (0,)))
        put_state(send, i, state, jnp.sum(phik, axis=0, keepdims=True))


def query_kernel(
    core_ref, q_own, q_other, t_own, t_other, w_ref, phik_ref, vf, pre,
    y_own, y_send, send, dphik_ref, grad_ref, loss_ref, qbuf, tbuf, ybuf,
):
    core = core_ref[0]

    @pl.when(pl.program_id(0) == 0)
    def _():
        loss_ref[...] = jnp.zeros_like(loss_ref)

    mask = lax.broadcasted_iota(jnp.int32, (TOK, TOK), 0) >= lax.broadcasted_iota(
        jnp.int32, (TOK, TOK), 1
    )
    mine = pl.ds(pl.multiple_of(core * ROWS, ROWS), ROWS)
    theirs = pl.ds(pl.multiple_of((1 - core) * ROWS, ROWS), ROWS)
    scale = 2.0 / (HEADS * WIDTH)
    for i in range(GRP):
        cols = slice(WIDTH * i, WIDTH * (i + 1))
        q = both_cores(core, q_own[:, cols], q_other[:, cols], qbuf.at[i])
        t = both_cores(core, t_own[:, cols], t_other[:, cols], tbuf.at[i])
        v = vf[:, cols]
        phikb = phik_ref[:, cols].astype(BF16)
        state, norm = get_state(pre, i)
        stateb = state.astype(BF16)
        phiq = feature_map(q, w_ref[i])
        phiqb = phiq.astype(BF16)
        scores = jnp.where(mask, dot(phiqb, phikb, ((1,), (1,))), 0.0)
        num = dot(scores.astype(BF16), v, ((1,), (0,))) + dot(phiqb, stateb, ((1,), (0,)))
        den = jnp.sum(
            scores[:, :WIDTH] + scores[:, WIDTH:] + phiq * norm, axis=1, keepdims=True
        )
        inv = 1.0 / den
        y = num * inv
        ybuf[i] = y
        y_own[:, cols] = ybuf[i, mine, :].astype(BF16)
        y_send[:, cols] = ybuf[i, theirs, :]
        err = y - t.astype(F32)
        loss_ref[...] += jnp.sum((err * err).reshape(TOK // 8, 8, WIDTH), axis=0)
        g = scale * err
        dnumb = (g * inv).astype(BF16)
        dden = -jnp.sum(g * y, axis=1, keepdims=True) * inv
        rev = dot(phiqb, dnumb, ((0,), (0,)))
        put_state(send, i, rev, jnp.sum(phiq * dden, axis=0, keepdims=True))
        grid = jnp.where(mask, dot(dnumb, v, ((1,), (1,))) + dden, 0.0)
        gridb = grid.astype(BF16)
        dphiq = dot(gridb, phikb, ((1,), (0,))) + dot(dnumb, stateb, ((1,), (1,)))
        dphiq = dphiq + dden * norm
        dphik_ref[:, cols] = dot(gridb, phiqb, ((0,), (0,)))
        grad_ref[64 * i : 64 * (i + 1), :] = soft_back(phiq, dphiq, q)


def final_kernel(kf, vf, phik_ref, dphik_ref, suf, grad_ref, loss_ref, send):
    row = jnp.sum(loss_ref[...], axis=0, keepdims=True)
    for i in range(GRP):
        cols = slice(WIDTH * i, WIDTH * (i + 1))
        state, norm = get_state(suf, i)
        dphik = dphik_ref[:, cols] + dot(vf[:, cols], state.astype(BF16), ((1,), (1,))) + norm
        grad_key = soft_back(phik_ref[:, cols], dphik, kf[:, cols])
        both = jnp.concatenate([grad_ref[64 * i : 64 * (i + 1), :], grad_key], axis=0)
        put_state(send, i, both, row)


SCAN_STEPS = 4
SCAN_PIECES = NCHIP // SCAN_STEPS
SCAN_ROWS = SCAN_PIECES * PIECE


def scan_kernel(x_ref, o_ref, acc_ref, *, reverse):
    @pl.when(pl.program_id(0) == 0)
    def _():
        acc_ref[...] = jnp.zeros_like(acc_ref)

    acc = acc_ref[...]
    order = range(SCAN_PIECES)
    for j in reversed(order) if reverse else order:
        o_ref[PIECE * j : PIECE * (j + 1), :] = acc
        acc = acc + x_ref[PIECE * j : PIECE * (j + 1), :]
    acc_ref[...] = acc


def sum_kernel(x_ref, o_ref):
    acc = x_ref[0:PIECE, :]
    for j in range(1, NCHIP):
        acc = acc + x_ref[PIECE * j : PIECE * (j + 1), :]
    for j in range(NCHIP):
        o_ref[PIECE * j : PIECE * (j + 1), :] = acc


def unpack_kernel(core_ref, mine, theirs, gq, gk, loss_ref):
    core = core_ref[0]
    half = pl.program_id(0)
    total = jnp.sum(mine[32:33, :] + theirs[32:33, :], keepdims=True)
    loss_ref[...] = total.reshape(1, 1) * (1.0 / (HEADS * WIDTH) / (NCHIP * TOK))

    def put(src):
        for i in range(HALF):
            for q in range(4):
                at = (4 * i + q) * PIECE
                dst = gq if q < 2 else gk
                dst[i, 32 * (q % 2) : 32 * (q % 2) + 32, :] = src[at : at + 32, :]

    @pl.when(half == core)
    def _():
        put(mine)

    @pl.when(half != core)
    def _():
        put(theirs)


def merge_kernel(core_ref, own, other, out):
    core = core_ref[0]

    @pl.when(pl.program_id(0) == core)
    def _():
        out[...] = own[...]

    @pl.when(pl.program_id(0) != core)
    def _():
        out[...] = other[...].astype(BF16)


def call(body, core, args, in_specs, outs, out_specs, scratch=(), steps=STEPS, name=None):
    spec = pltpu.PrefetchScalarGridSpec(
        num_scalar_prefetch=0 if core is None else 1,
        grid=(steps,),
        in_specs=in_specs,
        out_specs=out_specs,
        scratch_shapes=list(scratch),
    )
    lead = () if core is None else (core,)
    return pl.pallas_call(body, grid_spec=spec, out_shape=outs, name=name)(*lead, *args)


def sds(shape, dtype=F32):
    return jax.ShapeDtypeStruct(shape, dtype)


def exchange(x):
    pieces = lax.all_to_all(x.reshape(NCHIP, 1, PIECE * WIDTH), CHIPS, 0, 0, tiled=True)
    return pieces.reshape(ALL_ROWS, WIDTH)


def scan(x, reverse):
    at = (lambda g: (SCAN_STEPS - 1 - g, 0)) if reverse else (lambda g: (g, 0))
    spec = pl.BlockSpec((SCAN_ROWS, WIDTH), at)
    return call(
        functools.partial(scan_kernel, reverse=reverse),
        None, (x,), [spec], sds((ALL_ROWS, WIDTH)), spec,
        [pltpu.VMEM((PIECE, WIDTH), F32)], SCAN_STEPS, "scan",
    )


def swap(x):
    return lax.ppermute(x, "c", [(0, 1), (1, 0)])


def shards(queries, keys, values, teacher, query_map, key_map):
    c = lax.axis_index("c").astype(jnp.int32)
    core = c.reshape(1)
    half = HALF * WIDTH
    gcols = GRP * WIDTH

    def others(x):
        part = lax.dynamic_slice(x, (0, (1 - c) * half), (ROWS, half))
        return swap(part.astype(F32))

    k_other, v_other = others(keys), others(values)
    q_other, t_other = others(queries), others(teacher)

    own = pl.BlockSpec((ROWS, gcols), lambda g, c: (0, c[0] * STEPS + g))
    other = pl.BlockSpec((ROWS, gcols), lambda g, c: (0, g))
    weight = pl.BlockSpec((GRP, 64, WIDTH), lambda g, c: (c[0] * STEPS + g, 0, 0))
    full = pl.BlockSpec((TOK, gcols), lambda g, *c: (0, g))
    pieces = pl.BlockSpec((GROWS, WIDTH), lambda g, *c: (g, 0))
    grads = pl.BlockSpec((GRP * 64, WIDTH), lambda g, *c: (g, 0))
    lossy = pl.BlockSpec((8, WIDTH), lambda g, *c: (0, 0))
    payload = sds((ALL_ROWS, WIDTH))
    buf = pltpu.VMEM((GRP, TOK, WIDTH), BF16)

    kf, vf, phik, send = call(
        key_kernel, core, (keys, k_other, values, v_other, key_map),
        [own, other, own, other, weight],
        (sds((TOK, half), BF16), sds((TOK, half), BF16), sds((TOK, half)), payload),
        (full, full, full, pieces), [buf, buf], name="keys",
    )
    pre = exchange(scan(exchange(send), False))
    y_own, y_send, send, dphik, grad_query, loss = call(
        query_kernel, core,
        (queries, q_other, teacher, t_other, query_map, phik, vf, pre),
        [own, other, own, other, weight, full, full, pieces],
        (
            sds((ROWS, half), BF16), sds((ROWS, half)), payload, sds((TOK, half)),
            sds((HALF * 64, WIDTH)), sds((8, WIDTH)),
        ),
        (other, other, pieces, full, grads, lossy),
        [buf, buf, pltpu.VMEM((GRP, TOK, WIDTH), F32)], name="queries",
    )
    y_other = swap(y_send)
    suf = exchange(scan(exchange(send), True))
    send = call(
        final_kernel, None, (kf, vf, phik, dphik, suf, grad_query, loss),
        [full, full, full, full, pieces, grads, lossy], payload, pieces, name="final",
    )
    whole = pl.BlockSpec((ALL_ROWS, WIDTH), lambda g, *c: (0, 0))
    spread = call(
        sum_kernel, None, (exchange(send),), [whole], payload, whole, steps=1, name="sum"
    )
    mine = exchange(spread)
    theirs = swap(mine)
    gmap = pl.BlockSpec((HALF, 64, WIDTH), lambda g, c: (g, 0, 0))
    grad_query, grad_key, loss = call(
        unpack_kernel, core, (mine, theirs), [whole, whole],
        (sds((HEADS, 64, WIDTH)), sds((HEADS, 64, WIDTH)), sds((1, 1))),
        (gmap, gmap, pl.BlockSpec((1, 1), lambda g, c: (0, 0))), steps=2, name="unpack",
    )
    wide = pl.BlockSpec((ROWS, half), lambda g, c: (0, 0))
    attn = call(
        merge_kernel, core, (y_own, y_other), [wide, wide],
        sds((ROWS, HEADS * WIDTH), BF16),
        pl.BlockSpec((ROWS, half), lambda g, c: (0, g)), steps=2, name="merge",
    )
    return attn, loss[0, 0], grad_query, grad_key


def solution(mesh):
    fine = Mesh(mesh.devices.reshape(4, 4, 4, 2), ("x", "z", "y", "c"))
    tokens = P(("x", "z", "y", "c"), None)
    return jax.shard_map(
        shards,
        mesh=fine,
        in_specs=(tokens, tokens, tokens, tokens, P(), P()),
        out_specs=(tokens, P(), P(), P()),
        check_vma=False,
    )
```

time: 1060 us -> 208 us (0.20)
  waiting for transfers between devices: 691 us -> 37.5 us
  blocking collectives: 183 us -> 85 us
  other arithmetic: 88.6 us -> 2.5 us
  Pallas kernels: 0 us -> 50.1 us
  matrix products: 45.7 us -> 0 us
  local copies, waits for them, and re-layouts: 37.7 us -> 4.92 us
  starting transfers between devices: 0.29 us -> 26.2 us
  between operations: 17 us -> 0.73 us
    all_gather x4 -> x0, waiting for transfers between devices: 470 us -> none  [carried_in(): gathered = jax.tree.map(lambda a: lax.all_gather(a, axis), part)]
    psum x3 -> x0, waiting for transfers between devices: 221 us -> none  [the longest x2 141 us: from_root(): return lax.psum(jnp.where(mine, x, jnp.zeros_like(x)), axis)]
    psum x3 -> x0, blocking collectives: 115 us -> none  [the longest x1 64.8 us: shards(): lax.psum((local_error, grad_query, grad_key), ('outer', 'inner'))]
    all_to_all x0 -> x4, blocking collectives: none -> 85 us  [exchange(): lax.all_to_all(x.reshape(NCHIP, 1, PIECE * WIDTH), CHIPS, 0, 0, tiled=True)]
    add x47 -> x0, other arithmetic: 74 us -> none  [the longest x46 74 us: pair_add(): return (left[0] + right[0], left[1] + right[1])]
    all_gather x4 -> x0, blocking collectives: 68.1 us -> none  [carried_in(): gathered = jax.tree.map(lambda a: lax.all_gather(a, axis), part)]
    pallas_call x0 -> x8, Pallas kernels: none -> 50.1 us  [call(): pl.pallas_call(body, grid_spec=spec, out_shape=outs, name=name)]
    dot_general x14 -> x0, matrix products: 34.1 us -> none  [the longest x2 7.88 us: soft_back(): jnp.einsum('thf,thd->hfd', grad_logit.astype(jnp.bfloat16), x, preferred_...]
  transfers between devices with their start and end apart: 7 -> 8, of which waited for: 7 -> 6; matrix products, arithmetic and copies ran while one was open for 3% -> 1% of each run, Pallas kernels for 0% -> 3%
where the time goes in v1:
time: 208 us; the launch traced here: 207 us
  blocking collectives  85 us (41%)
  Pallas kernels  50.1 us (24%)
  waiting for transfers between devices  37.5 us (18%)
  starting transfers between devices  26.2 us (13%)
  local copies, waits for them, and re-layouts  4.92 us (2%)
  other arithmetic  2.5 us (1%)
    all_to_all x4, blocking collectives, exchange(): lax.all_to_all(x.reshape(NCHIP, 1, PIECE * WIDTH), CHIPS, 0, 0, tiled=True)  85 us
    pallas_call x8, Pallas kernels, call(): pl.pallas_call(body, grid_spec=spec, out_shape=outs, name=name)  50.1 us
    all_to_all x2, waiting for transfers between devices, exchange(): lax.all_to_all(x.reshape(NCHIP, 1, PIECE * WIDTH), CHIPS, 0, 0, tiled=True)  27.9 us
    all_to_all x2, starting transfers between devices, exchange(): lax.all_to_all(x.reshape(NCHIP, 1, PIECE * WIDTH), CHIPS, 0, 0, tiled=True)  17.2 us
    ppermute x6, waiting for transfers between devices, swap(): return lax.ppermute(x, 'c', [(0, 1), (1, 0)])  9.58 us
    ppermute x6, starting transfers between devices, swap(): return lax.ppermute(x, 'c', [(0, 1), (1, 0)])  8.99 us
    unnamed x26, local copies, waits for them, and re-layouts  4.92 us
  transfers between devices with their start and end apart: 8, of which 6 were waited for; matrix products, arithmetic and copies ran while one was open for 1% of the time, Pallas kernels for 3%

profile of v1, /device:TPU:1, one launch (start us, length us, event | category | flops | bytes accessed | tf_op | source)
XLA Modules:
  0.0 206.9 jit_solution(14184498376924160307)
XLA Ops:
  0.6 1.2 dynamic-slice_convert_fusion
  1.9 1.5 collective-permute-start.3
  3.5 0.1 collective-permute-start.2
  3.6 2.1 collective-permute-done.3.v_other
  5.6 1.5 collective-permute-done.2.k_other
  7.1 1.0 copy-done.10
  8.1 7.3 %keys.1 = (bf16[256,2048]{1,0:T(8,128)(2,1)}, bf16[256,2048]{1,0:T(8,128)(2,1)}, f32[256,2048]{1,0:T(8,128)}, f32[2112,128]{1,0:T(8,128)}) custom-call(s32[1]{0:T(128)} %bitcast.core_ref, bf16[128,4096]{1,0:T(8,128)(2,1)} %k_own.1, f32[128,2048]{1,0:T(8,128)} %copy-done.10, bf16[128,4096]{1,0:T(8,128)(2,1)} %v_own.1, f32[128,2048]{1,0:T(8,128)} %copy-done.9, ...), custom_call_target="tpu_custom_call" | custom-call | tf_op jit(solution)/shard_map/keys/pallas_call | solution.py:225
  15.4 11.4 %all-to-all-start = ((f32[64,1,4224]{2,1,0:T(1,128)}), f32[64,1,4224]{2,1,0:T(1,128)S(1)}, u32[]{:S(2)}, u32[]{:S(2)}) async-start(f32[64,1,4224]{2,1,0:T(1,128)} %bitcast.25), calls=%async_computation | async-start | bytes 2162688 | tf_op jit(solution)/shard_map/all_to_all | solution.py:233
  26.8 1.1 dynamic-slice_convert_fusion.2
  27.9 0.7 collective-permute-start.1
  28.6 15.6 %all-to-all-done = f32[64,1,4224]{2,1,0:T(1,128)S(1)} async-done(((f32[64,1,4224]{2,1,0:T(1,128)}), f32[64,1,4224]{2,1,0:T(1,128)S(1)}, u32[]{:S(2)}, u32[]{:S(2)}) %all-to-all-start) | async-done | bytes 1081376 | tf_op jit(solution)/shard_map/all_to_all | solution.py:233
  44.2 1.0 copy-done.2
  45.2 3.4 %scan.2 = f32[2112,128]{1,0:T(8,128)} custom-call(f32[2112,128]{1,0:T(8,128)} %bitcast.18), custom_call_target="tpu_custom_call" | custom-call | tf_op jit(solution)/shard_map/scan/pallas_call | solution.py:225
  48.6 5.8 %all-to-all-start.1 = ((f32[64,1,4224]{2,1,0:T(1,128)}), f32[64,1,4224]{2,1,0:T(1,128)S(1)}, u32[]{:S(2)}, u32[]{:S(2)}) async-start(f32[64,1,4224]{2,1,0:T(1,128)} %bitcast.17), calls=%async_computation.1 | async-start | bytes 2162688 | tf_op jit(solution)/shard_map/all_to_all | solution.py:233
  54.5 1.8 collective-permute-start
  56.3 2.3 %collective-permute-done.q_other = f32[128,2048]{1,0:T(8,128)S(1)} collective-permute-done((f32[128,2048]{1,0:T(8,128)S(1)}, f32[128,2048]{1,0:T(8,128)S(1)}, u32[]{:S(2)}, u32[]{:S(2)}) %collective-permute-start) | collective-permute-done | bytes 1048608 | tf_op jit(solution)/shard_map/ppermute | solution.py:248
  58.5 12.3 %all-to-all-done.1 = f32[64,1,4224]{2,1,0:T(1,128)S(1)} async-done(((f32[64,1,4224]{2,1,0:T(1,128)}), f32[64,1,4224]{2,1,0:T(1,128)S(1)}, u32[]{:S(2)}, u32[]{:S(2)}) %all-to-all-start.1) | async-done | bytes 1081376 | tf_op jit(solution)/shard_map/all_to_all | solution.py:233
  70.8 1.0 copy-done
  71.8 20.2 %queries.1 = (bf16[128,2048]{1,0:T(8,128)(2,1)}, f32[128,2048]{1,0:T(8,128)}, f32[2112,128]{1,0:T(8,128)}, f32[256,2048]{1,0:T(8,128)}, f32[1024,128]{1,0:T(8,128)}, /*index=5*/f32[8,128]{1,0:T(8,128)}) custom-call(s32[1]{0:T(128)} %bitcast.core_ref, bf16[128,4096]{1,0:T(8,128)(2,1)} %q_own.1, f32[128,2048]{1,0:T(8,128)} %copy-done.8, ...), custom_call_target="tpu_custom_call" | custom-call | tf_op jit(solution)/shard_map/queries/pallas_call | solution.py:225
  92.0 22.4 %all_to_all.30 = f32[64,1,4224]{2,1,0:T(1,128)} all-to-all(f32[64,1,4224]{2,1,0:T(1,128)} %bitcast.26), channel_id=1, replica_groups=mesh['x'=4,'z'=4,'y'=4,'c'=2] {'x','z','y'}, dimensions={0} | all-to-all | bytes 2162688 | tf_op jit(solution)/shard_map/all_to_all | solution.py:233
  114.4 3.4 %scan.3 = f32[2112,128]{1,0:T(8,128)} custom-call(f32[2112,128]{1,0:T(8,128)} %bitcast.19), custom_call_target="tpu_custom_call" | custom-call | tf_op jit(solution)/shard_map/scan/pallas_call | solution.py:225
  117.8 21.4 %all_to_all.31 = f32[64,1,4224]{2,1,0:T(1,128)} all-to-all(f32[64,1,4224]{2,1,0:T(1,128)} %bitcast.20), channel_id=1, replica_groups=mesh['x'=4,'z'=4,'y'=4,'c'=2] {'x','z','y'}, dimensions={0} | all-to-all | bytes 2162688 | tf_op jit(solution)/shard_map/all_to_all | solution.py:233
  139.2 7.9 %final.1 = f32[2112,128]{1,0:T(8,128)} custom-call(bf16[256,2048]{1,0:T(8,128)(2,1)} %get-tuple-element.22.kf, bf16[256,2048]{1,0:T(8,128)(2,1)} %get-tuple-element.18.vf, f32[256,2048]{1,0:T(8,128)} %get-tuple-element.17.phik_ref, f32[256,2048]{1,0:T(8,128)} %get-tuple-element.23.dphik_ref, f32[2112,128]{1,0:T(8,128)} %bitcast.23, ...), custom_call_target="tpu_custom_call" | custom-call | tf_op jit(solution)/shard_map/final/pallas_call | solution.py:225
  147.1 20.7 %all_to_all.32 = f32[64,1,4224]{2,1,0:T(1,128)} all-to-all(f32[64,1,4224]{2,1,0:T(1,128)} %bitcast.24), channel_id=1, replica_groups=mesh['x'=4,'z'=4,'y'=4,'c'=2] {'x','z','y'}, dimensions={0} | all-to-all | bytes 2162688 | tf_op jit(solution)/shard_map/all_to_all | solution.py:233
  167.8 2.4 %sum.1 = f32[2112,128]{1,0:T(8,128)} custom-call(f32[2112,128]{1,0:T(8,128)} %bitcast.21), custom_call_target="tpu_custom_call" | custom-call | tf_op jit(solution)/shard_map/sum/pallas_call | solution.py:225
  170.2 20.5 %all_to_all.33 = f32[64,1,4224]{2,1,0:T(1,128)S(1)} all-to-all(f32[64,1,4224]{2,1,0:T(1,128)} %bitcast.22), channel_id=1, replica_groups=mesh['x'=4,'z'=4,'y'=4,'c'=2] {'x','z','y'}, dimensions={0} | all-to-all | bytes 2162688 | tf_op jit(solution)/shard_map/all_to_all | solution.py:233
  190.7 4.9 %collective-permute-start.5 = (f32[2112,128]{1,0:T(8,128)S(1)}, f32[2112,128]{1,0:T(8,128)S(1)}, u32[]{:S(2)}, u32[]{:S(2)}) collective-permute-start(f32[2112,128]{1,0:T(8,128)S(1)} %bitcast.15), channel_id=1, source_target_pairs={{0,1},{1,0},{2,3},{3,2},{4,5},{5,4},{6,7},{7,6},{8,9},{9,8},{10,11... | collective-permute-start | bytes 3244040 | tf_op jit(solution)/shard_map/ppermute | solution.py:248
  195.7 3.7 %collective-permute-done.4.other = f32[128,2048]{1,0:T(8,128)S(1)} collective-permute-done((f32[128,2048]{1,0:T(8,128)S(1)}, f32[128,2048]{1,0:T(8,128)S(1)}, u32[]{:S(2)}, u32[]{:S(2)}) %collective-permute-start.4) | collective-permute-done | bytes 1048608 | tf_op jit(solution)/shard_map/ppermute | solution.py:248
  199.5 1.0 copy-done.11
  200.4 2.4 %merge.1 = bf16[128,4096]{1,0:T(8,128)(2,1)} custom-call(s32[1]{0:T(128)} %bitcast.core_ref, bf16[128,2048]{1,0:T(8,128)(2,1)} %get-tuple-element.20.own, f32[128,2048]{1,0:T(8,128)} %copy-done.11), custom_call_target="tpu_custom_call" | custom-call | tf_op jit(solution)/shard_map/merge/pallas_call | solution.py:225
  202.8 1.0 copy-done.6
  203.8 3.1 %unpack.1 = (f32[32,64,128]{2,1,0:T(8,128)}, f32[32,64,128]{2,1,0:T(8,128)}, f32[1,1]{1,0:T(1,128)}) custom-call(s32[1]{0:T(128)} %bitcast.core_ref, f32[2112,128]{1,0:T(8,128)} %bitcast.16, f32[2112,128]{1,0:T(8,128)} %copy-done.6), custom_call_target="tpu_custom_call" | custom-call | tf_op jit(solution)/shard_map/unpack/pallas_call | solution.py:225
  (26 shorter events, 0.3 us)
Async XLA Ops:
  0.6 2.7 %copy-start.3 = (bf16[128,4096]{1,0:T(8,128)(2,1)S(1)}, bf16[128,4096]{1,0:T(8,128)(2,1)}, u32[]{:S(2)}) copy-start(bf16[128,4096]{1,0:T(8,128)(2,1)} %k_own.1) | copy-start | bytes 3145732
  1.9 3.7 %collective-permute-start.3 = (f32[128,2048]{1,0:T(8,128)S(1)}, f32[128,2048]{1,0:T(8,128)S(1)}, u32[]{:S(2)}, u32[]{:S(2)}) collective-permute-start(f32[128,2048]{1,0:T(8,128)S(1)} %dynamic-slice_convert_fusion), channel_id=1, source_target_pairs={{0,1},{1,0},{2,3},{3,2},{4,5},{5,4},{6,7},{7,6},{8,9},{9,8},{10,11... | collective-permute-start | bytes 3145736 | tf_op jit(solution)/shard_map/ppermute | solution.py:248
  3.5 3.7 %collective-permute-start.2 = (f32[128,2048]{1,0:T(8,128)S(1)}, f32[128,2048]{1,0:T(8,128)S(1)}, u32[]{:S(2)}, u32[]{:S(2)}) collective-permute-start(f32[128,2048]{1,0:T(8,128)S(1)} %dynamic-slice_convert_fusion.1), channel_id=1, source_target_pairs={{0,1},{1,0},{2,3},{3,2},{4,5},{5,4},{6,7},{7,6},{8,9},{9,8},{10,11... | collective-permute-start | bytes 3145736 | tf_op jit(solution)/shard_map/ppermute | solution.py:248
  5.6 1.5 copy-start.9
  7.1 1.0 copy-start.10
  15.4 11.4 %copy-start.5 = (bf16[128,4096]{1,0:T(8,128)(2,1)S(1)}, bf16[128,4096]{1,0:T(8,128)(2,1)}, u32[]{:S(2)}) copy-start(bf16[128,4096]{1,0:T(8,128)(2,1)} %t_own.1) | copy-start | bytes 3145732
  15.4 28.7 %all-to-all-start = ((f32[64,1,4224]{2,1,0:T(1,128)}), f32[64,1,4224]{2,1,0:T(1,128)S(1)}, u32[]{:S(2)}, u32[]{:S(2)}) async-start(f32[64,1,4224]{2,1,0:T(1,128)} %bitcast.25), calls=%async_computation | async-start | bytes 2162688 | tf_op jit(solution)/shard_map/all_to_all | solution.py:233
  27.9 28.3 %collective-permute-start.1 = (f32[128,2048]{1,0:T(8,128)}, f32[128,2048]{1,0:T(8,128)S(1)}, u32[]{:S(2)}, u32[]{:S(2)}) collective-permute-start(f32[128,2048]{1,0:T(8,128)} %dynamic-slice_convert_fusion.2), channel_id=1, source_target_pairs={{0,1},{1,0},{2,3},{3,2},{4,5},{5,4},{6,7},{7,6},{8,9},{9,8},{10,11... | collective-permute-start | bytes 3145736 | tf_op jit(solution)/shard_map/ppermute | solution.py:248
  44.2 1.0 copy-start.2
  48.6 5.8 %copy-start.4 = (bf16[128,4096]{1,0:T(8,128)(2,1)S(1)}, bf16[128,4096]{1,0:T(8,128)(2,1)}, u32[]{:S(2)}) copy-start(bf16[128,4096]{1,0:T(8,128)(2,1)} %q_own.1) | copy-start | bytes 3145732
  48.6 22.3 %all-to-all-start.1 = ((f32[64,1,4224]{2,1,0:T(1,128)}), f32[64,1,4224]{2,1,0:T(1,128)S(1)}, u32[]{:S(2)}, u32[]{:S(2)}) async-start(f32[64,1,4224]{2,1,0:T(1,128)} %bitcast.17), calls=%async_computation.1 | async-start | bytes 2162688 | tf_op jit(solution)/shard_map/all_to_all | solution.py:233
  54.5 4.0 %collective-permute-start = (f32[128,2048]{1,0:T(8,128)S(1)}, f32[128,2048]{1,0:T(8,128)S(1)}, u32[]{:S(2)}, u32[]{:S(2)}) collective-permute-start(f32[128,2048]{1,0:T(8,128)S(1)} %dynamic-slice_convert_fusion.3), channel_id=1, source_target_pairs={{0,1},{1,0},{2,3},{3,2},{4,5},{5,4},{6,7},{7,6},{8,9},{9,8},{10,11... | collective-permute-start | bytes 3145736 | tf_op jit(solution)/shard_map/ppermute | solution.py:248
  56.3 14.6 %copy-start.7 = (f32[128,2048]{1,0:T(8,128)}, f32[128,2048]{1,0:T(8,128)S(1)}, u32[]{:S(2)}) copy-start(f32[128,2048]{1,0:T(8,128)S(1)} %collective-permute-done.1.t_other) | copy-start | bytes 3145732
  58.5 12.3 %copy-start.8 = (f32[128,2048]{1,0:T(8,128)}, f32[128,2048]{1,0:T(8,128)S(1)}, u32[]{:S(2)}) copy-start(f32[128,2048]{1,0:T(8,128)S(1)} %collective-permute-done.q_other) | copy-start | bytes 3145732
  70.8 1.0 copy-start
  170.2 25.4 %copy-start.12 = (f32[128,2048]{1,0:T(8,128)S(1)}, f32[128,2048]{1,0:T(8,128)}, u32[]{:S(2)}) copy-start(f32[128,2048]{1,0:T(8,128)} %get-tuple-element.21) | copy-start | bytes 3145732
  190.7 12.1 %copy-start.1 = (f32[64,1,4224]{2,1,0:T(1,128)}, f32[64,1,4224]{2,1,0:T(1,128)S(1)}, u32[]{:S(2)}) copy-start(f32[64,1,4224]{2,1,0:T(1,128)S(1)} %all_to_all.33) | copy-start | bytes 3244036
  190.7 12.1 %collective-permute-start.5 = (f32[2112,128]{1,0:T(8,128)S(1)}, f32[2112,128]{1,0:T(8,128)S(1)}, u32[]{:S(2)}, u32[]{:S(2)}) collective-permute-start(f32[2112,128]{1,0:T(8,128)S(1)} %bitcast.15), channel_id=1, source_target_pairs={{0,1},{1,0},{2,3},{3,2},{4,5},{5,4},{6,7},{7,6},{8,9},{9,8},{10,11... | collective-permute-start | bytes 3244040 | tf_op jit(solution)/shard_map/ppermute | solution.py:248
  195.6 3.8 %collective-permute-start.4 = (f32[128,2048]{1,0:T(8,128)S(1)}, f32[128,2048]{1,0:T(8,128)S(1)}, u32[]{:S(2)}, u32[]{:S(2)}) collective-permute-start(f32[128,2048]{1,0:T(8,128)S(1)} %copy-done.12), channel_id=1, source_target_pairs={{0,1},{1,0},{2,3},{3,2},{4,5},{5,4},{6,7},{7,6},{8,9},{9,8},{10,11... | collective-permute-start | bytes 3145736 | tf_op jit(solution)/shard_map/ppermute | solution.py:248
  199.5 1.0 copy-start.11
  202.8 1.0 copy-start.6

commit v2 on v0

v2 whole, which is shorter than its diff:
```python
import functools

import jax
import jax.numpy as jnp
from jax import lax
from jax.experimental import pallas as pl
from jax.experimental.pallas import tpu as pltpu
from jax.sharding import Mesh
from jax.sharding import PartitionSpec as P

F32 = jnp.float32
BF16 = jnp.bfloat16
CHIPS = ("x", "z", "y")
NCHIP = 64
HEADS = 32
HALF = 16
ROWS = 128
TOK = 256
WIDTH = 128
PIECE = 33
PAIRS = HALF // 2
PROWS = 2 * 4 * PIECE

NN = ((1,), (0,))
NT = ((1,), (1,))


def dot(a, b, dims=NN):
    return lax.dot_general(a, b, (dims, ((), ())), preferred_element_type=F32)


def two_parts(x):
    high = x.astype(BF16)
    return high, (x - high.astype(F32)).astype(BF16)


def feature_map(x, w):
    logits = dot(w, x, NT)
    e_one = jnp.exp(logits - jnp.max(logits, axis=0, keepdims=True))
    e_two = jnp.exp(jnp.min(logits, axis=0, keepdims=True) - logits)
    one = e_one * (1.0 / jnp.sum(e_one, axis=0, keepdims=True))
    two = e_two * (1.0 / jnp.sum(e_two, axis=0, keepdims=True))
    return jnp.concatenate([one, two], axis=0)


def soft_back(phi, dphi, x):
    prod = phi * dphi
    one = prod[:64] - phi[:64] * jnp.sum(prod[:64], axis=0, keepdims=True)
    two = prod[64:] - phi[64:] * jnp.sum(prod[64:], axis=0, keepdims=True)
    return dot((one - two).astype(BF16), x)


def columns(h, core=None):
    at = h if core is None else core * HALF + h
    return pl.ds(pl.multiple_of(at * WIDTH, WIDTH), WIDTH)


def both_cores(own, other, h, core):
    return jnp.concatenate(
        [own[:, columns(h, core)], other[:, columns(h)].astype(BF16)], axis=0
    )


def put_state(ref, pair, i, state, row):
    for q in range(4):
        at = (4 * i + q) * PIECE
        ref[pair, at : at + 32, :] = state[32 * q : 32 * q + 32]
        ref[pair, at + 32 : at + 33, :] = row


def get_state(ref, pair, i):
    parts = [ref[pair, (4 * i + q) * PIECE : (4 * i + q) * PIECE + 32, :] for q in range(4)]
    at = 4 * i * PIECE + 32
    return jnp.concatenate(parts, axis=0), ref[pair, at : at + 1, :]


def unit():
    shape = (WIDTH, WIDTH)
    same = lax.broadcasted_iota(jnp.int32, shape, 0) == lax.broadcasted_iota(jnp.int32, shape, 1)
    return same.astype(F32).astype(BF16)


def down_rows(row, lanes, eye):
    high, low = two_parts(jnp.broadcast_to(row, (lanes, WIDTH)))
    return dot(jnp.concatenate([eye, eye], axis=1), jnp.concatenate([high, low], axis=1), NT)


def causal(core):
    shift = core * ROWS
    at_query = lax.broadcasted_iota(jnp.int32, (TOK, TOK), 0) ^ shift
    at_key = lax.broadcasted_iota(jnp.int32, (TOK, TOK), 1) ^ shift
    return at_query >= at_key


def over_heads(body):
    def pair(p, carry):
        for i in range(2):
            body(p, i, 2 * p + i)
        return carry

    lax.fori_loop(0, PAIRS, pair, 0)


def key_kernel(core_ref, k_own, k_other, v_own, v_other, w_ref, kf, vf, phik_ref, send):
    core = core_ref[0]
    ones = jnp.ones((8, TOK), BF16)

    def head(p, i, h):
        k = both_cores(k_own, k_other, h, core)
        v = both_cores(v_own, v_other, h, core)
        kf[h] = k
        vf[h] = v
        phik = feature_map(k, w_ref[core * HALF + h])
        phik_ref[h] = phik
        phikb = phik.astype(BF16)
        put_state(send, p, i, dot(phikb, v), dot(ones, phikb, NT)[:1])

    over_heads(head)


def score_kernel(core_ref, q_own, q_other, w_ref, phik_ref, vf, qf, phiq_ref, phiqb_ref, part):
    core = core_ref[0]
    mask = causal(core)
    ones = jnp.ones((TOK, WIDTH), BF16)

    def head(p, i, h):
        q = both_cores(q_own, q_other, h, core)
        qf[h] = q
        phiq = feature_map(q, w_ref[core * HALF + h])
        phiq_ref[h] = phiq
        phiqb = phiq.astype(BF16).T
        phiqb_ref[h] = phiqb
        scores = jnp.where(mask, dot(phiqb, phik_ref[h].astype(BF16)), 0.0)
        part[h] = dot(scores.astype(BF16), jnp.concatenate([vf[h], ones], axis=1))

    over_heads(head)


def out_kernel(
    core_ref, pre, phiq_ref, phiqb_ref, part, t_own, t_other,
    y_own, y_send, dd, dden_ref, send, loss_ref,
):
    core = core_ref[0]
    eye = unit()
    ones = jnp.ones((8, TOK), BF16)
    none = jnp.zeros((WIDTH, WIDTH), BF16)
    scale = 2.0 / (HEADS * WIDTH)
    loss_ref[...] = jnp.zeros_like(loss_ref)

    def head(p, i, h):
        state, norm = get_state(pre, p, i)
        high, low = two_parts(down_rows(norm, WIDTH, eye))
        right = jnp.concatenate(
            [
                jnp.concatenate([state.astype(BF16), high], axis=1),
                jnp.concatenate([none, low], axis=1),
            ],
            axis=0,
        )
        phiqb = phiqb_ref[h]
        both = part[h] + dot(jnp.concatenate([phiqb, phiqb], axis=1), right)
        inv = 1.0 / both[:, WIDTH:]
        y = both[:, :WIDTH] * inv
        y_own[:, columns(h)] = y[:ROWS].astype(BF16)
        y_send[:, columns(h)] = y[ROWS:]
        t = both_cores(t_own, t_other, h, core)
        err = y - t.astype(F32)
        loss_ref[...] += jnp.sum((err * err).reshape(TOK // 8, 8, WIDTH), axis=0)
        dnum = (scale * err) * inv
        dnumb = dnum.astype(BF16)
        high, low = two_parts(dnum * y)
        dd[h] = jnp.concatenate([dnumb, high], axis=1)
        dden = -dot(ones, jnp.concatenate([high, low], axis=1), NT)
        dden_ref[h] = dden
        phiqt = phiq_ref[h].astype(BF16)
        high, low = two_parts(dden)
        rnorm = dot(high, phiqt, NT) + dot(low, phiqt, NT)
        put_state(send, p, i, dot(phiqt, dnumb), rnorm[:1])

    over_heads(head)


def grid_kernel(
    core_ref, pre, dd, dden_ref, phik_ref, phiq_ref, vf, qf, dphik_ref, grad_ref,
):
    mask = causal(core_ref[0])
    eye = unit()
    minus = jnp.full((TOK, WIDTH), -1.0, BF16)

    def head(p, i, h):
        state, norm = get_state(pre, p, i)
        both = dd[h]
        grid = dot(both, jnp.concatenate([vf[h], minus], axis=1), NT)
        gridb = jnp.where(mask, grid, 0.0).astype(BF16)
        phiq = phiq_ref[h]
        dphik_ref[h] = dot(phiq.astype(BF16), gridb)
        dphiq = dot(phik_ref[h].astype(BF16), gridb, NT)
        dphiq = dphiq + dot(state.astype(BF16), both[:, :WIDTH], NT)
        dphiq = dphiq + down_rows(norm, TOK, eye) * dden_ref[h][:1]
        grad_ref[h] = soft_back(phiq, dphiq, qf[h])

    over_heads(head)


def last_kernel(suf, vf, kf, phik_ref, dphik_ref, grad_ref, loss_ref, send):
    row = jnp.sum(loss_ref[...], axis=0, keepdims=True)
    eye = unit()

    def head(p, i, h):
        state, norm = get_state(suf, p, i)
        dphik = dphik_ref[h] + dot(state.astype(BF16), vf[h], NT) + down_rows(norm, TOK, eye)
        grad_key = soft_back(phik_ref[h], dphik, kf[h])
        put_state(send, p, i, jnp.concatenate([grad_ref[h], grad_key], axis=0), row)

    over_heads(head)


def scan_kernel(x_ref, o_ref, *, reverse):
    def pieces(step, acc):
        block = PAIRS - 1 - step if reverse else step
        order = range(8)
        for j in reversed(order) if reverse else order:
            o_ref[block, PIECE * j : PIECE * (j + 1), :] = acc
            acc = acc + x_ref[block, PIECE * j : PIECE * (j + 1), :]
        return acc

    lax.fori_loop(0, PAIRS, pieces, jnp.zeros((PIECE, WIDTH), F32))


def sum_kernel(x_ref, o_ref):
    def add(block, acc):
        for j in range(8):
            acc = acc + x_ref[block, PIECE * j : PIECE * (j + 1), :]
        return acc

    acc = lax.fori_loop(0, PAIRS, add, jnp.zeros((PIECE, WIDTH), F32))

    def put(block, carry):
        for j in range(8):
            o_ref[block, PIECE * j : PIECE * (j + 1), :] = acc
        return carry

    lax.fori_loop(0, PAIRS, put, 0)


def unpack_kernel(core_ref, mine, theirs, gq, gk, loss_ref):
    core = core_ref[0]
    total = jnp.sum(mine[0, 32:33, :] + theirs[0, 32:33, :], keepdims=True)
    loss_ref[...] = total.reshape(1, 1) * (1.0 / (HEADS * WIDTH) / (NCHIP * TOK))
    for src, start in ((mine, core * HALF), (theirs, (1 - core) * HALF)):

        def pair(p, carry, src=src, start=start):
            for i in range(2):
                for q in range(4):
                    at = (4 * i + q) * PIECE
                    dst = gq if q < 2 else gk
                    rows = slice(32 * (q % 2), 32 * (q % 2) + 32)
                    dst[start + 2 * p + i, rows, :] = src[p, at : at + 32, :]
            return carry

        lax.fori_loop(0, PAIRS, pair, 0)


def merge_kernel(core_ref, own, other, out):
    core = core_ref[0]

    def head(h, carry):
        out[:, columns(h, core)] = own[:, columns(h)]
        out[:, columns(h, 1 - core)] = other[:, columns(h)].astype(BF16)
        return carry

    lax.fori_loop(0, HALF, head, 0)


def call(body, name, args, outs, scalar=True):
    vmem = pl.BlockSpec(memory_space=pltpu.VMEM)
    specs = [vmem] * len(args)
    if scalar:
        specs[0] = pl.BlockSpec(memory_space=pltpu.SMEM)
    many = isinstance(outs, tuple)
    return pl.pallas_call(
        body,
        in_specs=specs,
        out_specs=(vmem,) * len(outs) if many else vmem,
        out_shape=outs,
        name=name,
        compiler_params=pltpu.CompilerParams(vmem_limit_bytes=56 * 1024 * 1024),
    )(*args)


def sds(shape, dtype=F32):
    return jax.ShapeDtypeStruct(shape, dtype)


PAYLOAD = sds((PAIRS, PROWS, WIDTH))


def exchange(x):
    pieces = lax.all_to_all(x.reshape(NCHIP, 1, PIECE * WIDTH), CHIPS, 0, 0, tiled=True)
    return pieces.reshape(PAIRS, PROWS, WIDTH)


def scan(x, reverse):
    return call(functools.partial(scan_kernel, reverse=reverse), "scan", (x,), PAYLOAD, False)


def swap(x):
    return lax.ppermute(x, "c", [(0, 1), (1, 0)])


def shards(queries, keys, values, teacher, query_map, key_map):
    c = lax.axis_index("c").astype(jnp.int32)
    core = c.reshape(1)
    half = HALF * WIDTH

    def others(x):
        part = lax.dynamic_slice(x, (0, (1 - c) * half), (ROWS, half))
        return swap(part.astype(F32))

    k_other, v_other = others(keys), others(values)
    q_other, t_other = others(queries), others(teacher)

    natural = sds((HALF, TOK, WIDTH), BF16)
    features = sds((HALF, WIDTH, TOK))
    wide = sds((HALF, TOK, 2 * WIDTH))

    kf, vf, phik, send = call(
        key_kernel, "keys", (core, keys, k_other, values, v_other, key_map),
        (natural, natural, features, PAYLOAD),
    )
    gathered = exchange(send)
    qf, phiq, phiqb, part = call(
        score_kernel, "scores", (core, queries, q_other, query_map, phik, vf),
        (natural, features, natural, wide),
    )
    pre = exchange(scan(gathered, False))
    y_own, y_send, dd, dden, send, loss = call(
        out_kernel, "outs", (core, pre, phiq, phiqb, part, teacher, t_other),
        (
            sds((ROWS, half), BF16), sds((ROWS, half)), sds((HALF, TOK, 2 * WIDTH), BF16),
            sds((HALF, 8, TOK)), PAYLOAD, sds((8, WIDTH)),
        ),
    )
    y_other = swap(y_send)
    gathered = exchange(send)
    dphik, grad_query = call(
        grid_kernel, "grids", (core, pre, dd, dden, phik, phiq, vf, qf),
        (features, sds((HALF, 64, WIDTH))),
    )
    suf = exchange(scan(gathered, True))
    attn = call(
        merge_kernel, "merge", (core, y_own, y_other), sds((ROWS, HEADS * WIDTH), BF16)
    )
    send = call(
        last_kernel, "last", (suf, vf, kf, phik, dphik, grad_query, loss), PAYLOAD, False
    )
    mine = exchange(call(sum_kernel, "sum", (exchange(send),), PAYLOAD, False))
    theirs = swap(mine)
    grad = sds((HEADS, 64, WIDTH))
    grad_query, grad_key, loss = call(
        unpack_kernel, "unpack", (core, mine, theirs), (grad, grad, sds((1, 1)))
    )
    return attn, loss[0, 0], grad_query, grad_key


def solution(mesh):
    fine = Mesh(mesh.devices.reshape(4, 4, 4, 2), ("x", "z", "y", "c"))
    tokens = P(("x", "z", "y", "c"), None)
    return jax.shard_map(
        shards,
        mesh=fine,
        in_specs=(tokens, tokens, tokens, tokens, P(), P()),
        out_specs=(tokens, P(), P(), P()),
        check_vma=False,
    )
```

time: 1060 us -> 209 us (0.20)
  waiting for transfers between devices: 691 us -> 29.3 us
  blocking collectives: 183 us -> 69.5 us
  other arithmetic: 88.6 us -> 1.53 us
  Pallas kernels: 0 us -> 70.7 us
  matrix products: 45.7 us -> 0 us
  local copies, waits for them, and re-layouts: 37.7 us -> 5.87 us
  starting transfers between devices: 0.29 us -> 31 us
  between operations: 17 us -> 0.74 us
    all_gather x4 -> x0, waiting for transfers between devices: 470 us -> none  [carried_in(): gathered = jax.tree.map(lambda a: lax.all_gather(a, axis), part)]
    psum x3 -> x0, waiting for transfers between devices: 221 us -> none  [the longest x2 141 us: from_root(): return lax.psum(jnp.where(mine, x, jnp.zeros_like(x)), axis)]
    psum x3 -> x0, blocking collectives: 115 us -> none  [the longest x1 64.8 us: shards(): lax.psum((local_error, grad_query, grad_key), ('outer', 'inner'))]
    add x47 -> x0, other arithmetic: 74 us -> none  [the longest x46 74 us: pair_add(): return (left[0] + right[0], left[1] + right[1])]
    pallas_call x0 -> x10, Pallas kernels: none -> 70.7 us  [call(): pl.pallas_call(body, in_specs=specs, out_specs=(vmem,) * len(outs) if man...]
    all_to_all x0 -> x3, blocking collectives: none -> 69.5 us  [exchange(): lax.all_to_all(x.reshape(NCHIP, 1, PIECE * WIDTH), CHIPS, 0, 0, tiled=True)]
    all_gather x4 -> x0, blocking collectives: 68.1 us -> none  [carried_in(): gathered = jax.tree.map(lambda a: lax.all_gather(a, axis), part)]
    dot_general x14 -> x0, matrix products: 34.1 us -> none  [the longest x2 7.88 us: soft_back(): jnp.einsum('thf,thd->hfd', grad_logit.astype(jnp.bfloat16), x, preferred_...]
  transfers between devices with their start and end apart: 7 -> 9, of which waited for: 7 -> 6; matrix products, arithmetic and copies ran while one was open for 3% -> 0% of each run, Pallas kernels for 0% -> 15%
where the time goes in v2:
time: 209 us
  Pallas kernels  70.7 us (34%)
  blocking collectives  69.5 us (33%)
  starting transfers between devices  31 us (15%)
  waiting for transfers between devices  29.3 us (14%)
  local copies, waits for them, and re-layouts  5.87 us (3%)
    pallas_call x10, Pallas kernels, call(): pl.pallas_call(body, in_specs=specs, out_specs=(vmem,) * len(outs) if man...  70.7 us
    all_to_all x3, blocking collectives, exchange(): lax.all_to_all(x.reshape(NCHIP, 1, PIECE * WIDTH), CHIPS, 0, 0, tiled=True)  69.5 us
    all_to_all x3, starting transfers between devices, exchange(): lax.all_to_all(x.reshape(NCHIP, 1, PIECE * WIDTH), CHIPS, 0, 0, tiled=True)  22.8 us
    all_to_all x3, waiting for transfers between devices, exchange(): lax.all_to_all(x.reshape(NCHIP, 1, PIECE * WIDTH), CHIPS, 0, 0, tiled=True)  22 us
    ppermute x6, starting transfers between devices, swap(): return lax.ppermute(x, 'c', [(0, 1), (1, 0)])  8.15 us
    ppermute x6, waiting for transfers between devices, swap(): return lax.ppermute(x, 'c', [(0, 1), (1, 0)])  7.31 us
    unnamed x26, local copies, waits for them, and re-layouts  5.87 us
  transfers between devices with their start and end apart: 9, of which 6 were waited for; matrix products, arithmetic and copies ran while one was open for 0% of the time, Pallas kernels for 15%

profile of v2, /device:TPU:1, one launch (start us, length us, event | category | flops | bytes accessed | tf_op | source)
XLA Modules:
  0.0 208.6 jit_solution(4344046437751817613)
XLA Ops:
  0.6 1.2 dynamic-slice_convert_fusion.2
  1.9 1.5 collective-permute-start.1
  3.6 2.1 collective-permute-done.1.v_other
  5.6 1.5 collective-permute-done.k_other
  7.1 1.0 copy-done.9
  8.1 7.7 %keys.1 = (bf16[16,256,128]{2,1,0:T(8,128)(2,1)}, bf16[16,256,128]{2,1,0:T(8,128)(2,1)}, f32[16,128,256]{2,1,0:T(8,128)}, f32[8,264,128]{2,1,0:T(8,128)}) custom-call(s32[1]{0:T(128)} %bitcast.core_ref, bf16[128,4096]{1,0:T(8,128)(2,1)} %k_own.1, f32[128,2048]{1,0:T(8,128)} %copy-done.9, bf16[128,4096]{1,0:T(8,128)(2,1)} %v_own.1, f32[128,2048]{1,0:T(8,128)} %copy-done.8, ...), custom_call_target="tpu_custom_call" | custom-call | tf_op jit(solution)/shard_map/keys/pallas_call | solution.py:281
  15.9 11.4 %all-to-all-start = ((f32[64,1,4224]{2,1,0:T(1,128)}), f32[64,1,4224]{2,1,0:T(1,128)S(1)}, u32[]{:S(2)}, u32[]{:S(2)}) async-start(f32[64,1,4224]{2,1,0:T(1,128)} %bitcast.26), calls=%async_computation | async-start | bytes 2162688 | tf_op jit(solution)/shard_map/all_to_all | solution.py:299
  28.1 16.5 %all-to-all-done = f32[64,1,4224]{2,1,0:T(1,128)S(1)} async-done(((f32[64,1,4224]{2,1,0:T(1,128)}), f32[64,1,4224]{2,1,0:T(1,128)S(1)}, u32[]{:S(2)}, u32[]{:S(2)}) %all-to-all-start) | async-done | bytes 1081376 | tf_op jit(solution)/shard_map/all_to_all | solution.py:299
  44.6 1.0 copy-done.2
  45.5 2.4 %scan.2 = f32[8,264,128]{2,1,0:T(8,128)} custom-call(f32[8,264,128]{2,1,0:T(8,128)} %bitcast.19), custom_call_target="tpu_custom_call" | custom-call | tf_op jit(solution)/shard_map/scan/pallas_call | solution.py:281
  47.9 5.8 %all-to-all-start.1 = ((f32[64,1,4224]{2,1,0:T(1,128)}), f32[64,1,4224]{2,1,0:T(1,128)S(1)}, u32[]{:S(2)}, u32[]{:S(2)}) async-start(f32[64,1,4224]{2,1,0:T(1,128)} %bitcast.18), calls=%async_computation.1 | async-start | bytes 2162688 | tf_op jit(solution)/shard_map/all_to_all | solution.py:299
  53.8 1.8 collective-permute-start.3
  55.6 12.3 %scores.1 = (bf16[16,256,128]{2,1,0:T(8,128)(2,1)}, f32[16,128,256]{2,1,0:T(8,128)}, bf16[16,256,128]{2,1,0:T(8,128)(2,1)}, f32[16,256,256]{2,1,0:T(8,128)}) custom-call(s32[1]{0:T(128)} %bitcast.core_ref, bf16[128,4096]{1,0:T(8,128)(2,1)} %q_own.1, f32[128,2048]{1,0:T(8,128)} %collective-permute-done.2.q_other, bf16[32,64,128]{2,1,0:T(8,128)(2,1)} %w_ref.3, ...), custom_call_target="tpu_custom_call" | custom-call | tf_op jit(solution)/shard_map/scores/pallas_call | solution.py:281
  67.9 2.3 %all-to-all-done.1 = f32[64,1,4224]{2,1,0:T(1,128)S(1)} async-done(((f32[64,1,4224]{2,1,0:T(1,128)}), f32[64,1,4224]{2,1,0:T(1,128)S(1)}, u32[]{:S(2)}, u32[]{:S(2)}) %all-to-all-start.1) | async-done | bytes 1081376 | tf_op jit(solution)/shard_map/all_to_all | solution.py:299
  70.2 1.0 copy-done
  71.2 14.7 %outs.1 = (bf16[128,2048]{1,0:T(8,128)(2,1)}, f32[128,2048]{1,0:T(8,128)}, bf16[16,256,256]{2,1,0:T(8,128)(2,1)}, f32[16,8,256]{2,1,0:T(8,128)}, f32[8,264,128]{2,1,0:T(8,128)}, /*index=5*/f32[8,128]{1,0:T(8,128)}) custom-call(s32[1]{0:T(128)} %bitcast.core_ref, f32[8,264,128]{2,1,0:T(8,128)} %bitcast.14, f32[16,128,256]{2,1,0:T(8,128)} %get-tuple-element.26.phiq_ref, ...), custom_call_target="tpu_custom_call" | custom-call | tf_op jit(solution)/shard_map/outs/pallas_call | solution.py:281
  85.9 25.5 %all_to_all.30 = f32[64,1,4224]{2,1,0:T(1,128)} all-to-all(f32[64,1,4224]{2,1,0:T(1,128)} %bitcast.27), channel_id=1, replica_groups=mesh['x'=4,'z'=4,'y'=4,'c'=2] {'x','z','y'}, dimensions={0} | all-to-all | bytes 2162688 | tf_op jit(solution)/shard_map/all_to_all | solution.py:299
  111.4 2.3 %scan.3 = f32[8,264,128]{2,1,0:T(8,128)} custom-call(f32[8,264,128]{2,1,0:T(8,128)} %bitcast.21), custom_call_target="tpu_custom_call" | custom-call | tf_op jit(solution)/shard_map/scan/pallas_call | solution.py:281
  113.7 5.6 %all-to-all-start.3 = ((f32[64,1,4224]{2,1,0:T(1,128)}), f32[64,1,4224]{2,1,0:T(1,128)S(1)}, u32[]{:S(2)}, u32[]{:S(2)}) async-start(f32[64,1,4224]{2,1,0:T(1,128)} %bitcast.20), calls=%async_computation.3 | async-start | bytes 2162688 | tf_op jit(solution)/shard_map/all_to_all | solution.py:299
  119.4 13.2 %grids.1 = (f32[16,128,256]{2,1,0:T(8,128)}, f32[16,64,128]{2,1,0:T(8,128)}) custom-call(s32[1]{0:T(128)} %bitcast.core_ref, f32[8,264,128]{2,1,0:T(8,128)} %bitcast.15, bf16[16,256,256]{2,1,0:T(8,128)(2,1)} %get-tuple-element.33.dd, f32[16,8,256]{2,1,0:T(8,128)} %get-tuple-element.34.dden_ref, f32[16,128,256]{2,1,0:T(8,128)} %get-tuple-element.24.phik_ref, ...), custom_call_target="tpu_custom_call" | custom-call | tf_op jit(solution)/shard_map/grids/pallas_call | solution.py:281
  132.6 3.2 %all-to-all-done.3 = f32[64,1,4224]{2,1,0:T(1,128)S(1)} async-done(((f32[64,1,4224]{2,1,0:T(1,128)}), f32[64,1,4224]{2,1,0:T(1,128)S(1)}, u32[]{:S(2)}, u32[]{:S(2)}) %all-to-all-start.3) | async-done | bytes 1081376 | tf_op jit(solution)/shard_map/all_to_all | solution.py:299
  135.8 1.0 copy-done.3
  136.8 9.7 %last.1 = f32[8,264,128]{2,1,0:T(8,128)} custom-call(f32[8,264,128]{2,1,0:T(8,128)} %bitcast.24, bf16[16,256,128]{2,1,0:T(8,128)(2,1)} %get-tuple-element.25.vf, bf16[16,256,128]{2,1,0:T(8,128)(2,1)} %get-tuple-element.32.kf, f32[16,128,256]{2,1,0:T(8,128)} %get-tuple-element.24.phik_ref, f32[16,128,256]{2,1,0:T(8,128)} %get-tuple-element.36.dphik_ref, ...), custom_call_target="tpu_custom_call" | custom-call | tf_op jit(solution)/shard_map/last/pallas_call | solution.py:281
  146.5 23.2 %all_to_all.31 = f32[64,1,4224]{2,1,0:T(1,128)} all-to-all(f32[64,1,4224]{2,1,0:T(1,128)} %bitcast.25), channel_id=1, replica_groups=mesh['x'=4,'z'=4,'y'=4,'c'=2] {'x','z','y'}, dimensions={0} | all-to-all | bytes 2162688 | tf_op jit(solution)/shard_map/all_to_all | solution.py:299
  169.7 2.4 %sum.1 = f32[8,264,128]{2,1,0:T(8,128)} custom-call(f32[8,264,128]{2,1,0:T(8,128)} %bitcast.22), custom_call_target="tpu_custom_call" | custom-call | tf_op jit(solution)/shard_map/sum/pallas_call | solution.py:281
  172.1 20.8 %all_to_all.32 = f32[64,1,4224]{2,1,0:T(1,128)S(1)} all-to-all(f32[64,1,4224]{2,1,0:T(1,128)} %bitcast.23), channel_id=1, replica_groups=mesh['x'=4,'z'=4,'y'=4,'c'=2] {'x','z','y'}, dimensions={0} | all-to-all | bytes 2162688 | tf_op jit(solution)/shard_map/all_to_all | solution.py:299
  192.9 4.0 %collective-permute-start.5 = (f32[8,264,128]{2,1,0:T(8,128)S(1)}, f32[8,264,128]{2,1,0:T(8,128)S(1)}, u32[]{:S(2)}, u32[]{:S(2)}) collective-permute-start(f32[8,264,128]{2,1,0:T(8,128)S(1)} %bitcast.16), channel_id=1, source_target_pairs={{0,1},{1,0},{2,3},{3,2},{4,5},{5,4},{6,7},{7,6},{8,9},{9,8},{10,11... | collective-permute-start | bytes 3244040 | tf_op jit(solution)/shard_map/ppermute | solution.py:308
  196.9 3.7 %collective-permute-done.4.other = f32[128,2048]{1,0:T(8,128)S(1)} collective-permute-done((f32[128,2048]{1,0:T(8,128)S(1)}, f32[128,2048]{1,0:T(8,128)S(1)}, u32[]{:S(2)}, u32[]{:S(2)}) %collective-permute-start.4) | collective-permute-done | bytes 1048608 | tf_op jit(solution)/shard_map/ppermute | solution.py:308
  200.7 1.0 copy-done.10
  201.7 2.8 %merge.1 = bf16[128,4096]{1,0:T(8,128)(2,1)} custom-call(s32[1]{0:T(128)} %bitcast.core_ref, bf16[128,2048]{1,0:T(8,128)(2,1)} %get-tuple-element.29.own, f32[128,2048]{1,0:T(8,128)} %copy-done.10), custom_call_target="tpu_custom_call" | custom-call | tf_op jit(solution)/shard_map/merge/pallas_call | solution.py:281
  204.5 1.0 copy-done.7
  205.4 3.2 %unpack.1 = (f32[32,64,128]{2,1,0:T(8,128)}, f32[32,64,128]{2,1,0:T(8,128)}, f32[1,1]{1,0:T(1,128)}) custom-call(s32[1]{0:T(128)} %bitcast.core_ref, f32[8,264,128]{2,1,0:T(8,128)} %bitcast.17, f32[8,264,128]{2,1,0:T(8,128)} %copy-done.7), custom_call_target="tpu_custom_call" | custom-call | tf_op jit(solution)/shard_map/unpack/pallas_call | solution.py:281
  (29 shorter events, 1.3 us)
Async XLA Ops:
  0.6 2.7 %copy-start.4 = (bf16[128,4096]{1,0:T(8,128)(2,1)S(1)}, bf16[128,4096]{1,0:T(8,128)(2,1)}, u32[]{:S(2)}) copy-start(bf16[128,4096]{1,0:T(8,128)(2,1)} %k_own.1) | copy-start | bytes 3145732
  1.9 3.7 %collective-permute-start.1 = (f32[128,2048]{1,0:T(8,128)S(1)}, f32[128,2048]{1,0:T(8,128)S(1)}, u32[]{:S(2)}, u32[]{:S(2)}) collective-permute-start(f32[128,2048]{1,0:T(8,128)S(1)} %dynamic-slice_convert_fusion.2), channel_id=1, source_target_pairs={{0,1},{1,0},{2,3},{3,2},{4,5},{5,4},{6,7},{7,6},{8,9},{9,8},{10,11... | collective-permute-start | bytes 3145736 | tf_op jit(solution)/shard_map/ppermute | solution.py:308
  3.5 3.7 %collective-permute-start = (f32[128,2048]{1,0:T(8,128)S(1)}, f32[128,2048]{1,0:T(8,128)S(1)}, u32[]{:S(2)}, u32[]{:S(2)}) collective-permute-start(f32[128,2048]{1,0:T(8,128)S(1)} %dynamic-slice_convert_fusion.3), channel_id=1, source_target_pairs={{0,1},{1,0},{2,3},{3,2},{4,5},{5,4},{6,7},{7,6},{8,9},{9,8},{10,11... | collective-permute-start | bytes 3145736 | tf_op jit(solution)/shard_map/ppermute | solution.py:308
  5.6 1.5 copy-start.8
  7.1 1.0 copy-start.9
  15.8 11.4 %copy-start.5 = (bf16[128,4096]{1,0:T(8,128)(2,1)S(1)}, bf16[128,4096]{1,0:T(8,128)(2,1)}, u32[]{:S(2)}) copy-start(bf16[128,4096]{1,0:T(8,128)(2,1)} %q_own.1) | copy-start | bytes 3145732
  15.9 28.7 %all-to-all-start = ((f32[64,1,4224]{2,1,0:T(1,128)}), f32[64,1,4224]{2,1,0:T(1,128)S(1)}, u32[]{:S(2)}, u32[]{:S(2)}) async-start(f32[64,1,4224]{2,1,0:T(1,128)} %bitcast.26), calls=%async_computation | async-start | bytes 2162688 | tf_op jit(solution)/shard_map/all_to_all | solution.py:299
  27.4 28.2 %collective-permute-start.2 = (f32[128,2048]{1,0:T(8,128)S(1)}, f32[128,2048]{1,0:T(8,128)}, u32[]{:S(2)}, u32[]{:S(2)}) collective-permute-start(f32[128,2048]{1,0:T(8,128)S(1)} %dynamic-slice_convert_fusion.1), channel_id=1, source_target_pairs={{0,1},{1,0},{2,3},{3,2},{4,5},{5,4},{6,7},{7,6},{8,9},{9,8},{10,11... | collective-permute-start | bytes 3145736 | tf_op jit(solution)/shard_map/ppermute | solution.py:308
  44.6 1.0 copy-start.2
  47.9 5.8 %copy-start.6 = (bf16[128,4096]{1,0:T(8,128)(2,1)S(1)}, bf16[128,4096]{1,0:T(8,128)(2,1)}, u32[]{:S(2)}) copy-start(bf16[128,4096]{1,0:T(8,128)(2,1)} %t_own.1) | copy-start | bytes 3145732
  47.9 22.3 %all-to-all-start.1 = ((f32[64,1,4224]{2,1,0:T(1,128)}), f32[64,1,4224]{2,1,0:T(1,128)S(1)}, u32[]{:S(2)}, u32[]{:S(2)}) async-start(f32[64,1,4224]{2,1,0:T(1,128)} %bitcast.18), calls=%async_computation.1 | async-start | bytes 2162688 | tf_op jit(solution)/shard_map/all_to_all | solution.py:299
  53.8 14.1 %collective-permute-start.3 = (f32[128,2048]{1,0:T(8,128)S(1)}, f32[128,2048]{1,0:T(8,128)S(1)}, u32[]{:S(2)}, u32[]{:S(2)}) collective-permute-start(f32[128,2048]{1,0:T(8,128)S(1)} %dynamic-slice_convert_fusion), channel_id=1, source_target_pairs={{0,1},{1,0},{2,3},{3,2},{4,5},{5,4},{6,7},{7,6},{8,9},{9,8},{10,11... | collective-permute-start | bytes 3145736 | tf_op jit(solution)/shard_map/ppermute | solution.py:308
  67.9 2.3 %copy-start.11 = (f32[128,2048]{1,0:T(8,128)}, f32[128,2048]{1,0:T(8,128)S(1)}, u32[]{:S(2)}) copy-start(f32[128,2048]{1,0:T(8,128)S(1)} %collective-permute-done.3.t_other) | copy-start | bytes 3145732
  70.2 1.0 copy-start
  113.7 22.1 %all-to-all-start.3 = ((f32[64,1,4224]{2,1,0:T(1,128)}), f32[64,1,4224]{2,1,0:T(1,128)S(1)}, u32[]{:S(2)}, u32[]{:S(2)}) async-start(f32[64,1,4224]{2,1,0:T(1,128)} %bitcast.20), calls=%async_computation.3 | async-start | bytes 2162688 | tf_op jit(solution)/shard_map/all_to_all | solution.py:299
  135.8 1.0 copy-start.3
  172.1 24.8 %copy-start.12 = (f32[128,2048]{1,0:T(8,128)S(1)}, f32[128,2048]{1,0:T(8,128)}, u32[]{:S(2)}) copy-start(f32[128,2048]{1,0:T(8,128)} %get-tuple-element.30) | copy-start | bytes 3145732
  192.9 11.6 %copy-start.1 = (f32[64,1,4224]{2,1,0:T(1,128)}, f32[64,1,4224]{2,1,0:T(1,128)S(1)}, u32[]{:S(2)}) copy-start(f32[64,1,4224]{2,1,0:T(1,128)S(1)} %all_to_all.32) | copy-start | bytes 3244036
  192.9 11.6 %collective-permute-start.5 = (f32[8,264,128]{2,1,0:T(8,128)S(1)}, f32[8,264,128]{2,1,0:T(8,128)S(1)}, u32[]{:S(2)}, u32[]{:S(2)}) collective-permute-start(f32[8,264,128]{2,1,0:T(8,128)S(1)} %bitcast.16), channel_id=1, source_target_pairs={{0,1},{1,0},{2,3},{3,2},{4,5},{5,4},{6,7},{7,6},{8,9},{9,8},{10,11... | collective-permute-start | bytes 3244040 | tf_op jit(solution)/shard_map/ppermute | solution.py:308
  196.9 3.8 %collective-permute-start.4 = (f32[128,2048]{1,0:T(8,128)S(1)}, f32[128,2048]{1,0:T(8,128)S(1)}, u32[]{:S(2)}, u32[]{:S(2)}) collective-permute-start(f32[128,2048]{1,0:T(8,128)S(1)} %copy-done.12), channel_id=1, source_target_pairs={{0,1},{1,0},{2,3},{3,2},{4,5},{5,4},{6,7},{7,6},{8,9},{9,8},{10,11... | collective-permute-start | bytes 3145736 | tf_op jit(solution)/shard_map/ppermute | solution.py:308
  200.7 1.0 copy-start.10
  204.4 1.0 copy-start.7

commit v3 on v2

v3 whole, which is shorter than its diff:
```python
import functools

import jax
import jax.numpy as jnp
from jax import lax
from jax.experimental import pallas as pl
from jax.experimental.pallas import tpu as pltpu
from jax.sharding import Mesh
from jax.sharding import PartitionSpec as P

F32 = jnp.float32
BF16 = jnp.bfloat16
CHIPS = ("x", "z", "y")
NCHIP = 64
HEADS = 32
HALF = 16
ROWS = 128
TOK = 256
WIDTH = 128
PIECE = 33
PAIRS = HALF // 2
GRP = 4
STEPS = HALF // GRP
PROWS = 2 * 4 * PIECE

NN = ((1,), (0,))
NT = ((1,), (1,))


def dot(a, b, dims=NN):
    return lax.dot_general(a, b, (dims, ((), ())), preferred_element_type=F32)


def two_parts(x):
    high = x.astype(BF16)
    return high, (x - high.astype(F32)).astype(BF16)


def soft_maps(logits):
    e_one = jnp.exp(logits - jnp.max(logits, axis=0, keepdims=True))
    e_two = jnp.exp(jnp.min(logits, axis=0, keepdims=True) - logits)
    one = e_one * (1.0 / jnp.sum(e_one, axis=0, keepdims=True))
    two = e_two * (1.0 / jnp.sum(e_two, axis=0, keepdims=True))
    return jnp.concatenate([one, two], axis=0)


def soft_back(phi, dphi, x):
    prod = phi * dphi
    one = prod[:64] - phi[:64] * jnp.sum(prod[:64], axis=0, keepdims=True)
    two = prod[64:] - phi[64:] * jnp.sum(prod[64:], axis=0, keepdims=True)
    return dot((one - two).astype(BF16), x)


def columns(h):
    return pl.ds(pl.multiple_of(h * WIDTH, WIDTH), WIDTH)


def both_cores(own, other, h, base=0):
    return jnp.concatenate(
        [own[:, columns(h)], other[:, columns(base + h)].astype(BF16)], axis=0
    )


def put_state(ref, pair, i, state, row):
    for q in range(4):
        at = (4 * i + q) * PIECE
        ref[pair, at : at + 32, :] = state[32 * q : 32 * q + 32]
        ref[pair, at + 32 : at + 33, :] = row


def get_state(ref, pair, i):
    parts = [ref[pair, (4 * i + q) * PIECE : (4 * i + q) * PIECE + 32, :] for q in range(4)]
    at = 4 * i * PIECE + 32
    return jnp.concatenate(parts, axis=0), ref[pair, at : at + 1, :]


def unit():
    shape = (WIDTH, WIDTH)
    same = lax.broadcasted_iota(jnp.int32, shape, 0) == lax.broadcasted_iota(jnp.int32, shape, 1)
    return same.astype(F32).astype(BF16)


def down_rows(row, lanes, eye):
    high, low = two_parts(jnp.broadcast_to(row, (lanes, WIDTH)))
    return dot(jnp.concatenate([eye, eye], axis=1), jnp.concatenate([high, low], axis=1), NT)


def causal(core):
    shift = core * ROWS
    at_query = lax.broadcasted_iota(jnp.int32, (TOK, TOK), 0) ^ shift
    at_key = lax.broadcasted_iota(jnp.int32, (TOK, TOK), 1) ^ shift
    return at_query >= at_key


def over_heads(body):
    running = []
    waiting = list(range(GRP))
    while running or waiting:
        if waiting:
            h = waiting.pop(0)
            running.append(body(h // 2, h % 2, h))
        running = [r for r in running if next(r, "end") != "end"]


def key_kernel(core_ref, k_own, k_other, v_own, v_other, w_ref, kf, vf, phik_ref, send):
    ones = jnp.ones((8, TOK), BF16)
    base = pl.program_id(0) * GRP

    def head(p, i, h):
        k = both_cores(k_own, k_other, h, base)
        kf[h] = k
        logits = dot(w_ref[h], k, NT)
        yield
        phik = soft_maps(logits)
        phik_ref[h] = phik
        phikb = phik.astype(BF16)
        v = both_cores(v_own, v_other, h, base)
        vf[h] = v
        yield
        state = dot(phikb, v)
        row = dot(ones, phikb, NT)[:1]
        yield
        put_state(send, p, i, state, row)

    over_heads(head)


def score_kernel(
    core_ref, q_own, q_other, w_ref, phik_ref, vf, qf, phiq_ref, phiqt_ref, phiqb_ref, part
):
    mask = causal(core_ref[0])
    ones = jnp.ones((TOK, WIDTH), BF16)

    def head(p, i, h):
        q = both_cores(q_own, q_other, h)
        qf[h] = q
        logits = dot(w_ref[h], q, NT)
        yield
        phiq = soft_maps(logits)
        phiq_ref[h] = phiq
        phiqt = phiq.astype(BF16)
        phiqt_ref[h] = phiqt
        phiqb = phiqt.T
        phiqb_ref[h] = phiqb
        yield
        scores = dot(phiqb, phik_ref[h].astype(BF16))
        yield
        scoresb = jnp.where(mask, scores, 0.0).astype(BF16)
        part[h] = dot(scoresb, jnp.concatenate([vf[h], ones], axis=1))

    over_heads(head)


def out_kernel(
    core_ref, pre, phiqt_ref, phiqb_ref, part, t_own, t_other,
    y_own, y_send, dd, dden_ref, send, loss_ref,
):
    eye = unit()
    ones = jnp.ones((8, TOK), BF16)
    none = jnp.zeros((WIDTH, WIDTH), BF16)
    scale = 2.0 / (HEADS * WIDTH)
    first = pl.program_id(0) * (GRP // 2)

    @pl.when(pl.program_id(0) == 0)
    def _():
        loss_ref[...] = jnp.zeros_like(loss_ref)

    def head(p, i, h):
        state, norm = get_state(pre, first + p, i)
        down = down_rows(norm, WIDTH, eye)
        yield
        high, low = two_parts(down)
        right = jnp.concatenate(
            [
                jnp.concatenate([state.astype(BF16), high], axis=1),
                jnp.concatenate([none, low], axis=1),
            ],
            axis=0,
        )
        phiqb = phiqb_ref[h]
        carried = dot(jnp.concatenate([phiqb, phiqb], axis=1), right)
        yield
        both = part[h] + carried
        inv = 1.0 / both[:, WIDTH:]
        y = both[:, :WIDTH] * inv
        y_own[:, columns(h)] = y[:ROWS].astype(BF16)
        y_send[:, columns(h)] = y[ROWS:]
        err = y - both_cores(t_own, t_other, h).astype(F32)
        loss_ref[...] += jnp.sum((err * err).reshape(TOK // 8, 8, WIDTH), axis=0)
        dnum = (scale * err) * inv
        dnumb = dnum.astype(BF16)
        high, low = two_parts(dnum * y)
        both = jnp.concatenate([dnumb, high, low], axis=1)
        dd[h] = both
        yield
        dden = -dot(ones, both[:, WIDTH:], NT)
        rev = dot(phiqt_ref[h], dnumb)
        yield
        dden_ref[h] = dden
        high, low = two_parts(dden)
        phiqt = phiqt_ref[h]
        rnorm = dot(high, phiqt, NT) + dot(low, phiqt, NT)
        yield
        put_state(send, p, i, rev, rnorm[:1])

    over_heads(head)


def grid_kernel(
    core_ref, pre, dd, dden_ref, phik_ref, phiq_ref, phiqt_ref, vf, qf, dphik_ref, grad_ref,
):
    mask = causal(core_ref[0])
    eye = unit()
    minus = jnp.full((TOK, WIDTH), -1.0, BF16)

    def head(p, i, h):
        state, norm = get_state(pre, p, i)
        grid = dot(dd[h], jnp.concatenate([vf[h], minus, minus], axis=1), NT)
        yield
        gridb = jnp.where(mask, grid, 0.0).astype(BF16)
        dphik_ref[h] = dot(phiqt_ref[h], gridb)
        left = jnp.concatenate([phik_ref[h].astype(BF16), state.astype(BF16)], axis=1)
        dphiq = dot(left, jnp.concatenate([gridb, dd[h, :, :WIDTH]], axis=1), NT)
        down = down_rows(norm, TOK, eye)
        yield
        grad_ref[h] = soft_back(phiq_ref[h], dphiq + down * dden_ref[h][:1], qf[h])

    over_heads(head)


def merge_kernel(core_ref, y_own, y_other, attn):
    core = core_ref[0]
    wide = GRP * WIDTH
    at = pl.program_id(0) * wide
    mine = pl.multiple_of(core * HALF * WIDTH + at, wide)
    theirs = pl.multiple_of((1 - core) * HALF * WIDTH + at, wide)
    attn[:, pl.ds(mine, wide)] = y_own[...]
    attn[:, pl.ds(theirs, wide)] = y_other[...].astype(BF16)


def last_kernel(core_ref, suf, vf, kf, phik_ref, dphik_ref, grad_ref, loss_ref, send):
    row = jnp.sum(loss_ref[...], axis=0, keepdims=True)
    eye = unit()
    first = pl.program_id(0) * (GRP // 2)

    def head(p, i, h):
        state, norm = get_state(suf, first + p, i)
        carried = dot(state.astype(BF16), vf[h], NT) + down_rows(norm, TOK, eye)
        yield
        grad_key = soft_back(phik_ref[h], dphik_ref[h] + carried, kf[h])
        yield
        put_state(send, p, i, jnp.concatenate([grad_ref[h], grad_key], axis=0), row)

    over_heads(head)


BLOCKS = PAIRS // STEPS


def scan_kernel(core_ref, x_ref, o_ref, acc_ref, *, reverse):
    step = pl.program_id(0)

    @pl.when(step == 0)
    def _():
        acc_ref[...] = jnp.zeros_like(acc_ref)

    first = (STEPS - 1 - step if reverse else step) * BLOCKS
    order = [(b, j) for b in range(BLOCKS) for j in range(8)]
    acc = acc_ref[...]
    for b, j in reversed(order) if reverse else order:
        o_ref[b, PIECE * j : PIECE * (j + 1), :] = acc
        acc = acc + x_ref[first + b, PIECE * j : PIECE * (j + 1), :]
    acc_ref[...] = acc


def sum_kernel(core_ref, x_ref, o_ref, acc_ref):
    @pl.when(pl.program_id(0) == 0)
    def _():
        acc = x_ref[0, :PIECE, :]
        for n in range(1, NCHIP):
            j = n % 8
            acc = acc + x_ref[n // 8, PIECE * j : PIECE * (j + 1), :]
        acc_ref[...] = acc

    acc = acc_ref[...]
    for b in range(BLOCKS):
        for j in range(8):
            o_ref[b, PIECE * j : PIECE * (j + 1), :] = acc


def unpack_kernel(core_ref, mine, theirs, gq, gk, loss_ref):
    step = pl.program_id(0)
    total = jnp.sum(mine[0, 32:33, :] + theirs[0, 32:33, :], keepdims=True)
    loss_ref[...] = total.reshape(1, 1) * (1.0 / (HEADS * WIDTH) / (NCHIP * TOK))
    first = lax.rem(step, 2) * (PAIRS // 2)

    def put(src):
        for p in range(PAIRS // 2):
            for i in range(2):
                for q in range(4):
                    at = (4 * i + q) * PIECE
                    dst = gq if q < 2 else gk
                    rows = slice(32 * (q % 2), 32 * (q % 2) + 32)
                    dst[2 * p + i, rows, :] = src[first + p, at : at + 32, :]

    @pl.when(step // 2 == core_ref[0])
    def _():
        put(mine)

    @pl.when(step // 2 != core_ref[0])
    def _():
        put(theirs)


def call(body, name, core, args, outs, scratch=()):
    specs, values = [], []
    for value, spec in args:
        space = pltpu.HBM
        if spec is None:
            spec = pl.BlockSpec(memory_space=pltpu.VMEM)
            space = pltpu.VMEM
        specs.append(spec)
        values.append(pltpu.with_memory_space_constraint(value, space))
    grid = pltpu.PrefetchScalarGridSpec(
        num_scalar_prefetch=1,
        grid=(STEPS,),
        in_specs=specs,
        out_specs=tuple(spec for _, spec in outs),
        scratch_shapes=list(scratch),
    )
    return pl.pallas_call(
        body,
        grid_spec=grid,
        out_shape=tuple(shape for shape, _ in outs),
        name=name,
        compiler_params=pltpu.CompilerParams(vmem_limit_bytes=48 * 1024 * 1024),
    )(core, *values)


def sds(shape, dtype=F32):
    return pltpu.HBM(shape, dtype)


def heads_block(*tail):
    return pl.BlockSpec((GRP,) + tail, lambda g, c: (g,) + (0,) * len(tail))


PAYLOAD = sds((PAIRS, PROWS, WIDTH))
PIECES = pl.BlockSpec((BLOCKS, PROWS, WIDTH), lambda g, c: (g, 0, 0))
ACC = pltpu.VMEM((PIECE, WIDTH), F32)


def exchange(x):
    pieces = lax.all_to_all(x.reshape(NCHIP, 1, PIECE * WIDTH), CHIPS, 0, 0, tiled=True)
    return pieces.reshape(PAIRS, PROWS, WIDTH)


def scan(core, x, reverse):
    at = (lambda g, c: (STEPS - 1 - g, 0, 0)) if reverse else (lambda g, c: (g, 0, 0))
    spec = pl.BlockSpec((BLOCKS, PROWS, WIDTH), at)
    return call(
        functools.partial(scan_kernel, reverse=reverse), "scan", core, [(x, None)],
        [(PAYLOAD, spec)], scratch=[ACC],
    )[0]


def swap(x):
    return lax.ppermute(x, "c", [(0, 1), (1, 0)])


def shards(queries, keys, values, teacher, query_map, key_map):
    c = lax.axis_index("c").astype(jnp.int32)
    half = HALF * WIDTH
    gcols = GRP * WIDTH

    def others(x):
        part = lax.dynamic_slice(x, (0, (1 - c) * half), (ROWS, half))
        return swap(part.astype(F32))

    k_other, v_other = others(keys), others(values)
    q_other, t_other = others(queries), others(teacher)

    core = c.reshape(1)
    own = pl.BlockSpec((ROWS, gcols), lambda g, c: (0, c[0] * STEPS + g))
    cols = pl.BlockSpec((ROWS, gcols), lambda g, c: (0, g))
    natural = (sds((HALF, TOK, WIDTH), BF16), heads_block(TOK, WIDTH))
    features = (sds((HALF, WIDTH, TOK)), heads_block(WIDTH, TOK))
    wide = (sds((HALF, TOK, 2 * WIDTH)), heads_block(TOK, 2 * WIDTH))
    triple = (sds((HALF, TOK, 3 * WIDTH), BF16), heads_block(TOK, 3 * WIDTH))
    halved = (sds((HALF, WIDTH, TOK), BF16), heads_block(WIDTH, TOK))
    row = (sds((HALF, 8, TOK)), heads_block(8, TOK))
    grads = (sds((HALF, 64, WIDTH)), heads_block(64, WIDTH))
    weight = pl.BlockSpec((GRP, 64, WIDTH), lambda g, c: (c[0] * STEPS + g, 0, 0))
    payload = (PAYLOAD, PIECES)
    lossy = (sds((8, WIDTH)), pl.BlockSpec((8, WIDTH), lambda g, c: (0, 0)))

    def with_spec(value, like):
        return (value, like[1])

    kf, vf, phik, send = call(
        key_kernel, "keys", core,
        [(keys, own), (k_other, None), (values, own), (v_other, None),
         (key_map, weight)],
        [natural, natural, features, payload],
    )
    gathered = exchange(send)
    qf, phiq, phiqt, phiqb, part = call(
        score_kernel, "scores", core,
        [(queries, own), (q_other, cols), (query_map, weight),
         with_spec(phik, features), with_spec(vf, natural)],
        [natural, features, halved, natural, wide],
    )
    pre = exchange(scan(core, gathered, False))
    y_own, y_send, dd, dden, send, loss = call(
        out_kernel, "outs", core,
        [(pre, None), with_spec(phiqt, halved), with_spec(phiqb, natural),
         with_spec(part, wide), (teacher, own), (t_other, cols)],
        [(sds((ROWS, half), BF16), cols), (sds((ROWS, half)), cols), triple, row, payload,
         lossy],
    )
    gathered = exchange(send)
    dphik, grad_query = call(
        grid_kernel, "grids", core,
        [(pre, PIECES), with_spec(dd, triple), with_spec(dden, row),
         with_spec(phik, features), with_spec(phiq, features), with_spec(phiqt, halved),
         with_spec(vf, natural), with_spec(qf, natural)],
        [features, grads],
    )
    gathered, dphik, grad_query, y_send = lax.optimization_barrier(
        (gathered, dphik, grad_query, y_send)
    )
    y_other = swap(y_send)
    attn, = call(
        merge_kernel, "merge", core, [(y_own, cols), (y_other, cols)],
        [(sds((ROWS, HEADS * WIDTH), BF16),
          pl.BlockSpec((ROWS, HEADS * WIDTH), lambda g, c: (0, 0)))],
    )
    suf = exchange(scan(core, gathered, True))
    suf, attn = lax.optimization_barrier((suf, attn))
    send, = call(
        last_kernel, "last", core,
        [(suf, None), with_spec(vf, natural), with_spec(kf, natural),
         with_spec(phik, features), with_spec(dphik, features),
         with_spec(grad_query, grads), with_spec(loss, lossy)],
        [payload],
    )
    spread, = call(sum_kernel, "sum", core, [(exchange(send), None)], [payload], scratch=[ACC])
    total = exchange(spread)
    grad = (sds((HEADS, 64, WIDTH)), pl.BlockSpec((HALF // 2, 64, WIDTH), lambda g, c: (g, 0, 0)))
    grad_query, grad_key, loss = call(
        unpack_kernel, "unpack", core, [(total, None), (swap(total), None)],
        [grad, grad, (sds((1, 1)), pl.BlockSpec((1, 1), lambda g, c: (0, 0)))],
    )
    return attn, loss[0, 0], grad_query, grad_key


def solution(mesh):
    fine = Mesh(mesh.devices.reshape(4, 4, 4, 2), ("x", "z", "y", "c"))
    tokens = P(("x", "z", "y", "c"), None)
    return jax.shard_map(
        shards,
        mesh=fine,
        in_specs=(tokens, tokens, tokens, tokens, P(), P()),
        out_specs=(tokens, P(), P(), P()),
        check_vma=False,
    )
```

time: 209 us -> 177 us (0.85)
  blocking collectives: 69.5 us -> 39.6 us
  Pallas kernels: 70.7 us -> 47.1 us
  waiting for transfers between devices: 29.3 us -> 45.2 us
  starting transfers between devices: 31 us -> 40.9 us
  local copies, waits for them, and re-layouts: 5.87 us -> 0.98 us
    all_to_all x3 -> x2, blocking collectives: 69.5 us -> 39.6 us  [exchange(): lax.all_to_all(x.reshape(NCHIP, 1, PIECE * WIDTH), CHIPS, 0, 0, tiled=True)]
    pallas_call x10, Pallas kernels: 70.7 us -> 47.1 us  [call(): pl.pallas_call(body, grid_spec=grid, out_shape=tuple((shape for shape, _...]
    all_to_all x3 -> x4, waiting for transfers between devices: 22 us -> 37 us  [exchange(): lax.all_to_all(x.reshape(NCHIP, 1, PIECE * WIDTH), CHIPS, 0, 0, tiled=True)]
    all_to_all x3 -> x4, starting transfers between devices: 22.8 us -> 27.9 us  [exchange(): lax.all_to_all(x.reshape(NCHIP, 1, PIECE * WIDTH), CHIPS, 0, 0, tiled=True)]
    unnamed x26 -> x14, local copies, waits for them, and re-layouts: 5.87 us -> 0.98 us
    ppermute x6, starting transfers between devices: 8.15 us -> 13 us  [swap(): return lax.ppermute(x, 'c', [(0, 1), (1, 0)])]
  transfers between devices with their start and end apart: 9 -> 10, of which waited for: 6 -> 8; matrix products, arithmetic and copies ran while one was open for 0% -> 0% of each run, Pallas kernels for 15% -> 12%
where the time goes in v3:
time: 177 us; the launch traced here: 176 us
  Pallas kernels  47.1 us (27%)
  waiting for transfers between devices  45.2 us (26%)
  starting transfers between devices  40.9 us (23%)
  blocking collectives  39.6 us (22%)
    pallas_call x10, Pallas kernels, call(): pl.pallas_call(body, grid_spec=grid, out_shape=tuple((shape for shape, _...  47.1 us
    all_to_all x2, blocking collectives, exchange(): lax.all_to_all(x.reshape(NCHIP, 1, PIECE * WIDTH), CHIPS, 0, 0, tiled=True)  39.6 us
    all_to_all x4, waiting for transfers between devices, exchange(): lax.all_to_all(x.reshape(NCHIP, 1, PIECE * WIDTH), CHIPS, 0, 0, tiled=True)  37 us
    all_to_all x4, starting transfers between devices, exchange(): lax.all_to_all(x.reshape(NCHIP, 1, PIECE * WIDTH), CHIPS, 0, 0, tiled=True)  27.9 us
    ppermute x6, starting transfers between devices, swap(): return lax.ppermute(x, 'c', [(0, 1), (1, 0)])  13 us
    ppermute x6, waiting for transfers between devices, swap(): return lax.ppermute(x, 'c', [(0, 1), (1, 0)])  8.18 us
  transfers between devices with their start and end apart: 10, of which 8 were waited for; matrix products, arithmetic and copies ran while one was open for 0% of the time, Pallas kernels for 12%

profile of v3, /device:TPU:1, one launch (start us, length us, event | category | flops | bytes accessed | tf_op | source)
XLA Modules:
  0.0 176.1 jit_solution(17926719603214845618)
XLA Ops:
  0.6 1.2 dynamic-slice_convert_fusion.2
  1.9 1.5 collective-permute-start.1
  3.5 0.1 collective-permute-start
  3.6 2.1 %collective-permute-done.1.v_other = f32[128,2048]{1,0:T(8,128)S(1)} collective-permute-done((f32[128,2048]{1,0:T(8,128)S(1)}, f32[128,2048]{1,0:T(8,128)S(1)}, u32[]{:S(2)}, u32[]{:S(2)}) %collective-permute-start.1) | collective-permute-done | bytes 1048608 | tf_op jit(solution)/shard_map/ppermute | solution.py:368
  5.6 1.5 collective-permute-done.k_other
  7.1 5.1 %keys.1 = (bf16[16,256,128]{2,1,0:T(8,128)(2,1)}, bf16[16,256,128]{2,1,0:T(8,128)(2,1)}, f32[16,128,256]{2,1,0:T(8,128)}, f32[8,264,128]{2,1,0:T(8,128)}) custom-call(s32[1]{0:T(128)} %bitcast.core_ref, bf16[128,4096]{1,0:T(8,128)(2,1)} %k_own.1, f32[128,2048]{1,0:T(8,128)S(1)} %collective-permute-done.k_other, bf16[128,4096]{1,0:T(8,128)(2,1)} %v_own.1, ...), custom_call_target="tpu_custom_call" | custom-call | tf_op jit(solution)/shard_map/keys/pallas_call | solution.py:331
  12.2 11.4 %all-to-all-start = ((f32[64,1,4224]{2,1,0:T(1,128)}), f32[64,1,4224]{2,1,0:T(1,128)S(1)}, u32[]{:S(2)}, u32[]{:S(2)}) async-start(f32[64,1,4224]{2,1,0:T(1,128)} %bitcast.27), calls=%async_computation | async-start | bytes 2162688 | tf_op jit(solution)/shard_map/all_to_all | solution.py:354
  23.8 0.7 collective-permute-start.2
  24.5 16.5 %all-to-all-done = f32[64,1,4224]{2,1,0:T(1,128)S(1)} async-done(((f32[64,1,4224]{2,1,0:T(1,128)}), f32[64,1,4224]{2,1,0:T(1,128)S(1)}, u32[]{:S(2)}, u32[]{:S(2)}) %all-to-all-start) | async-done | bytes 1081376 | tf_op jit(solution)/shard_map/all_to_all | solution.py:354
  41.0 1.6 scan.2
  42.5 5.8 %all-to-all-start.1 = ((f32[64,1,4224]{2,1,0:T(1,128)}), f32[64,1,4224]{2,1,0:T(1,128)S(1)}, u32[]{:S(2)}, u32[]{:S(2)}) async-start(f32[64,1,4224]{2,1,0:T(1,128)} %bitcast.22), calls=%async_computation.1 | async-start | bytes 2162688 | tf_op jit(solution)/shard_map/all_to_all | solution.py:354
  48.5 1.8 %collective-permute-start.3 = (f32[128,2048]{1,0:T(8,128)S(1)}, f32[128,2048]{1,0:T(8,128)S(1)}, u32[]{:S(2)}, u32[]{:S(2)}) collective-permute-start(f32[128,2048]{1,0:T(8,128)S(1)} %dynamic-slice_convert_fusion), channel_id=1, source_target_pairs={{0,1},{1,0},{2,3},{3,2},{4,5},{5,4},{6,7},{7,6},{8,9},{9,8},{10,11... | collective-permute-start | bytes 3145736 | tf_op jit(solution)/shard_map/ppermute | solution.py:368
  50.2 7.4 %scores.1 = (bf16[16,256,128]{2,1,0:T(8,128)(2,1)}, f32[16,128,256]{2,1,0:T(8,128)}, bf16[16,128,256]{2,1,0:T(8,128)(2,1)}, bf16[16,256,128]{2,1,0:T(8,128)(2,1)}, f32[16,256,256]{2,1,0:T(8,128)}) custom-call(s32[1]{0:T(128)} %bitcast.core_ref, bf16[128,4096]{1,0:T(8,128)(2,1)} %q_own.1, f32[128,2048]{1,0:T(8,128)} %collective-permute-done.2.q_other, ...), custom_call_target="tpu_custom_call" | custom-call | tf_op jit(solution)/shard_map/scores/pallas_call | solution.py:331
  57.7 7.1 %all-to-all-done.1 = f32[64,1,4224]{2,1,0:T(1,128)S(1)} async-done(((f32[64,1,4224]{2,1,0:T(1,128)}), f32[64,1,4224]{2,1,0:T(1,128)S(1)}, u32[]{:S(2)}, u32[]{:S(2)}) %all-to-all-start.1) | async-done | bytes 1081376 | tf_op jit(solution)/shard_map/all_to_all | solution.py:354
  64.8 8.1 %outs.1 = (bf16[128,2048]{1,0:T(8,128)(2,1)}, f32[128,2048]{1,0:T(8,128)}, bf16[16,256,384]{2,1,0:T(8,128)(2,1)}, f32[16,8,256]{2,1,0:T(8,128)}, f32[8,264,128]{2,1,0:T(8,128)}, /*index=5*/f32[8,128]{1,0:T(8,128)}) custom-call(s32[1]{0:T(128)} %bitcast.core_ref, f32[8,264,128]{2,1,0:T(8,128)S(1)} %bitcast.14, ...), custom_call_target="tpu_custom_call" | custom-call | tf_op jit(solution)/shard_map/outs/pallas_call | solution.py:331
  72.9 5.9 %all-to-all-start.2 = ((f32[64,1,4224]{2,1,0:T(1,128)}), f32[64,1,4224]{2,1,0:T(1,128)S(1)}, u32[]{:S(2)}, u32[]{:S(2)}) async-start(f32[64,1,4224]{2,1,0:T(1,128)} %bitcast.26), calls=%async_computation.2 | async-start | bytes 2162688 | tf_op jit(solution)/shard_map/all_to_all | solution.py:354
  78.8 9.5 %grids.1 = (f32[16,128,256]{2,1,0:T(8,128)}, f32[16,64,128]{2,1,0:T(8,128)}) custom-call(s32[1]{0:T(128)} %bitcast.core_ref, f32[8,264,128]{2,1,0:T(8,128)} %bitcast.15, bf16[16,256,384]{2,1,0:T(8,128)(2,1)} %get-tuple-element.37.dd, f32[16,8,256]{2,1,0:T(8,128)} %get-tuple-element.38.dden_ref, f32[16,128,256]{2,1,0:T(8,128)} %get-tuple-element.31.phik_ref, ...), custom_call_target="tpu_custom_call" | custom-call | tf_op jit(solution)/shard_map/grids/pallas_call | solution.py:331
  88.3 7.3 %all-to-all-done.2 = f32[64,1,4224]{2,1,0:T(1,128)S(1)} async-done(((f32[64,1,4224]{2,1,0:T(1,128)}), f32[64,1,4224]{2,1,0:T(1,128)S(1)}, u32[]{:S(2)}, u32[]{:S(2)}) %all-to-all-start.2) | async-done | bytes 1081376 | tf_op jit(solution)/shard_map/all_to_all | solution.py:354
  95.6 1.6 scan.3
  97.2 4.8 %all-to-all-start.3 = ((f32[64,1,4224]{2,1,0:T(1,128)}), f32[64,1,4224]{2,1,0:T(1,128)S(1)}, u32[]{:S(2)}, u32[]{:S(2)}) async-start(f32[64,1,4224]{2,1,0:T(1,128)} %bitcast.23), calls=%async_computation.3 | async-start | bytes 2162688 | tf_op jit(solution)/shard_map/all_to_all | solution.py:354
  102.0 3.4 %collective-permute-start.4 = (f32[128,2048]{1,0:T(8,128)S(1)}, f32[128,2048]{1,0:T(8,128)S(1)}, u32[]{:S(2)}, u32[]{:S(2)}) collective-permute-start(f32[128,2048]{1,0:T(8,128)S(1)} %copy-done.6), channel_id=1, source_target_pairs={{0,1},{1,0},{2,3},{3,2},{4,5},{5,4},{6,7},{7,6},{8,9},{9,8},{10,11... | collective-permute-start | bytes 3145736 | tf_op jit(solution)/shard_map/ppermute | solution.py:368
  105.3 2.3 %collective-permute-done.4.y_other = f32[128,2048]{1,0:T(8,128)S(1)} collective-permute-done((f32[128,2048]{1,0:T(8,128)S(1)}, f32[128,2048]{1,0:T(8,128)S(1)}, u32[]{:S(2)}, u32[]{:S(2)}) %collective-permute-start.4) | collective-permute-done | bytes 1048608 | tf_op jit(solution)/shard_map/ppermute | solution.py:368
  107.6 1.0 copy-done.5
  108.6 3.2 %merge.1 = bf16[128,4096]{1,0:T(8,128)(2,1)} custom-call(s32[1]{0:T(128)} %bitcast.core_ref, bf16[128,2048]{1,0:T(8,128)(2,1)} %get-tuple-element.45.y_own, f32[128,2048]{1,0:T(8,128)} %copy-done.5), custom_call_target="tpu_custom_call" | custom-call | tf_op jit(solution)/shard_map/merge/pallas_call | solution.py:331
  111.8 6.1 %all-to-all-done.3 = f32[64,1,4224]{2,1,0:T(1,128)S(1)} async-done(((f32[64,1,4224]{2,1,0:T(1,128)}), f32[64,1,4224]{2,1,0:T(1,128)S(1)}, u32[]{:S(2)}, u32[]{:S(2)}) %all-to-all-start.3) | async-done | bytes 1081376 | tf_op jit(solution)/shard_map/all_to_all | solution.py:354
  117.9 6.9 %last.1 = f32[8,264,128]{2,1,0:T(8,128)} custom-call(s32[1]{0:T(128)} %bitcast.core_ref, f32[8,264,128]{2,1,0:T(8,128)S(1)} %bitcast.21, bf16[16,256,128]{2,1,0:T(8,128)(2,1)} %get-tuple-element.32.vf, bf16[16,256,128]{2,1,0:T(8,128)(2,1)} %get-tuple-element.49.kf, f32[16,128,256]{2,1,0:T(8,128)} %get-tuple-element.31.phik_ref, ...), custom_call_target="tpu_custom_call" | custom-call | tf_op jit(solution)/shard_map/last/pallas_call | solution.py:331
  124.8 20.4 %all_to_all.30 = f32[64,1,4224]{2,1,0:T(1,128)S(1)} all-to-all(f32[64,1,4224]{2,1,0:T(1,128)} %bitcast.25), channel_id=1, replica_groups=mesh['x'=4,'z'=4,'y'=4,'c'=2] {'x','z','y'}, dimensions={0} | all-to-all | bytes 2162688 | tf_op jit(solution)/shard_map/all_to_all | solution.py:354
  145.3 1.7 sum.1
  147.0 19.2 %all_to_all.31 = f32[64,1,4224]{2,1,0:T(1,128)S(1)} all-to-all(f32[64,1,4224]{2,1,0:T(1,128)} %bitcast.24), channel_id=1, replica_groups=mesh['x'=4,'z'=4,'y'=4,'c'=2] {'x','z','y'}, dimensions={0} | all-to-all | bytes 2162688 | tf_op jit(solution)/shard_map/all_to_all | solution.py:354
  166.2 5.6 %collective-permute-start.5 = (f32[8,264,128]{2,1,0:T(8,128)S(1)}, f32[8,264,128]{2,1,0:T(8,128)S(1)}, u32[]{:S(2)}, u32[]{:S(2)}) collective-permute-start(f32[8,264,128]{2,1,0:T(8,128)S(1)} %bitcast.18), channel_id=1, source_target_pairs={{0,1},{1,0},{2,3},{3,2},{4,5},{5,4},{6,7},{7,6},{8,9},{9,8},{10,11... | collective-permute-start | bytes 3244040 | tf_op jit(solution)/shard_map/ppermute | solution.py:368
  171.8 2.3 %collective-permute-done.5.theirs = f32[8,264,128]{2,1,0:T(8,128)S(1)} collective-permute-done((f32[8,264,128]{2,1,0:T(8,128)S(1)}, f32[8,264,128]{2,1,0:T(8,128)S(1)}, u32[]{:S(2)}, u32[]{:S(2)}) %collective-permute-start.5) | collective-permute-done | bytes 1081376 | tf_op jit(solution)/shard_map/ppermute | solution.py:368
  174.1 2.0 %unpack.1 = (f32[32,64,128]{2,1,0:T(8,128)}, f32[32,64,128]{2,1,0:T(8,128)}, f32[1,1]{1,0:T(1,128)}) custom-call(s32[1]{0:T(128)} %bitcast.core_ref, f32[8,264,128]{2,1,0:T(8,128)S(1)} %bitcast.19, f32[8,264,128]{2,1,0:T(8,128)S(1)} %collective-permute-done.5.theirs), custom_call_target="tpu_custom_call" | custom-call | tf_op jit(solution)/shard_map/unpack/pallas_call | solution.py:331
  (18 shorter events, 0.3 us)
Async XLA Ops:
  0.6 2.7 %copy-start.1 = (bf16[128,4096]{1,0:T(8,128)(2,1)S(1)}, bf16[128,4096]{1,0:T(8,128)(2,1)}, u32[]{:S(2)}) copy-start(bf16[128,4096]{1,0:T(8,128)(2,1)} %k_own.1) | copy-start | bytes 3145732
  1.9 3.7 %collective-permute-start.1 = (f32[128,2048]{1,0:T(8,128)S(1)}, f32[128,2048]{1,0:T(8,128)S(1)}, u32[]{:S(2)}, u32[]{:S(2)}) collective-permute-start(f32[128,2048]{1,0:T(8,128)S(1)} %dynamic-slice_convert_fusion.2), channel_id=1, source_target_pairs={{0,1},{1,0},{2,3},{3,2},{4,5},{5,4},{6,7},{7,6},{8,9},{9,8},{10,11... | collective-permute-start | bytes 3145736 | tf_op jit(solution)/shard_map/ppermute | solution.py:368
  3.5 3.7 %collective-permute-start = (f32[128,2048]{1,0:T(8,128)S(1)}, f32[128,2048]{1,0:T(8,128)S(1)}, u32[]{:S(2)}, u32[]{:S(2)}) collective-permute-start(f32[128,2048]{1,0:T(8,128)S(1)} %dynamic-slice_convert_fusion.3), channel_id=1, source_target_pairs={{0,1},{1,0},{2,3},{3,2},{4,5},{5,4},{6,7},{7,6},{8,9},{9,8},{10,11... | collective-permute-start | bytes 3145736 | tf_op jit(solution)/shard_map/ppermute | solution.py:368
  12.2 11.4 %copy-start.3 = (bf16[128,4096]{1,0:T(8,128)(2,1)S(1)}, bf16[128,4096]{1,0:T(8,128)(2,1)}, u32[]{:S(2)}) copy-start(bf16[128,4096]{1,0:T(8,128)(2,1)} %q_own.1) | copy-start | bytes 3145732
  12.2 28.7 %all-to-all-start = ((f32[64,1,4224]{2,1,0:T(1,128)}), f32[64,1,4224]{2,1,0:T(1,128)S(1)}, u32[]{:S(2)}, u32[]{:S(2)}) async-start(f32[64,1,4224]{2,1,0:T(1,128)} %bitcast.27), calls=%async_computation | async-start | bytes 2162688 | tf_op jit(solution)/shard_map/all_to_all | solution.py:354
  23.8 26.5 %collective-permute-start.2 = (f32[128,2048]{1,0:T(8,128)S(1)}, f32[128,2048]{1,0:T(8,128)}, u32[]{:S(2)}, u32[]{:S(2)}) collective-permute-start(f32[128,2048]{1,0:T(8,128)S(1)} %dynamic-slice_convert_fusion.1), channel_id=1, source_target_pairs={{0,1},{1,0},{2,3},{3,2},{4,5},{5,4},{6,7},{7,6},{8,9},{9,8},{10,11... | collective-permute-start | bytes 3145736 | tf_op jit(solution)/shard_map/ppermute | solution.py:368
  42.5 5.8 %copy-start.2 = (bf16[128,4096]{1,0:T(8,128)(2,1)S(1)}, bf16[128,4096]{1,0:T(8,128)(2,1)}, u32[]{:S(2)}) copy-start(bf16[128,4096]{1,0:T(8,128)(2,1)} %t_own.1) | copy-start | bytes 3145732
  42.5 22.3 %all-to-all-start.1 = ((f32[64,1,4224]{2,1,0:T(1,128)}), f32[64,1,4224]{2,1,0:T(1,128)S(1)}, u32[]{:S(2)}, u32[]{:S(2)}) async-start(f32[64,1,4224]{2,1,0:T(1,128)} %bitcast.22), calls=%async_computation.1 | async-start | bytes 2162688 | tf_op jit(solution)/shard_map/all_to_all | solution.py:354
  48.5 9.2 %collective-permute-start.3 = (f32[128,2048]{1,0:T(8,128)S(1)}, f32[128,2048]{1,0:T(8,128)S(1)}, u32[]{:S(2)}, u32[]{:S(2)}) collective-permute-start(f32[128,2048]{1,0:T(8,128)S(1)} %dynamic-slice_convert_fusion), channel_id=1, source_target_pairs={{0,1},{1,0},{2,3},{3,2},{4,5},{5,4},{6,7},{7,6},{8,9},{9,8},{10,11... | collective-permute-start | bytes 3145736 | tf_op jit(solution)/shard_map/ppermute | solution.py:368
  57.7 7.1 %copy-start.4 = (f32[128,2048]{1,0:T(8,128)}, f32[128,2048]{1,0:T(8,128)S(1)}, u32[]{:S(2)}) copy-start(f32[128,2048]{1,0:T(8,128)S(1)} %collective-permute-done.3.t_other) | copy-start | bytes 3145732
  64.8 8.1 %copy-start = (f32[64,1,4224]{2,1,0:T(1,128)}, f32[64,1,4224]{2,1,0:T(1,128)S(1)}, u32[]{:S(2)}) copy-start(f32[64,1,4224]{2,1,0:T(1,128)S(1)} %all-to-all-done.1) | copy-start | bytes 3244036
  72.9 22.7 %all-to-all-start.2 = ((f32[64,1,4224]{2,1,0:T(1,128)}), f32[64,1,4224]{2,1,0:T(1,128)S(1)}, u32[]{:S(2)}, u32[]{:S(2)}) async-start(f32[64,1,4224]{2,1,0:T(1,128)} %bitcast.26), calls=%async_computation.2 | async-start | bytes 2162688 | tf_op jit(solution)/shard_map/all_to_all | solution.py:354
  97.2 4.8 %copy-start.6 = (f32[128,2048]{1,0:T(8,128)S(1)}, f32[128,2048]{1,0:T(8,128)}, u32[]{:S(2)}) copy-start(f32[128,2048]{1,0:T(8,128)} %get-tuple-element.46) | copy-start | bytes 3145732
  97.2 20.8 %all-to-all-start.3 = ((f32[64,1,4224]{2,1,0:T(1,128)}), f32[64,1,4224]{2,1,0:T(1,128)S(1)}, u32[]{:S(2)}, u32[]{:S(2)}) async-start(f32[64,1,4224]{2,1,0:T(1,128)} %bitcast.23), calls=%async_computation.3 | async-start | bytes 2162688 | tf_op jit(solution)/shard_map/all_to_all | solution.py:354
  102.0 5.6 %collective-permute-start.4 = (f32[128,2048]{1,0:T(8,128)S(1)}, f32[128,2048]{1,0:T(8,128)S(1)}, u32[]{:S(2)}, u32[]{:S(2)}) collective-permute-start(f32[128,2048]{1,0:T(8,128)S(1)} %copy-done.6), channel_id=1, source_target_pairs={{0,1},{1,0},{2,3},{3,2},{4,5},{5,4},{6,7},{7,6},{8,9},{9,8},{10,11... | collective-permute-start | bytes 3145736 | tf_op jit(solution)/shard_map/ppermute | solution.py:368
  107.6 1.0 copy-start.5
  166.2 7.9 %collective-permute-start.5 = (f32[8,264,128]{2,1,0:T(8,128)S(1)}, f32[8,264,128]{2,1,0:T(8,128)S(1)}, u32[]{:S(2)}, u32[]{:S(2)}) collective-permute-start(f32[8,264,128]{2,1,0:T(8,128)S(1)} %bitcast.18), channel_id=1, source_target_pairs={{0,1},{1,0},{2,3},{3,2},{4,5},{5,4},{6,7},{7,6},{8,9},{9,8},{10,11... | collective-permute-start | bytes 3244040 | tf_op jit(solution)/shard_map/ppermute | solution.py:368

commit v4 on v3

v4 whole, which is shorter than its diff:
```python
import functools

import jax
import jax.numpy as jnp
from jax import lax
from jax.experimental import pallas as pl
from jax.experimental.pallas import tpu as pltpu
from jax.sharding import Mesh
from jax.sharding import PartitionSpec as P

F32 = jnp.float32
BF16 = jnp.bfloat16
CHIPS = ("x", "z", "y")
NCHIP = 64
HEADS = 32
HALF = 16
ROWS = 128
TOK = 256
WIDTH = 128
PIECE = 33
PAIRS = HALF // 2
GROUPS = ((4, 12), (12, 4))
PROWS = 2 * 4 * PIECE

NN = ((1,), (0,))
NT = ((1,), (1,))


def dot(a, b, dims=NN):
    return lax.dot_general(a, b, (dims, ((), ())), preferred_element_type=F32)


def two_parts(x):
    high = x.astype(BF16)
    return high, (x - high.astype(F32)).astype(BF16)


def soft_maps(logits):
    e_one = jnp.exp(logits - jnp.max(logits, axis=0, keepdims=True))
    e_two = jnp.exp(jnp.min(logits, axis=0, keepdims=True) - logits)
    one = e_one * (1.0 / jnp.sum(e_one, axis=0, keepdims=True))
    two = e_two * (1.0 / jnp.sum(e_two, axis=0, keepdims=True))
    return jnp.concatenate([one, two], axis=0)


def soft_back(phi, dphi, x):
    prod = phi * dphi
    one = prod[:64] - phi[:64] * jnp.sum(prod[:64], axis=0, keepdims=True)
    two = prod[64:] - phi[64:] * jnp.sum(prod[64:], axis=0, keepdims=True)
    return dot((one - two).astype(BF16), x)


def columns(h):
    return slice(h * WIDTH, (h + 1) * WIDTH)


def both_cores(own, other, h):
    return jnp.concatenate(
        [own[:, columns(h)], other[:, columns(h)].astype(BF16)], axis=0
    )


def put_state(ref, h, state, row):
    pair = h // 2
    for q in range(4):
        at = (4 * (h % 2) + q) * PIECE
        ref[pair, at : at + 32, :] = state[32 * q : 32 * q + 32]
        ref[pair, at + 32 : at + 33, :] = row


def get_state(ref, h):
    first = 4 * (h % 2)
    parts = [ref[h // 2, (first + q) * PIECE : (first + q) * PIECE + 32, :] for q in range(4)]
    at = first * PIECE + 32
    return jnp.concatenate(parts, axis=0), ref[h // 2, at : at + 1, :]


def as_column(row, lanes):
    return jnp.broadcast_to(row, (lanes, row.shape[1])).T


def as_row(column):
    return jnp.broadcast_to(column, (column.shape[0], WIDTH)).T[:1]


def twice(x):
    return jnp.concatenate([x, x], axis=1)


def causal(core):
    shift = core * ROWS
    at_query = lax.broadcasted_iota(jnp.int32, (TOK, TOK), 0) ^ shift
    at_key = lax.broadcasted_iota(jnp.int32, (TOK, TOK), 1) ^ shift
    return at_query >= at_key


def key_kernel(core, k_own, k_other, v_own, v_other, w_ref, kf, vf, phik_ref, send):

    def head(h):
        k = both_cores(k_own, k_other, h)
        kf[h] = k
        logits = dot(w_ref[h], k, NT)
        yield
        phik = soft_maps(logits)
        phik_ref[h] = phik
        phikb = phik.astype(BF16)
        v = both_cores(v_own, v_other, h)
        vf[h] = v
        yield
        state = dot(phikb, v)
        yield
        put_state(send, h, state, as_row(jnp.sum(phik, axis=1, keepdims=True)))

    return head


def score_kernel(
    core, q_own, q_other, w_ref, phik_ref, vf, qf, phiq_ref, phiqb_ref, den_ref, num_ref
):
    mask = causal(core)
    ones = jnp.ones((8, 2 * TOK), BF16)

    def head(h):
        q = both_cores(q_own, q_other, h)
        qf[h] = q
        logits = dot(w_ref[h], q, NT)
        yield
        phiq = soft_maps(logits)
        phiq_ref[h] = phiq
        phiqb = phiq.astype(BF16).T
        phiqb_ref[h] = phiqb
        yield
        scores = dot(phiqb, phik_ref[h].astype(BF16))
        yield
        high, low = two_parts(jnp.where(mask, scores, 0.0))
        num_ref[h] = dot(high, vf[h])
        den_ref[h] = dot(ones, jnp.concatenate([high, low], axis=1), NT)

    return head


def out_kernel(
    core, pre, num_ref, phiq_ref, phiqb_ref, den_ref, t_own, t_other,
    y_own, y_send, dnum_ref, dden_ref, send, loss_ref,
):
    ones = jnp.ones((8, 2 * WIDTH), BF16)
    scale = 2.0 / (HEADS * WIDTH)
    loss_ref[...] = jnp.zeros_like(loss_ref)

    def head(h):
        state, norm = get_state(pre, h)
        carried = dot(phiqb_ref[h], state.astype(BF16))
        down = as_column(norm, WIDTH)
        yield
        phiq = phiq_ref[h]
        before = jnp.sum(phiq * twice(down), axis=0, keepdims=True)
        inv = as_column(1.0 / (den_ref[h][:1] + before), WIDTH)
        yield
        y = (num_ref[h] + carried) * inv
        y_own[:, columns(h)] = y[:ROWS].astype(BF16)
        y_send[:, columns(h)] = y[ROWS:]
        err = y - both_cores(t_own, t_other, h).astype(F32)
        loss_ref[...] += jnp.sum((err * err).reshape(TOK // 8, 8, WIDTH), axis=0)
        dnum = (scale * err) * inv
        dnumb = dnum.astype(BF16)
        dnum_ref[h] = dnumb
        high, low = two_parts(dnum * y)
        both = jnp.concatenate([high, low], axis=1)
        yield
        dden = -dot(ones, both, NT)
        rev = dot(phiq_ref[h].astype(BF16), dnumb)
        yield
        dden_ref[h] = dden
        rnorm = as_row(jnp.sum(phiq_ref[h] * dden[:1], axis=1, keepdims=True))
        yield
        put_state(send, h, rev, rnorm)

    return head


def out_kernel(
    core, pre, num_ref, phiqt_ref, phiqb_ref, den_ref, t_own, t_other,
    y_own, y_send, dnum_ref, dden_ref, send, loss_ref,
):
    ones = jnp.ones((8, 2 * WIDTH), BF16)
    none = jnp.zeros((WIDTH, WIDTH), BF16)
    scale = 2.0 / (HEADS * WIDTH)
    loss_ref[...] = jnp.zeros_like(loss_ref)

    def head(h):
        state, norm = get_state(pre, h)
        high, low = two_parts(as_column(norm, WIDTH))
        den = as_column(den_ref[h][:1], WIDTH)
        right = jnp.concatenate(
            [
                jnp.concatenate([state.astype(BF16), high], axis=1),
                jnp.concatenate([none, low], axis=1),
            ],
            axis=0,
        )
        yield
        both = dot(twice(phiqb_ref[h]), right)
        yield
        inv = 1.0 / (den + both[:, WIDTH:])
        y = (num_ref[h] + both[:, :WIDTH]) * inv
        y_own[:, columns(h)] = y[:ROWS].astype(BF16)
        y_send[:, columns(h)] = y[ROWS:]
        err = y - both_cores(t_own, t_other, h).astype(F32)
        loss_ref[...] += jnp.sum((err * err).reshape(TOK // 8, 8, WIDTH), axis=0)
        dnum = (scale * err) * inv
        dnumb = dnum.astype(BF16)
        dnum_ref[h] = dnumb
        high, low = two_parts(dnum * y)
        both = jnp.concatenate([high, low], axis=1)
        yield
        dden = -dot(ones, both, NT)
        rev = dot(phiqt_ref[h], dnumb)
        yield
        dden_ref[h] = dden
        high, low = two_parts(dden)
        phiqt = phiqt_ref[h]
        rnorm = dot(jnp.concatenate([high, low], axis=1), twice(phiqt), NT)
        yield
        put_state(send, h, rev, rnorm[:1])

    return head


def grid_kernel(
    core, dnum_ref, vf, dden_ref, phiq_ref, phik_ref, pre, qf, grad_ref, dphik_ref,
):
    mask = causal(core)

    def head(h):
        grid = dot(dnum_ref[h], vf[h], NT)
        column = as_column(dden_ref[h][:1], WIDTH)
        yield
        gridb = jnp.where(mask, grid + twice(column), 0.0).astype(BF16)
        dphik_ref[h] = dot(phiq_ref[h].astype(BF16), gridb)
        state, norm = get_state(pre, h)
        left = jnp.concatenate([phik_ref[h].astype(BF16), state.astype(BF16)], axis=1)
        dphiq = dot(left, jnp.concatenate([gridb, dnum_ref[h]], axis=1), NT)
        down = twice(as_column(norm, WIDTH))
        yield
        grad_ref[h] = soft_back(phiq_ref[h], dphiq + down * dden_ref[h][:1], qf[h])

    return head


def merge_kernel(core, y_own, y_other, attn_mine, attn_theirs):
    del core

    def head(h):
        attn_mine[:, columns(h)] = y_own[:, columns(h)]
        attn_theirs[:, columns(h)] = y_other[:, columns(h)].astype(BF16)
        yield

    return head


def last_kernel(
    core, suf, vf, phik_ref, kf, dphik_ref, grad_ref, loss_ref, loss_other, send
):
    row = jnp.sum(loss_ref[...] + loss_other[...], axis=0, keepdims=True)

    def head(h):
        state, norm = get_state(suf, h)
        carried = dot(state.astype(BF16), vf[h], NT) + twice(as_column(norm, WIDTH))
        yield
        grad_key = soft_back(phik_ref[h], dphik_ref[h] + carried, kf[h])
        yield
        put_state(send, h, jnp.concatenate([grad_ref[h], grad_key], axis=0), row)

    return head


def scan_kernel(core, x_ref, o_ref, *, reverse):
    del core
    acc = jnp.zeros((PIECE, WIDTH), F32)

    def head(h):
        nonlocal acc
        for j in range(3, -1, -1) if reverse else range(4):
            at = (4 * (h % 2) + j) * PIECE
            o_ref[h // 2, at : at + PIECE, :] = acc
            acc = acc + x_ref[h // 2, at : at + PIECE, :]
        yield

    return head


def sum_kernel(core_ref, x_ref, o_ref, buf, sems):
    del core_ref
    parts = []
    for b in range(PAIRS):
        part = x_ref[b, :PIECE, :]
        for j in range(1, 8):
            part = part + x_ref[b, PIECE * j : PIECE * (j + 1), :]
        parts.append(part)
    while len(parts) > 1:
        parts = [x + y for x, y in zip(parts[::2], parts[1::2])]
    for j in range(8):
        buf[PIECE * j : PIECE * (j + 1), :] = parts[0]
    copies = [pltpu.make_async_copy(buf, o_ref.at[b], sems.at[b]) for b in range(PAIRS)]
    for copy in copies:
        copy.start()
    for copy in copies:
        copy.wait()


def unpack_kernel(core, *refs):
    del core
    src, gq, gk = refs[0], refs[-2], refs[-1]

    def head(h):
        state, _ = get_state(src, h)
        gq[h] = state[:64]
        gk[h] = state[64:]
        yield

    return head


class Block:
    def __init__(self, shape, view, cut=None):
        self.shape = shape
        self.view = view
        self.cut = cut or (lambda ref, core, start, count: view(ref, start, count))


def heads_block(*tail):
    return Block((HALF,) + tail, lambda ref, start, count: ref.at[pl.ds(start, count)])


def core_heads(*tail, other=False):
    def cut(ref, core, start, count):
        return ref.at[pl.ds(((1 - core) if other else core) * HALF + start, count)]

    return Block((HALF,) + tail, heads_block(*tail).view, cut)


def group_columns(core_part=None):
    def view(ref, start, count):
        return ref.at[:, pl.ds(start * WIDTH, count * WIDTH)]

    def cut(ref, core, start, count):
        side = core if core_part == "own" else 1 - core
        at = pl.multiple_of(side * HALF * WIDTH + start * WIDTH, WIDTH)
        return ref.at[:, pl.ds(at, count * WIDTH)]

    return Block((ROWS, HALF * WIDTH), view, cut if core_part else None)


def pieces_block():
    def view(ref, start, count):
        return ref.at[pl.ds(start // 2, count // 2)]

    return Block((PAIRS, PROWS, WIDTH), view)


def is_block(spec):
    return isinstance(spec, Block)


def stream(*refs, body, ins, outs, n_out, groups, backward):
    core = refs[0][0]
    arrays = refs[1 : 1 + len(ins)]
    results = refs[1 + len(ins) : 1 + len(ins) + n_out]
    in_sems, out_sems, *buffers = refs[1 + len(ins) + n_out :]
    given = [buffers.pop(0) if is_block(spec) else ref for spec, ref in zip(ins, arrays)]
    streamed = [at for at, _ in outs]
    whole = [ref for n, ref in enumerate(results) if n not in streamed]
    heads = list(range(HALF))
    if backward:
        heads.reverse()

    def spans_of(counts):
        spans = []
        for g, count in enumerate(counts):
            part = heads[sum(counts[:g]) : sum(counts[:g]) + count]
            spans.append((min(part), count))
        return spans

    spans_in, spans_out = spans_of(groups[0]), spans_of(groups[1])

    def copies_in(g):
        return [
            pltpu.make_async_copy(
                spec.cut(ref, core, *spans_in[g]), spec.view(buf, *spans_in[g]), in_sems.at[n, g]
            )
            for n, (spec, ref, buf) in enumerate(zip(ins, arrays, given))
            if is_block(spec)
        ]

    def copies_out(g):
        return [
            pltpu.make_async_copy(
                spec.view(buf, *spans_out[g]),
                spec.cut(results[at], core, *spans_out[g]),
                out_sems.at[n, g],
            )
            for n, ((at, spec), buf) in enumerate(zip(outs, buffers))
        ]

    for g in range(len(spans_in)):
        for copy in copies_in(g):
            copy.start()
    head = body(core, *given, *buffers, *whole)
    done = 0
    ends = [sum(groups[1][: g + 1]) for g in range(len(spans_out))]

    running = []

    def advance():
        nonlocal done
        for item in list(running):
            if next(item, "end") == "end":
                running.remove(item)
                done += 1
                if done in ends:
                    for copy in copies_out(ends.index(done)):
                        copy.start()

    for g, (_, count) in enumerate(spans_in):
        for copy in copies_in(g):
            copy.wait()
        for _ in range(count):
            running.append(head(heads.pop(0)))
            advance()
    while running:
        advance()
    for g in range(len(spans_out)):
        for copy in copies_out(g):
            copy.wait()


def raw_call(body, name, core, values, specs, shapes, scratch, aliases=()):
    spaces = {None: pltpu.VMEM}
    constrained = [
        pltpu.with_memory_space_constraint(v, spaces.get(s, pltpu.HBM))
        for v, s in zip(values, specs)
    ]
    return pl.pallas_call(
        body,
        in_specs=[pl.BlockSpec(memory_space=pltpu.SMEM)]
        + [pl.BlockSpec(memory_space=spaces.get(s, pltpu.HBM)) for s in specs],
        out_specs=tuple(pl.BlockSpec(memory_space=shape.memory_space) for shape in shapes),
        out_shape=tuple(shapes),
        scratch_shapes=scratch,
        name=name,
        input_output_aliases=dict(aliases),
        compiler_params=pltpu.CompilerParams(vmem_limit_bytes=48 * 1024 * 1024),
    )(core, *constrained)


def call(
    body, name, core, args, shapes, outs, aliases=(), groups=GROUPS, backward=False
):
    ins = [spec for _, spec in args]
    scratch = [
        pltpu.SemaphoreType.DMA((len(ins), len(groups[0]))),
        pltpu.SemaphoreType.DMA((len(outs), len(groups[1]))),
    ]
    scratch += [pltpu.VMEM(spec.shape, value.dtype) for value, spec in args if is_block(spec)]
    scratch += [pltpu.VMEM(spec.shape, shapes[at].dtype) for at, spec in outs]
    kernel = functools.partial(
        stream, body=body, ins=ins, outs=outs, n_out=len(shapes), groups=groups,
        backward=backward,
    )
    return raw_call(kernel, name, core, [v for v, _ in args], ins, shapes, scratch, aliases)


def sds(shape, dtype=F32):
    return pltpu.HBM(shape, dtype)


PAYLOAD = sds((PAIRS, PROWS, WIDTH))


def exchange(x):
    pieces = lax.all_to_all(x.reshape(NCHIP, 1, PIECE * WIDTH), CHIPS, 0, 0, tiled=True)
    return pieces.reshape(PAIRS, PROWS, WIDTH)


def scan(core, x, reverse):
    body = functools.partial(scan_kernel, reverse=reverse)
    return call(
        body, "scan", core, [(x, None)], [PAYLOAD], [(0, pieces_block())], backward=reverse
    )[0]


def swap(x):
    return lax.ppermute(x, "c", [(0, 1), (1, 0)])


def shards(queries, keys, values, teacher, query_map, key_map):
    c = lax.axis_index("c").astype(jnp.int32)
    core = c.reshape(1)
    half = HALF * WIDTH

    def others(x):
        part = lax.dynamic_slice(x, (0, (1 - c) * half), (ROWS, half))
        return swap(part.astype(F32))

    k_other, v_other = others(keys), others(values)
    q_other, t_other = others(queries), others(teacher)

    def run(body, name, args, results, groups=GROUPS):
        shapes = [shape for shape, _ in results]
        outs = [(n, spec) for n, (_, spec) in enumerate(results) if spec is not None]
        return call(body, name, core, args, shapes, outs, groups=groups)

    own = group_columns("own")
    cols = group_columns()
    natural = (sds((HALF, TOK, WIDTH), BF16), heads_block(TOK, WIDTH))
    features = (sds((HALF, WIDTH, TOK)), heads_block(WIDTH, TOK))
    row = (sds((HALF, 8, TOK)), heads_block(8, TOK))
    grads = (sds((HALF, 64, WIDTH)), heads_block(64, WIDTH))
    weight = core_heads(64, WIDTH)
    payload = (PAYLOAD, pieces_block())
    lossy = (pltpu.VMEM((8, WIDTH), F32), None)

    kf, vf, phik, send = run(
        key_kernel, "keys",
        [(keys, own), (k_other, None), (values, own), (v_other, None), (key_map, weight)],
        [natural, natural, features, payload],
    )
    gathered = exchange(send)
    qf, phiq, phiqb, den, num = run(
        score_kernel, "scores",
        [(queries, own), (q_other, cols), (query_map, weight), (phik, features[1]),
         (vf, natural[1])],
        [natural, features, natural, row, (pltpu.VMEM((HALF, TOK, WIDTH), F32), None)],
    )
    pre = exchange(scan(core, gathered, False))
    y_own, y_send, dnum, dden, send, loss = run(
        out_kernel, "outs",
        [(pre, None), (num, None), (phiq, features[1]), (phiqb, natural[1]), (den, row[1]),
         (teacher, own), (t_other, cols)],
        [(sds((ROWS, half), BF16), cols), (sds((ROWS, half)), cols), natural, row, payload,
         lossy],
    )
    loss_other = swap(loss)
    gathered = exchange(send)
    grad_query, dphik = run(
        grid_kernel, "grids",
        [(dnum, natural[1]), (vf, natural[1]), (dden, row[1]), (phiq, features[1]),
         (phik, features[1]), (pre, payload[1]), (qf, natural[1])],
        [grads, (pltpu.VMEM((HALF, WIDTH, TOK), F32), None)],
    )
    gathered, dphik, grad_query, y_send = lax.optimization_barrier(
        (gathered, dphik, grad_query, y_send)
    )
    y_other = swap(y_send)
    suf, y_other = lax.optimization_barrier((exchange(scan(core, gathered, True)), y_other))
    send, = run(
        last_kernel, "last",
        [(suf, None), (vf, natural[1]), (phik, features[1]), (kf, natural[1]),
         (dphik, None), (grad_query, grads[1]), (loss, None), (loss_other, None)],
        [payload],
    )
    attn, = call(
        merge_kernel, "merge", core, [(y_own, cols), (y_other, None)],
        [sds((ROWS, HEADS * WIDTH), BF16)],
        [(0, own), (0, group_columns("other"))],
    )
    gathered, attn = lax.optimization_barrier((exchange(send), attn))
    spread, = raw_call(
        sum_kernel, "sum", core, [gathered], [None], [PAYLOAD],
        [pltpu.VMEM((PROWS, WIDTH), F32), pltpu.SemaphoreType.DMA((PAIRS,))],
    )
    total = exchange(spread)
    theirs = swap(total)
    loss = jnp.sum(total[0, 32]) * (1.0 / (HEADS * WIDTH) / (NCHIP * TOK))
    grad = sds((HEADS, 64, WIDTH))
    mine, other = core_heads(64, WIDTH), core_heads(64, WIDTH, other=True)
    grad_query, grad_key = call(
        unpack_kernel, "unpack_mine", core, [(total, None)], [grad, grad],
        [(0, mine), (1, mine)],
    )
    grad_query, grad_key = call(
        unpack_kernel, "unpack", core,
        [(theirs, None), (grad_query, pltpu.HBM), (grad_key, pltpu.HBM)], [grad, grad],
        [(0, other), (1, other)], aliases=[(2, 0), (3, 1)],
    )
    return attn, loss, grad_query, grad_key


def solution(mesh):
    fine = Mesh(mesh.devices.reshape(4, 4, 4, 2), ("x", "z", "y", "c"))
    tokens = P(("x", "z", "y", "c"), None)
    return jax.shard_map(
        shards,
        mesh=fine,
        in_specs=(tokens, tokens, tokens, tokens, P(), P()),
        out_specs=(tokens, P(), P(), P()),
        check_vma=False,
    )
```

time: 177 us -> 172 us (0.972)
  blocking collectives: 39.6 us -> 19.2 us
  waiting for transfers between devices: 45.2 us -> 59.5 us
  Pallas kernels: 47.1 us -> 40.2 us
  starting transfers between devices: 40.9 us -> 46.2 us
  between operations: 0.76 us -> 2.66 us
    all_to_all x2 -> x1, blocking collectives: 39.6 us -> 19.2 us  [exchange(): lax.all_to_all(x.reshape(NCHIP, 1, PIECE * WIDTH), CHIPS, 0, 0, tiled=True)]
    all_to_all x4 -> x5, waiting for transfers between devices: 37 us -> 53.4 us  [exchange(): lax.all_to_all(x.reshape(NCHIP, 1, PIECE * WIDTH), CHIPS, 0, 0, tiled=True)]
    pallas_call x10 -> x11, Pallas kernels: 47.1 us -> 40.2 us  [raw_call(): pl.pallas_call(body, in_specs=[pl.BlockSpec(memory_space=pltpu.SMEM)] + [...]
    all_to_all x4 -> x5, starting transfers between devices: 27.9 us -> 33.1 us  [exchange(): lax.all_to_all(x.reshape(NCHIP, 1, PIECE * WIDTH), CHIPS, 0, 0, tiled=True)]
    ppermute x6 -> x7, waiting for transfers between devices: 8.18 us -> 6.01 us  [swap(): return lax.ppermute(x, 'c', [(0, 1), (1, 0)])]
    ppermute x6 -> x7, starting transfers between devices: 13 us -> 13.1 us  [swap(): return lax.ppermute(x, 'c', [(0, 1), (1, 0)])]
  transfers between devices with their start and end apart: 10 -> 12, of which waited for: 8 -> 8; matrix products, arithmetic and copies ran while one was open for 0% -> 1% of each run, Pallas kernels for 12% -> 12%
where the time goes in v4:
time: 172 us; the launch traced here: 171 us
  waiting for transfers between devices  59.5 us (35%)
  starting transfers between devices  46.2 us (27%)
  Pallas kernels  40.2 us (23%)
  blocking collectives  19.2 us (11%)
  between operations  2.66 us (2%)
  other arithmetic  2.13 us (1%)
    all_to_all x5, waiting for transfers between devices, exchange(): lax.all_to_all(x.reshape(NCHIP, 1, PIECE * WIDTH), CHIPS, 0, 0, tiled=True)  53.4 us
    pallas_call x11, Pallas kernels, raw_call(): pl.pallas_call(body, in_specs=[pl.BlockSpec(memory_space=pltpu.SMEM)] + [...  40.2 us
    all_to_all x5, starting transfers between devices, exchange(): lax.all_to_all(x.reshape(NCHIP, 1, PIECE * WIDTH), CHIPS, 0, 0, tiled=True)  33.1 us
    all_to_all x1, blocking collectives, exchange(): lax.all_to_all(x.reshape(NCHIP, 1, PIECE * WIDTH), CHIPS, 0, 0, tiled=True)  19.2 us
    ppermute x7, starting transfers between devices, swap(): return lax.ppermute(x, 'c', [(0, 1), (1, 0)])  13.1 us
    ppermute x7, waiting for transfers between devices, swap(): return lax.ppermute(x, 'c', [(0, 1), (1, 0)])  6.01 us
  transfers between devices with their start and end apart: 12, of which 8 were waited for; matrix products, arithmetic and copies ran while one was open for 1% of the time, Pallas kernels for 12%

profile of v4, /device:TPU:1, one launch (start us, length us, event | category | flops | bytes accessed | tf_op | source)
XLA Modules:
  0.0 170.8 jit_solution(17421198404874222638)
XLA Ops:
  0.6 1.2 dynamic-slice_convert_fusion.2
  1.9 1.5 collective-permute-start.1
  3.6 2.1 %collective-permute-done.1.refs_4_ = f32[128,2048]{1,0:T(8,128)S(1)} collective-permute-done((f32[128,2048]{1,0:T(8,128)S(1)}, f32[128,2048]{1,0:T(8,128)S(1)}, u32[]{:S(2)}, u32[]{:S(2)}) %collective-permute-start.1) | collective-permute-done | bytes 1048608 | tf_op jit(solution)/shard_map/ppermute | solution.py:493
  5.6 1.5 collective-permute-done.refs_2_
  7.1 4.4 %keys.1 = (bf16[16,256,128]{2,1,0:T(8,128)(2,1)}, bf16[16,256,128]{2,1,0:T(8,128)(2,1)}, f32[16,128,256]{2,1,0:T(8,128)}, f32[8,264,128]{2,1,0:T(8,128)}) custom-call(s32[1]{0:T(128)} %bitcast.refs_0_.core_ref, bf16[128,4096]{1,0:T(8,128)(2,1)} %refs_1_.2, f32[128,2048]{1,0:T(8,128)S(1)} %collective-permute-done.refs_2_, bf16[128,4096]{1,0:T(8,128)(2,1)} %refs_3_.2, ...), custom_call_target="tpu_custom_call" | custom-call | tf_op jit(solution)/shard_map/keys/pallas_call | solution.py:443
  11.6 11.4 %all-to-all-start = ((f32[64,1,4224]{2,1,0:T(1,128)}), f32[64,1,4224]{2,1,0:T(1,128)S(1)}, u32[]{:S(2)}, u32[]{:S(2)}) async-start(f32[64,1,4224]{2,1,0:T(1,128)} %bitcast.27), calls=%async_computation | async-start | bytes 2162688 | tf_op jit(solution)/shard_map/all_to_all | solution.py:481
  23.1 0.7 collective-permute-start.2
  23.8 16.5 %all-to-all-done = f32[64,1,4224]{2,1,0:T(1,128)S(1)} async-done(((f32[64,1,4224]{2,1,0:T(1,128)}), f32[64,1,4224]{2,1,0:T(1,128)S(1)}, u32[]{:S(2)}, u32[]{:S(2)}) %all-to-all-start) | async-done | bytes 1081376 | tf_op jit(solution)/shard_map/all_to_all | solution.py:481
  40.3 1.1 scan.2
  41.5 5.8 %all-to-all-start.1 = ((f32[64,1,4224]{2,1,0:T(1,128)}), f32[64,1,4224]{2,1,0:T(1,128)S(1)}, u32[]{:S(2)}, u32[]{:S(2)}) async-start(f32[64,1,4224]{2,1,0:T(1,128)} %bitcast.22), calls=%async_computation.1 | async-start | bytes 2162688 | tf_op jit(solution)/shard_map/all_to_all | solution.py:481
  47.4 1.8 %collective-permute-start.3 = (f32[128,2048]{1,0:T(8,128)S(1)}, f32[128,2048]{1,0:T(8,128)}, u32[]{:S(2)}, u32[]{:S(2)}) collective-permute-start(f32[128,2048]{1,0:T(8,128)S(1)} %dynamic-slice_convert_fusion), channel_id=1, source_target_pairs={{0,1},{1,0},{2,3},{3,2},{4,5},{5,4},{6,7},{7,6},{8,9},{9,8},{10,11... | collective-permute-start | bytes 3145736 | tf_op jit(solution)/shard_map/ppermute | solution.py:493
  49.1 6.4 %scores.1 = (bf16[16,256,128]{2,1,0:T(8,128)(2,1)}, f32[16,128,256]{2,1,0:T(8,128)}, bf16[16,256,128]{2,1,0:T(8,128)(2,1)}, f32[16,8,256]{2,1,0:T(8,128)}, f32[16,256,128]{2,1,0:T(8,128)S(1)}) custom-call(s32[1]{0:T(128)} %bitcast.refs_0_.core_ref, bf16[128,4096]{1,0:T(8,128)(2,1)} %refs_1_.3, f32[128,2048]{1,0:T(8,128)} %collective-permute-done.2.refs_2_, ...), custom_call_target="tpu_custom_call" | custom-call | tf_op jit(solution)/shard_map/scores/pallas_call | solution.py:443
  55.6 8.1 %all-to-all-done.1 = f32[64,1,4224]{2,1,0:T(1,128)S(1)} async-done(((f32[64,1,4224]{2,1,0:T(1,128)}), f32[64,1,4224]{2,1,0:T(1,128)S(1)}, u32[]{:S(2)}, u32[]{:S(2)}) %all-to-all-start.1) | async-done | bytes 1081376 | tf_op jit(solution)/shard_map/all_to_all | solution.py:481
  63.7 6.6 %outs.1 = (bf16[128,2048]{1,0:T(8,128)(2,1)}, f32[128,2048]{1,0:T(8,128)}, bf16[16,256,128]{2,1,0:T(8,128)(2,1)}, f32[16,8,256]{2,1,0:T(8,128)}, f32[8,264,128]{2,1,0:T(8,128)}, /*index=5*/f32[8,128]{1,0:T(8,128)S(1)}) custom-call(s32[1]{0:T(128)} %bitcast.refs_0_.core_ref, f32[8,264,128]{2,1,0:T(8,128)S(1)} %bitcast.13, ...), custom_call_target="tpu_custom_call" | custom-call | tf_op jit(solution)/shard_map/outs/pallas_call | solution.py:443
  70.4 6.1 %all-to-all-start.2 = ((f32[64,1,4224]{2,1,0:T(1,128)}), f32[64,1,4224]{2,1,0:T(1,128)S(1)}, u32[]{:S(2)}, u32[]{:S(2)}) async-start(f32[64,1,4224]{2,1,0:T(1,128)} %bitcast.26), calls=%async_computation.2 | async-start | bytes 2162688 | tf_op jit(solution)/shard_map/all_to_all | solution.py:481
  76.5 10.1 %grids.1 = (f32[16,64,128]{2,1,0:T(8,128)}, f32[16,128,256]{2,1,0:T(8,128)S(1)}) custom-call(s32[1]{0:T(128)} %bitcast.refs_0_.core_ref, bf16[16,256,128]{2,1,0:T(8,128)(2,1)} %get-tuple-element.41.refs_1_, bf16[16,256,128]{2,1,0:T(8,128)(2,1)} %get-tuple-element.35.refs_5_.refs_2_, f32[16,8,256]{2,1,0:T(8,128)} %get-tuple-element.42.refs_3_, ...), custom_call_target="tpu_custom_call" | custom-call | tf_op jit(solution)/shard_map/grids/pallas_call | solution.py:443
  86.6 6.5 %all-to-all-done.2 = f32[64,1,4224]{2,1,0:T(1,128)S(1)} async-done(((f32[64,1,4224]{2,1,0:T(1,128)}), f32[64,1,4224]{2,1,0:T(1,128)S(1)}, u32[]{:S(2)}, u32[]{:S(2)}) %all-to-all-start.2) | async-done | bytes 1081376 | tf_op jit(solution)/shard_map/all_to_all | solution.py:481
  93.1 1.1 scan.3
  94.2 4.7 %all-to-all-start.3 = ((f32[64,1,4224]{2,1,0:T(1,128)}), f32[64,1,4224]{2,1,0:T(1,128)S(1)}, u32[]{:S(2)}, u32[]{:S(2)}) async-start(f32[64,1,4224]{2,1,0:T(1,128)} %bitcast.23), calls=%async_computation.3 | async-start | bytes 2162688 | tf_op jit(solution)/shard_map/all_to_all | solution.py:481
  98.9 3.4 %collective-permute-start.4 = (f32[128,2048]{1,0:T(8,128)}, f32[128,2048]{1,0:T(8,128)S(1)}, u32[]{:S(2)}, u32[]{:S(2)}) collective-permute-start(f32[128,2048]{1,0:T(8,128)} %get-tuple-element.48), channel_id=1, source_target_pairs={{0,1},{1,0},{2,3},{3,2},{4,5},{5,4},{6,7},{7,6},{8,9},{9,8},{10,11... | collective-permute-start | bytes 3145736 | tf_op jit(solution)/shard_map/ppermute | solution.py:493
  102.3 2.4 %collective-permute-done.4.refs_2_ = f32[128,2048]{1,0:T(8,128)S(1)} collective-permute-done((f32[128,2048]{1,0:T(8,128)}, f32[128,2048]{1,0:T(8,128)S(1)}, u32[]{:S(2)}, u32[]{:S(2)}) %collective-permute-start.4) | collective-permute-done | bytes 1048608 | tf_op jit(solution)/shard_map/ppermute | solution.py:493
  104.7 1.0 copy-done.1
  105.7 9.1 %all-to-all-done.3 = f32[64,1,4224]{2,1,0:T(1,128)S(1)} async-done(((f32[64,1,4224]{2,1,0:T(1,128)}), f32[64,1,4224]{2,1,0:T(1,128)S(1)}, u32[]{:S(2)}, u32[]{:S(2)}) %all-to-all-start.3) | async-done | bytes 1081376 | tf_op jit(solution)/shard_map/all_to_all | solution.py:481
  114.8 4.9 %last.1 = f32[8,264,128]{2,1,0:T(8,128)} custom-call(s32[1]{0:T(128)} %bitcast.refs_0_.core_ref, f32[8,264,128]{2,1,0:T(8,128)S(1)} %bitcast.21, bf16[16,256,128]{2,1,0:T(8,128)(2,1)} %get-tuple-element.35.refs_5_.refs_2_, f32[16,128,256]{2,1,0:T(8,128)} %get-tuple-element.34.refs_4_.refs_5_.refs_3_, bf16[16,256,128]{2,1,0:T(8,128)(2,1)} %get-tuple-element.50.refs_4_, ...), custom_call_target="tpu_custom_call" | custom-call | tf_op jit(solution)/shard_map/last/pallas_call | solution.py:443
  119.8 5.2 %all-to-all-start.4 = ((f32[64,1,4224]{2,1,0:T(1,128)}), f32[64,1,4224]{2,1,0:T(1,128)S(1)}, u32[]{:S(2)}, u32[]{:S(2)}) async-start(f32[64,1,4224]{2,1,0:T(1,128)} %bitcast.25), calls=%async_computation.4 | async-start | bytes 2162688 | tf_op jit(solution)/shard_map/all_to_all | solution.py:481
  124.9 2.2 %merge.1 = bf16[128,4096]{1,0:T(8,128)(2,1)} custom-call(s32[1]{0:T(128)} %bitcast.refs_0_.core_ref, bf16[128,2048]{1,0:T(8,128)(2,1)} %get-tuple-element.54.refs_1_, f32[128,2048]{1,0:T(8,128)S(1)} %copy-done.2), custom_call_target="tpu_custom_call" | custom-call | tf_op jit(solution)/shard_map/merge/pallas_call | solution.py:443
  127.1 13.2 %all-to-all-done.4 = f32[64,1,4224]{2,1,0:T(1,128)S(1)} async-done(((f32[64,1,4224]{2,1,0:T(1,128)}), f32[64,1,4224]{2,1,0:T(1,128)S(1)}, u32[]{:S(2)}, u32[]{:S(2)}) %all-to-all-start.4) | async-done | bytes 1081376 | tf_op jit(solution)/shard_map/all_to_all | solution.py:481
  140.4 1.2 sum.1
  141.5 19.2 %all_to_all.30 = f32[64,1,4224]{2,1,0:T(1,128)S(1)} all-to-all(f32[64,1,4224]{2,1,0:T(1,128)} %bitcast.24), channel_id=1, replica_groups=mesh['x'=4,'z'=4,'y'=4,'c'=2] {'x','z','y'}, dimensions={0} | all-to-all | bytes 2162688 | tf_op jit(solution)/shard_map/all_to_all | solution.py:481
  160.7 5.6 %collective-permute-start.6 = (f32[8,264,128]{2,1,0:T(8,128)S(1)}, f32[8,264,128]{2,1,0:T(8,128)S(1)}, u32[]{:S(2)}, u32[]{:S(2)}) collective-permute-start(f32[8,264,128]{2,1,0:T(8,128)S(1)} %bitcast.18), channel_id=1, source_target_pairs={{0,1},{1,0},{2,3},{3,2},{4,5},{5,4},{6,7},{7,6},{8,9},{9,8},{10,11... | collective-permute-start | bytes 3244040 | tf_op jit(solution)/shard_map/ppermute | solution.py:493
  166.3 1.0 unpack_mine.1
  168.6 1.1 unpack.1
  (21 shorter events, 1.2 us)
Async XLA Ops:
  0.6 2.7 %copy-start.3 = (bf16[128,4096]{1,0:T(8,128)(2,1)S(1)}, bf16[128,4096]{1,0:T(8,128)(2,1)}, u32[]{:S(2)}) copy-start(bf16[128,4096]{1,0:T(8,128)(2,1)} %refs_1_.2) | copy-start | bytes 3145732
  1.9 3.7 %collective-permute-start.1 = (f32[128,2048]{1,0:T(8,128)S(1)}, f32[128,2048]{1,0:T(8,128)S(1)}, u32[]{:S(2)}, u32[]{:S(2)}) collective-permute-start(f32[128,2048]{1,0:T(8,128)S(1)} %dynamic-slice_convert_fusion.2), channel_id=1, source_target_pairs={{0,1},{1,0},{2,3},{3,2},{4,5},{5,4},{6,7},{7,6},{8,9},{9,8},{10,11... | collective-permute-start | bytes 3145736 | tf_op jit(solution)/shard_map/ppermute | solution.py:493
  3.5 3.7 %collective-permute-start = (f32[128,2048]{1,0:T(8,128)S(1)}, f32[128,2048]{1,0:T(8,128)S(1)}, u32[]{:S(2)}, u32[]{:S(2)}) collective-permute-start(f32[128,2048]{1,0:T(8,128)S(1)} %dynamic-slice_convert_fusion.3), channel_id=1, source_target_pairs={{0,1},{1,0},{2,3},{3,2},{4,5},{5,4},{6,7},{7,6},{8,9},{9,8},{10,11... | collective-permute-start | bytes 3145736 | tf_op jit(solution)/shard_map/ppermute | solution.py:493
  11.6 11.4 %copy-start.5 = (bf16[128,4096]{1,0:T(8,128)(2,1)S(1)}, bf16[128,4096]{1,0:T(8,128)(2,1)}, u32[]{:S(2)}) copy-start(bf16[128,4096]{1,0:T(8,128)(2,1)} %refs_1_.3) | copy-start | bytes 3145732
  11.6 28.7 %all-to-all-start = ((f32[64,1,4224]{2,1,0:T(1,128)}), f32[64,1,4224]{2,1,0:T(1,128)S(1)}, u32[]{:S(2)}, u32[]{:S(2)}) async-start(f32[64,1,4224]{2,1,0:T(1,128)} %bitcast.27), calls=%async_computation | async-start | bytes 2162688 | tf_op jit(solution)/shard_map/all_to_all | solution.py:481
  23.1 26.0 %collective-permute-start.2 = (f32[128,2048]{1,0:T(8,128)S(1)}, f32[128,2048]{1,0:T(8,128)}, u32[]{:S(2)}, u32[]{:S(2)}) collective-permute-start(f32[128,2048]{1,0:T(8,128)S(1)} %dynamic-slice_convert_fusion.1), channel_id=1, source_target_pairs={{0,1},{1,0},{2,3},{3,2},{4,5},{5,4},{6,7},{7,6},{8,9},{9,8},{10,11... | collective-permute-start | bytes 3145736 | tf_op jit(solution)/shard_map/ppermute | solution.py:493
  41.4 5.8 %copy-start.4 = (bf16[128,4096]{1,0:T(8,128)(2,1)S(1)}, bf16[128,4096]{1,0:T(8,128)(2,1)}, u32[]{:S(2)}) copy-start(bf16[128,4096]{1,0:T(8,128)(2,1)} %refs_6_.1) | copy-start | bytes 3145732
  41.5 22.3 %all-to-all-start.1 = ((f32[64,1,4224]{2,1,0:T(1,128)}), f32[64,1,4224]{2,1,0:T(1,128)S(1)}, u32[]{:S(2)}, u32[]{:S(2)}) async-start(f32[64,1,4224]{2,1,0:T(1,128)} %bitcast.22), calls=%async_computation.1 | async-start | bytes 2162688 | tf_op jit(solution)/shard_map/all_to_all | solution.py:481
  47.4 8.2 %collective-permute-start.3 = (f32[128,2048]{1,0:T(8,128)S(1)}, f32[128,2048]{1,0:T(8,128)}, u32[]{:S(2)}, u32[]{:S(2)}) collective-permute-start(f32[128,2048]{1,0:T(8,128)S(1)} %dynamic-slice_convert_fusion), channel_id=1, source_target_pairs={{0,1},{1,0},{2,3},{3,2},{4,5},{5,4},{6,7},{7,6},{8,9},{9,8},{10,11... | collective-permute-start | bytes 3145736 | tf_op jit(solution)/shard_map/ppermute | solution.py:493
  63.7 6.6 %copy-start = (f32[64,1,4224]{2,1,0:T(1,128)}, f32[64,1,4224]{2,1,0:T(1,128)S(1)}, u32[]{:S(2)}) copy-start(f32[64,1,4224]{2,1,0:T(1,128)S(1)} %all-to-all-done.1) | copy-start | bytes 3244036
  70.4 22.7 %all-to-all-start.2 = ((f32[64,1,4224]{2,1,0:T(1,128)}), f32[64,1,4224]{2,1,0:T(1,128)S(1)}, u32[]{:S(2)}, u32[]{:S(2)}) async-start(f32[64,1,4224]{2,1,0:T(1,128)} %bitcast.26), calls=%async_computation.2 | async-start | bytes 2162688 | tf_op jit(solution)/shard_map/all_to_all | solution.py:481
  94.2 20.6 %all-to-all-start.3 = ((f32[64,1,4224]{2,1,0:T(1,128)}), f32[64,1,4224]{2,1,0:T(1,128)S(1)}, u32[]{:S(2)}, u32[]{:S(2)}) async-start(f32[64,1,4224]{2,1,0:T(1,128)} %bitcast.23), calls=%async_computation.3 | async-start | bytes 2162688 | tf_op jit(solution)/shard_map/all_to_all | solution.py:481
  98.9 5.9 %collective-permute-start.4 = (f32[128,2048]{1,0:T(8,128)}, f32[128,2048]{1,0:T(8,128)S(1)}, u32[]{:S(2)}, u32[]{:S(2)}) collective-permute-start(f32[128,2048]{1,0:T(8,128)} %get-tuple-element.48), channel_id=1, source_target_pairs={{0,1},{1,0},{2,3},{3,2},{4,5},{5,4},{6,7},{7,6},{8,9},{9,8},{10,11... | collective-permute-start | bytes 3145736 | tf_op jit(solution)/shard_map/ppermute | solution.py:493
  102.2 12.6 %collective-permute-start.5 = (f32[8,128]{1,0:T(8,128)S(1)}, f32[8,128]{1,0:T(8,128)S(1)}, u32[]{:S(2)}, u32[]{:S(2)}) collective-permute-start(f32[8,128]{1,0:T(8,128)S(1)} %get-tuple-element.53.refs_7_), channel_id=1, source_target_pairs={{0,1},{1,0},{2,3},{3,2},{4,5},{5,4},{6,7},{7,6},{8,9},{9,8},{10,11... | collective-permute-start | bytes 12296 | tf_op jit(solution)/shard_map/ppermute | solution.py:493
  104.7 1.0 copy-start.1
  119.8 5.2 %copy-start.2 = (f32[128,2048]{1,0:T(8,128)S(1)}, f32[128,2048]{1,0:T(8,128)}, u32[]{:S(2)}) copy-start(f32[128,2048]{1,0:T(8,128)} %copy-done.1) | copy-start | bytes 3145732
  119.8 20.6 %all-to-all-start.4 = ((f32[64,1,4224]{2,1,0:T(1,128)}), f32[64,1,4224]{2,1,0:T(1,128)S(1)}, u32[]{:S(2)}, u32[]{:S(2)}) async-start(f32[64,1,4224]{2,1,0:T(1,128)} %bitcast.25), calls=%async_computation.4 | async-start | bytes 2162688 | tf_op jit(solution)/shard_map/all_to_all | solution.py:481
  160.7 7.9 %collective-permute-start.6 = (f32[8,264,128]{2,1,0:T(8,128)S(1)}, f32[8,264,128]{2,1,0:T(8,128)S(1)}, u32[]{:S(2)}, u32[]{:S(2)}) collective-permute-start(f32[8,264,128]{2,1,0:T(8,128)S(1)} %bitcast.18), channel_id=1, source_target_pairs={{0,1},{1,0},{2,3},{3,2},{4,5},{5,4},{6,7},{7,6},{8,9},{9,8},{10,11... | collective-permute-start | bytes 3244040 | tf_op jit(solution)/shard_map/ppermute | solution.py:493

commit v5 on v4

--- a/solution.py
+++ b/solution.py
@@ -19,7 +19,7 @@
 WIDTH = 128
 PIECE = 33
 PAIRS = HALF // 2
-GROUPS = ((4, 12), (12, 4))
+GROUPS = ((8, 8), (12, 4))
 PROWS = 2 * 4 * PIECE
 
 NN = ((1,), (0,))
@@ -43,11 +43,15 @@
     return jnp.concatenate([one, two], axis=0)
 
 
-def soft_back(phi, dphi, x):
-    prod = phi * dphi
-    one = prod[:64] - phi[:64] * jnp.sum(prod[:64], axis=0, keepdims=True)
-    two = prod[64:] - phi[64:] * jnp.sum(prod[64:], axis=0, keepdims=True)
-    return dot((one - two).astype(BF16), x)
+def soft_back(phi, dphi, x, rounded=False):
+    halves = []
+    for part in (slice(0, 64), slice(64, 128)):
+        prod = phi[part] * dphi[part]
+        mean = jnp.sum(prod, axis=0, keepdims=True)
+        if rounded:
+            mean = mean * (1.0 / jnp.sum(phi[part], axis=0, keepdims=True))
+        halves.append(prod - phi[part] * mean)
+    return dot((halves[0] - halves[1]).astype(BF16), x)
 
 
 def columns(h):
@@ -68,6 +72,19 @@
         ref[pair, at + 32 : at + 33, :] = row
 
 
+def put_grad(ref, h, grad, row):
+    for q in range(2):
+        at = (2 * (h % 4) + q) * PIECE
+        ref[h // 4, at : at + 32, :] = grad[32 * q : 32 * q + 32]
+        ref[h // 4, at + 32 : at + 33, :] = row
+
+
+def get_grad(ref, h, side):
+    at = 2 * (h % 4) * PIECE
+    parts = [ref[h // 4, side, at + q * PIECE : at + q * PIECE + 32, :] for q in range(2)]
+    return jnp.concatenate(parts, axis=0)
+
+
 def get_state(ref, h):
     first = 4 * (h % 2)
     parts = [ref[h // 2, (first + q) * PIECE : (first + q) * PIECE + 32, :] for q in range(4)]
@@ -79,10 +96,6 @@
     return jnp.broadcast_to(row, (lanes, row.shape[1])).T
 
 
-def as_row(column):
-    return jnp.broadcast_to(column, (column.shape[0], WIDTH)).T[:1]
-
-
 def twice(x):
     return jnp.concatenate([x, x], axis=1)
 
@@ -94,28 +107,36 @@
     return at_query >= at_key
 
 
-def key_kernel(core, k_own, k_other, v_own, v_other, w_ref, kf, vf, phik_ref, send):
-
-    def head(h):
-        k = both_cores(k_own, k_other, h)
-        kf[h] = k
-        logits = dot(w_ref[h], k, NT)
+def key_kernel(core, k_own, k_other, v_own, v_other, w_ref, phik_ref, send):
+    ones = jnp.ones((8, 2 * TOK), BF16)
+
+    def head(h):
+        logits = dot(w_ref[h], both_cores(k_own, k_other, h), NT)
         yield
         phik = soft_maps(logits)
-        phik_ref[h] = phik
-        phikb = phik.astype(BF16)
-        v = both_cores(v_own, v_other, h)
-        vf[h] = v
-        yield
-        state = dot(phikb, v)
-        yield
-        put_state(send, h, state, as_row(jnp.sum(phik, axis=1, keepdims=True)))
+        phikb, low = two_parts(phik)
+        phik_ref[h] = phikb
+        yield
+        state = dot(phikb, both_cores(v_own, v_other, h))
+        row = dot(ones, jnp.concatenate([phikb, low], axis=1), NT)[:1]
+        yield
+        put_state(send, h, state, row)
+
+    return head
+
+
+def pack_kernel(core, k_own, k_other, v_own, v_other, kf, vf):
+    def head(h):
+        kf[h] = both_cores(k_own, k_other, h)
+        vf[h] = both_cores(v_own, v_other, h)
+        yield
 
     return head
 
 
 def score_kernel(
-    core, q_own, q_other, w_ref, phik_ref, vf, qf, phiq_ref, phiqb_ref, den_ref, num_ref
+    core, q_own, q_other, w_ref, phik_ref, vf, t_own, t_other,
+    qf, phiq_ref, phiqb_ref, tf, den_ref, num_ref,
 ):
     mask = causal(core)
     ones = jnp.ones((8, 2 * TOK), BF16)
@@ -129,8 +150,9 @@
         phiq_ref[h] = phiq
         phiqb = phiq.astype(BF16).T
         phiqb_ref[h] = phiqb
-        yield
-        scores = dot(phiqb, phik_ref[h].astype(BF16))
+        tf[h] = both_cores(t_own, t_other, h)
+        yield
+        scores = dot(phiqb, phik_ref[h])
         yield
         high, low = two_parts(jnp.where(mask, scores, 0.0))
         num_ref[h] = dot(high, vf[h])
@@ -140,10 +162,11 @@
 
 
 def out_kernel(
-    core, pre, num_ref, phiq_ref, phiqb_ref, den_ref, t_own, t_other,
+    core, pre, num_ref, phiq_ref, phiqb_ref, den_ref, tf,
     y_own, y_send, dnum_ref, dden_ref, send, loss_ref,
 ):
     ones = jnp.ones((8, 2 * WIDTH), BF16)
+    wide = jnp.ones((8, 2 * TOK), BF16)
     scale = 2.0 / (HEADS * WIDTH)
     loss_ref[...] = jnp.zeros_like(loss_ref)
 
@@ -159,7 +182,7 @@
         y = (num_ref[h] + carried) * inv
         y_own[:, columns(h)] = y[:ROWS].astype(BF16)
         y_send[:, columns(h)] = y[ROWS:]
-        err = y - both_cores(t_own, t_other, h).astype(F32)
+        err = y - tf[h].astype(F32)
         loss_ref[...] += jnp.sum((err * err).reshape(TOK // 8, 8, WIDTH), axis=0)
         dnum = (scale * err) * inv
         dnumb = dnum.astype(BF16)
@@ -171,55 +194,9 @@
         rev = dot(phiq_ref[h].astype(BF16), dnumb)
         yield
         dden_ref[h] = dden
-        rnorm = as_row(jnp.sum(phiq_ref[h] * dden[:1], axis=1, keepdims=True))
-        yield
-        put_state(send, h, rev, rnorm)
-
-    return head
-
-
-def out_kernel(
-    core, pre, num_ref, phiqt_ref, phiqb_ref, den_ref, t_own, t_other,
-    y_own, y_send, dnum_ref, dden_ref, send, loss_ref,
-):
-    ones = jnp.ones((8, 2 * WIDTH), BF16)
-    none = jnp.zeros((WIDTH, WIDTH), BF16)
-    scale = 2.0 / (HEADS * WIDTH)
-    loss_ref[...] = jnp.zeros_like(loss_ref)
-
-    def head(h):
-        state, norm = get_state(pre, h)
-        high, low = two_parts(as_column(norm, WIDTH))
-        den = as_column(den_ref[h][:1], WIDTH)
-        right = jnp.concatenate(
-            [
-                jnp.concatenate([state.astype(BF16), high], axis=1),
-                jnp.concatenate([none, low], axis=1),
-            ],
-            axis=0,
-        )
-        yield
-        both = dot(twice(phiqb_ref[h]), right)
-        yield
-        inv = 1.0 / (den + both[:, WIDTH:])
-        y = (num_ref[h] + both[:, :WIDTH]) * inv
-        y_own[:, columns(h)] = y[:ROWS].astype(BF16)
-        y_send[:, columns(h)] = y[ROWS:]
-        err = y - both_cores(t_own, t_other, h).astype(F32)
-        loss_ref[...] += jnp.sum((err * err).reshape(TOK // 8, 8, WIDTH), axis=0)
-        dnum = (scale * err) * inv
-        dnumb = dnum.astype(BF16)
-        dnum_ref[h] = dnumb
-        high, low = two_parts(dnum * y)
-        both = jnp.concatenate([high, low], axis=1)
-        yield
-        dden = -dot(ones, both, NT)
-        rev = dot(phiqt_ref[h], dnumb)
-        yield
-        dden_ref[h] = dden
-        high, low = two_parts(dden)
-        phiqt = phiqt_ref[h]
-        rnorm = dot(jnp.concatenate([high, low], axis=1), twice(phiqt), NT)
+        high, low = two_parts(phiq_ref[h] * dden[:1])
+        yield
+        rnorm = dot(wide, jnp.concatenate([high, low], axis=1), NT)
         yield
         put_state(send, h, rev, rnorm[:1])
 
@@ -227,7 +204,7 @@
 
 
 def grid_kernel(
-    core, dnum_ref, vf, dden_ref, phiq_ref, phik_ref, pre, qf, grad_ref, dphik_ref,
+    core, dnum_ref, vf, dden_ref, phiq_ref, phik_ref, pre, qf, send, dphik_ref,
 ):
     mask = causal(core)
 
@@ -238,11 +215,12 @@
         gridb = jnp.where(mask, grid + twice(column), 0.0).astype(BF16)
         dphik_ref[h] = dot(phiq_ref[h].astype(BF16), gridb)
         state, norm = get_state(pre, h)
-        left = jnp.concatenate([phik_ref[h].astype(BF16), state.astype(BF16)], axis=1)
+        left = jnp.concatenate([phik_ref[h], state.astype(BF16)], axis=1)
         dphiq = dot(left, jnp.concatenate([gridb, dnum_ref[h]], axis=1), NT)
         down = twice(as_column(norm, WIDTH))
         yield
-        grad_ref[h] = soft_back(phiq_ref[h], dphiq + down * dden_ref[h][:1], qf[h])
+        grad = soft_back(phiq_ref[h], dphiq + down * dden_ref[h][:1], qf[h])
+        put_grad(send, h, grad, jnp.zeros((1, WIDTH), F32))
 
     return head
 
@@ -259,17 +237,20 @@
 
 
 def last_kernel(
-    core, suf, vf, phik_ref, kf, dphik_ref, grad_ref, loss_ref, loss_other, send
+    core, suf, vf, phik_ref, kf, dphik_ref, loss_ref, loss_other, queries_sent, send
 ):
+    del queries_sent
     row = jnp.sum(loss_ref[...] + loss_other[...], axis=0, keepdims=True)
 
     def head(h):
         state, norm = get_state(suf, h)
         carried = dot(state.astype(BF16), vf[h], NT) + twice(as_column(norm, WIDTH))
         yield
-        grad_key = soft_back(phik_ref[h], dphik_ref[h] + carried, kf[h])
-        yield
-        put_state(send, h, jnp.concatenate([grad_ref[h], grad_key], axis=0), row)
+        grad_key = soft_back(
+            phik_ref[h].astype(F32), dphik_ref[h] + carried, kf[h], rounded=True
+        )
+        yield
+        put_grad(send, h, grad_key, row)
 
     return head
 
@@ -313,9 +294,8 @@
     src, gq, gk = refs[0], refs[-2], refs[-1]
 
     def head(h):
-        state, _ = get_state(src, h)
-        gq[h] = state[:64]
-        gk[h] = state[64:]
+        gq[h] = get_grad(src, h, 0)
+        gk[h] = get_grad(src, h, 1)
         yield
 
     return head
@@ -432,6 +412,16 @@
     for g in range(len(spans_out)):
         for copy in copies_out(g):
             copy.wait()
+
+
+def quads_block(side):
+    def view(ref, start, count):
+        return ref.at[pl.ds(start // 4, count // 4)]
+
+    def cut(ref, core, start, count):
+        return ref.at[pl.ds(start // 4, count // 4), side]
+
+    return Block((HALF // 4, PROWS, WIDTH), view, cut)
 
 
 def raw_call(body, name, core, values, specs, shapes, scratch, aliases=()):
@@ -477,6 +467,9 @@
 PAYLOAD = sds((PAIRS, PROWS, WIDTH))
 
 
+GRADS = sds((HALF // 4, 2, PROWS, WIDTH))
+
+
 def exchange(x):
     pieces = lax.all_to_all(x.reshape(NCHIP, 1, PIECE * WIDTH), CHIPS, 0, 0, tiled=True)
     return pieces.reshape(PAIRS, PROWS, WIDTH)
@@ -515,49 +508,51 @@
     natural = (sds((HALF, TOK, WIDTH), BF16), heads_block(TOK, WIDTH))
     features = (sds((HALF, WIDTH, TOK)), heads_block(WIDTH, TOK))
     row = (sds((HALF, 8, TOK)), heads_block(8, TOK))
-    grads = (sds((HALF, 64, WIDTH)), heads_block(64, WIDTH))
     weight = core_heads(64, WIDTH)
     payload = (PAYLOAD, pieces_block())
     lossy = (pltpu.VMEM((8, WIDTH), F32), None)
 
-    kf, vf, phik, send = run(
-        key_kernel, "keys",
-        [(keys, own), (k_other, None), (values, own), (v_other, None), (key_map, weight)],
-        [natural, natural, features, payload],
-    )
+    halved = (sds((HALF, WIDTH, TOK), BF16), heads_block(WIDTH, TOK))
+    swapped = [(keys, own), (k_other, None), (values, own), (v_other, None)]
+    phik, send = run(key_kernel, "keys", swapped + [(key_map, weight)], [halved, payload])
     gathered = exchange(send)
-    qf, phiq, phiqb, den, num = run(
+    kf, vf = run(pack_kernel, "pack", swapped, [natural, natural])
+    gathered, kf, vf, q_other, t_other = lax.optimization_barrier(
+        (gathered, kf, vf, q_other, t_other)
+    )
+    qf, phiq, phiqb, tf, den, num = run(
         score_kernel, "scores",
-        [(queries, own), (q_other, cols), (query_map, weight), (phik, features[1]),
-         (vf, natural[1])],
-        [natural, features, natural, row, (pltpu.VMEM((HALF, TOK, WIDTH), F32), None)],
+        [(queries, own), (q_other, cols), (query_map, weight), (phik, halved[1]),
+         (vf, natural[1]), (teacher, own), (t_other, cols)],
+        [natural, features, natural, natural, row, (pltpu.VMEM((HALF, TOK, WIDTH), F32), None)],
     )
     pre = exchange(scan(core, gathered, False))
     y_own, y_send, dnum, dden, send, loss = run(
         out_kernel, "outs",
         [(pre, None), (num, None), (phiq, features[1]), (phiqb, natural[1]), (den, row[1]),
-         (teacher, own), (t_other, cols)],
+         (tf, natural[1])],
         [(sds((ROWS, half), BF16), cols), (sds((ROWS, half)), cols), natural, row, payload,
          lossy],
+        groups=((6, 10), (12, 4)),
     )
     loss_other = swap(loss)
     gathered = exchange(send)
-    grad_query, dphik = run(
+    query_sent, dphik = run(
         grid_kernel, "grids",
         [(dnum, natural[1]), (vf, natural[1]), (dden, row[1]), (phiq, features[1]),
-         (phik, features[1]), (pre, payload[1]), (qf, natural[1])],
-        [grads, (pltpu.VMEM((HALF, WIDTH, TOK), F32), None)],
-    )
-    gathered, dphik, grad_query, y_send = lax.optimization_barrier(
-        (gathered, dphik, grad_query, y_send)
+         (phik, halved[1]), (pre, payload[1]), (qf, natural[1])],
+        [(GRADS, quads_block(0)), (pltpu.VMEM((HALF, WIDTH, TOK), F32), None)],
+    )
+    gathered, dphik, query_sent, y_send = lax.optimization_barrier(
+        (gathered, dphik, query_sent, y_send)
     )
     y_other = swap(y_send)
     suf, y_other = lax.optimization_barrier((exchange(scan(core, gathered, True)), y_other))
-    send, = run(
-        last_kernel, "last",
-        [(suf, None), (vf, natural[1]), (phik, features[1]), (kf, natural[1]),
-         (dphik, None), (grad_query, grads[1]), (loss, None), (loss_other, None)],
-        [payload],
+    send, = call(
+        last_kernel, "last", core,
+        [(suf, None), (vf, natural[1]), (phik, halved[1]), (kf, natural[1]), (dphik, None),
+         (loss, None), (loss_other, None), (query_sent, pltpu.HBM)],
+        [GRADS], [(0, quads_block(1))], aliases=[(8, 0)],
     )
     attn, = call(
         merge_kernel, "merge", core, [(y_own, cols), (y_other, None)],
@@ -569,9 +564,9 @@
         sum_kernel, "sum", core, [gathered], [None], [PAYLOAD],
         [pltpu.VMEM((PROWS, WIDTH), F32), pltpu.SemaphoreType.DMA((PAIRS,))],
     )
-    total = exchange(spread)
+    total = exchange(spread).reshape(GRADS.shape)
     theirs = swap(total)
-    loss = jnp.sum(total[0, 32]) * (1.0 / (HEADS * WIDTH) / (NCHIP * TOK))
+    loss = jnp.sum(total[0, 1, 32]) * (1.0 / (HEADS * WIDTH) / (NCHIP * TOK))
     grad = sds((HEADS, 64, WIDTH))
     mine, other = core_heads(64, WIDTH), core_heads(64, WIDTH, other=True)
     grad_query, grad_key = call(

time: 172 us -> 170 us (0.988)
  waiting for transfers between devices: 59.5 us -> 55.7 us
  other arithmetic: 2.13 us -> 4.12 us
    ppermute x7, waiting for transfers between devices: 6.01 us -> 4.01 us  [swap(): return lax.ppermute(x, 'c', [(0, 1), (1, 0)])]
    convert_element_type x4, other arithmetic: 1.53 us -> 3.52 us  [others(): return swap(part.astype(F32))]
    all_to_all x5, waiting for transfers between devices: 53.4 us -> 51.7 us  [exchange(): lax.all_to_all(x.reshape(NCHIP, 1, PIECE * WIDTH), CHIPS, 0, 0, tiled=True)]
    pallas_call x11 -> x12, Pallas kernels: 40.2 us -> 41.6 us  [raw_call(): pl.pallas_call(body, in_specs=[pl.BlockSpec(memory_space=pltpu.SMEM)] + [...]
  transfers between devices with their start and end apart: 12 -> 12, of which waited for: 8 -> 8; matrix products, arithmetic and copies ran while one was open for 1% -> 2% of each run, Pallas kernels for 12% -> 16%
where the time goes in v5:
time: 170 us; the launch traced here: 169 us
  waiting for transfers between devices  55.7 us (33%)
  starting transfers between devices  45 us (26%)
  Pallas kernels  41.6 us (24%)
  blocking collectives  19.2 us (11%)
  other arithmetic  4.12 us (2%)
  between operations  2.64 us (2%)
    all_to_all x5, waiting for transfers between devices, exchange(): lax.all_to_all(x.reshape(NCHIP, 1, PIECE * WIDTH), CHIPS, 0, 0, tiled=True)  51.7 us
    pallas_call x12, Pallas kernels, raw_call(): pl.pallas_call(body, in_specs=[pl.BlockSpec(memory_space=pltpu.SMEM)] + [...  41.6 us
    all_to_all x5, starting transfers between devices, exchange(): lax.all_to_all(x.reshape(NCHIP, 1, PIECE * WIDTH), CHIPS, 0, 0, tiled=True)  32.7 us
    all_to_all x1, blocking collectives, exchange(): lax.all_to_all(x.reshape(NCHIP, 1, PIECE * WIDTH), CHIPS, 0, 0, tiled=True)  19.2 us
    ppermute x7, starting transfers between devices, swap(): return lax.ppermute(x, 'c', [(0, 1), (1, 0)])  12.3 us
    ppermute x7, waiting for transfers between devices, swap(): return lax.ppermute(x, 'c', [(0, 1), (1, 0)])  4.01 us
    convert_element_type x4, other arithmetic, others(): return swap(part.astype(F32))  3.52 us
  transfers between devices with their start and end apart: 12, of which 8 were waited for; matrix products, arithmetic and copies ran while one was open for 2% of the time, Pallas kernels for 16%

profile of v5, /device:TPU:1, one launch (start us, length us, event | category | flops | bytes accessed | tf_op | source)
XLA Modules:
  0.0 169.2 jit_solution(10249033986401101849)
XLA Ops:
  0.6 1.2 dynamic-slice_convert_fusion.2
  1.9 1.5 collective-permute-start.1
  3.6 1.1 dynamic-slice_convert_fusion
  5.6 1.5 collective-permute-done.refs_2_
  7.1 4.1 %keys.1 = (bf16[16,128,256]{2,1,0:T(8,128)(2,1)}, f32[8,264,128]{2,1,0:T(8,128)}) custom-call(s32[1]{0:T(128)} %bitcast.refs_0_.core_ref, bf16[128,4096]{1,0:T(8,128)(2,1)} %refs_1_.4, f32[128,2048]{1,0:T(8,128)S(1)} %collective-permute-done.refs_2_, bf16[128,4096]{1,0:T(8,128)(2,1)} %refs_3_.4, f32[128,2048]{1,0:T(8,128)S(1)} %collective-permute-done.1.refs_4_, ...), custom_call_target="tpu_custom_call" | custom-call | tf_op jit(solution)/shard_map/keys/pallas_call | solution.py:433
  11.2 11.3 %all-to-all-start = ((f32[64,1,4224]{2,1,0:T(1,128)}), f32[64,1,4224]{2,1,0:T(1,128)S(1)}, u32[]{:S(2)}, u32[]{:S(2)}) async-start(f32[64,1,4224]{2,1,0:T(1,128)} %bitcast.26), calls=%async_computation | async-start | bytes 2162688 | tf_op jit(solution)/shard_map/all_to_all | solution.py:474
  22.5 1.1 dynamic-slice_convert_fusion.1
  24.4 2.6 %pack.1 = (bf16[16,256,128]{2,1,0:T(8,128)(2,1)}, bf16[16,256,128]{2,1,0:T(8,128)(2,1)}) custom-call(s32[1]{0:T(128)} %bitcast.refs_0_.core_ref, bf16[128,4096]{1,0:T(8,128)(2,1)} %refs_1_.4, f32[128,2048]{1,0:T(8,128)S(1)} %collective-permute-done.refs_2_, bf16[128,4096]{1,0:T(8,128)(2,1)} %refs_3_.4, f32[128,2048]{1,0:T(8,128)S(1)} %collective-permute-done.1.refs_4_), custom_call_target="tpu_custom_call" | custom-call | tf_op jit(solution)/shard_map/pack/pallas_call | solution.py:433
  27.0 12.8 %all-to-all-done = f32[64,1,4224]{2,1,0:T(1,128)S(1)} async-done(((f32[64,1,4224]{2,1,0:T(1,128)}), f32[64,1,4224]{2,1,0:T(1,128)S(1)}, u32[]{:S(2)}, u32[]{:S(2)}) %all-to-all-start) | async-done | bytes 1081376 | tf_op jit(solution)/shard_map/all_to_all | solution.py:474
  39.8 1.1 scan.2
  40.9 5.7 %all-to-all-start.1 = ((f32[64,1,4224]{2,1,0:T(1,128)}), f32[64,1,4224]{2,1,0:T(1,128)S(1)}, u32[]{:S(2)}, u32[]{:S(2)}) async-start(f32[64,1,4224]{2,1,0:T(1,128)} %bitcast.24), calls=%async_computation.1 | async-start | bytes 2162688 | tf_op jit(solution)/shard_map/all_to_all | solution.py:474
  46.6 6.8 %scores.1 = (bf16[16,256,128]{2,1,0:T(8,128)(2,1)}, f32[16,128,256]{2,1,0:T(8,128)}, bf16[16,256,128]{2,1,0:T(8,128)(2,1)}, bf16[16,256,128]{2,1,0:T(8,128)(2,1)...) custom-call(s32[1]{0:T(128)} %bitcast.refs_0_.core_ref, bf16[128,4096]{1,0:T(8,128)(2,1)} %refs_1_.5, ...), custom_call_target="tpu_custom_call" | custom-call | tf_op jit(solution)/shard_map/scores/pallas_call | solution.py:433
  53.4 9.7 %all-to-all-done.1 = f32[64,1,4224]{2,1,0:T(1,128)S(1)} async-done(((f32[64,1,4224]{2,1,0:T(1,128)}), f32[64,1,4224]{2,1,0:T(1,128)S(1)}, u32[]{:S(2)}, u32[]{:S(2)}) %all-to-all-start.1) | async-done | bytes 1081376 | tf_op jit(solution)/shard_map/all_to_all | solution.py:474
  63.1 6.1 %outs.1 = (bf16[128,2048]{1,0:T(8,128)(2,1)}, f32[128,2048]{1,0:T(8,128)}, bf16[16,256,128]{2,1,0:T(8,128)(2,1)}, f32[16,8,256]{2,1,0:T(8,128)}, f32[8,264,128]{2,1,0:T(8,128)}, /*index=5*/f32[8,128]{1,0:T(8,128)S(1)}) custom-call(s32[1]{0:T(128)} %bitcast.refs_0_.core_ref, f32[8,264,128]{2,1,0:T(8,128)S(1)} %bitcast.13, ...), custom_call_target="tpu_custom_call" | custom-call | tf_op jit(solution)/shard_map/outs/pallas_call | solution.py:433
  69.1 5.9 %all-to-all-start.2 = ((f32[64,1,4224]{2,1,0:T(1,128)}), f32[64,1,4224]{2,1,0:T(1,128)S(1)}, u32[]{:S(2)}, u32[]{:S(2)}) async-start(f32[64,1,4224]{2,1,0:T(1,128)} %bitcast.27), calls=%async_computation.2 | async-start | bytes 2162688 | tf_op jit(solution)/shard_map/all_to_all | solution.py:474
  75.1 9.9 %grids.1 = (f32[4,2,264,128]{3,2,1,0:T(8,128)}, f32[16,128,256]{2,1,0:T(8,128)S(1)}) custom-call(s32[1]{0:T(128)} %bitcast.refs_0_.core_ref, bf16[16,256,128]{2,1,0:T(8,128)(2,1)} %get-tuple-element.53.refs_1_, bf16[16,256,128]{2,1,0:T(8,128)(2,1)} %get-tuple-element.45.refs_5_.refs_2_, f32[16,8,256]{2,1,0:T(8,128)} %get-tuple-element.54.refs_3_, ...), custom_call_target="tpu_custom_call" | custom-call | tf_op jit(solution)/shard_map/grids/pallas_call | solution.py:433
  85.0 6.8 %all-to-all-done.2 = f32[64,1,4224]{2,1,0:T(1,128)S(1)} async-done(((f32[64,1,4224]{2,1,0:T(1,128)}), f32[64,1,4224]{2,1,0:T(1,128)S(1)}, u32[]{:S(2)}, u32[]{:S(2)}) %all-to-all-start.2) | async-done | bytes 1081376 | tf_op jit(solution)/shard_map/all_to_all | solution.py:474
  91.8 1.1 scan.3
  92.9 4.7 %all-to-all-start.3 = ((f32[64,1,4224]{2,1,0:T(1,128)}), f32[64,1,4224]{2,1,0:T(1,128)S(1)}, u32[]{:S(2)}, u32[]{:S(2)}) async-start(f32[64,1,4224]{2,1,0:T(1,128)} %bitcast.23), calls=%async_computation.3 | async-start | bytes 2162688 | tf_op jit(solution)/shard_map/all_to_all | solution.py:474
  97.6 3.4 %collective-permute-start.4 = (f32[128,2048]{1,0:T(8,128)}, f32[128,2048]{1,0:T(8,128)S(1)}, u32[]{:S(2)}, u32[]{:S(2)}) collective-permute-start(f32[128,2048]{1,0:T(8,128)} %get-tuple-element.60), channel_id=1, source_target_pairs={{0,1},{1,0},{2,3},{3,2},{4,5},{5,4},{6,7},{7,6},{8,9},{9,8},{10,11... | collective-permute-start | bytes 3145736 | tf_op jit(solution)/shard_map/ppermute | solution.py:486
  101.1 2.4 %collective-permute-done.4.refs_2_ = f32[128,2048]{1,0:T(8,128)S(1)} collective-permute-done((f32[128,2048]{1,0:T(8,128)}, f32[128,2048]{1,0:T(8,128)S(1)}, u32[]{:S(2)}, u32[]{:S(2)}) %collective-permute-start.4) | collective-permute-done | bytes 1048608 | tf_op jit(solution)/shard_map/ppermute | solution.py:486
  103.5 1.0 copy-done.1
  104.4 9.1 %all-to-all-done.3 = f32[64,1,4224]{2,1,0:T(1,128)S(1)} async-done(((f32[64,1,4224]{2,1,0:T(1,128)}), f32[64,1,4224]{2,1,0:T(1,128)S(1)}, u32[]{:S(2)}, u32[]{:S(2)}) %all-to-all-start.3) | async-done | bytes 1081376 | tf_op jit(solution)/shard_map/all_to_all | solution.py:474
  113.6 4.5 %last.1 = f32[4,2,264,128]{3,2,1,0:T(8,128)} custom-call(s32[1]{0:T(128)} %bitcast.refs_0_.core_ref, f32[8,264,128]{2,1,0:T(8,128)S(1)} %bitcast.15, bf16[16,256,128]{2,1,0:T(8,128)(2,1)} %get-tuple-element.45.refs_5_.refs_2_, bf16[16,128,256]{2,1,0:T(8,128)(2,1)} %get-tuple-element.44.refs_4_.refs_5_.refs_3_, ...), custom_call_target="tpu_custom_call", output_to_operand_aliasing={{}: (8, {})} | custom-call | tf_op jit(solution)/shard_map/last/pallas_call | solution.py:433
  118.1 5.2 %all-to-all-start.4 = ((f32[64,1,4224]{2,1,0:T(1,128)}), f32[64,1,4224]{2,1,0:T(1,128)S(1)}, u32[]{:S(2)}, u32[]{:S(2)}) async-start(f32[64,1,4224]{2,1,0:T(1,128)} %bitcast.22), calls=%async_computation.4 | async-start | bytes 2162688 | tf_op jit(solution)/shard_map/all_to_all | solution.py:474
  123.3 2.1 %merge.1 = bf16[128,4096]{1,0:T(8,128)(2,1)} custom-call(s32[1]{0:T(128)} %bitcast.refs_0_.core_ref, bf16[128,2048]{1,0:T(8,128)(2,1)} %get-tuple-element.66.refs_1_, f32[128,2048]{1,0:T(8,128)S(1)} %copy-done.2), custom_call_target="tpu_custom_call" | custom-call | tf_op jit(solution)/shard_map/merge/pallas_call | solution.py:433
  125.4 13.3 %all-to-all-done.4 = f32[64,1,4224]{2,1,0:T(1,128)S(1)} async-done(((f32[64,1,4224]{2,1,0:T(1,128)}), f32[64,1,4224]{2,1,0:T(1,128)S(1)}, u32[]{:S(2)}, u32[]{:S(2)}) %all-to-all-start.4) | async-done | bytes 1081376 | tf_op jit(solution)/shard_map/all_to_all | solution.py:474
  138.7 1.2 sum.1
  139.9 19.2 %all_to_all.30 = f32[64,1,4224]{2,1,0:T(1,128)S(1)} all-to-all(f32[64,1,4224]{2,1,0:T(1,128)} %bitcast.25), channel_id=1, replica_groups=mesh['x'=4,'z'=4,'y'=4,'c'=2] {'x','z','y'}, dimensions={0} | all-to-all | bytes 2162688 | tf_op jit(solution)/shard_map/all_to_all | solution.py:474
  159.1 5.6 %collective-permute-start.6 = (f32[4,2,264,128]{3,2,1,0:T(8,128)S(1)}, f32[4,2,264,128]{3,2,1,0:T(8,128)S(1)}, u32[]{:S(2)}, u32[]{:S(2)}) collective-permute-start(f32[4,2,264,128]{3,2,1,0:T(8,128)S(1)} %bitcast.19), channel_id=1, source_target_pairs={{0,1},{1,0},{2,3},{3,2},{4,5},{5,4},{6,7},{7,6},{8,9},{9,8},{10,11... | collective-permute-start | bytes 3244040 | tf_op jit(solution)/shard_map/ppermute | solution.py:486
  164.7 1.0 unpack_mine.1
  167.0 1.1 unpack.1
  (20 shorter events, 2.7 us)
Async XLA Ops:
  0.6 2.7 %copy-start.3 = (bf16[128,4096]{1,0:T(8,128)(2,1)S(1)}, bf16[128,4096]{1,0:T(8,128)(2,1)}, u32[]{:S(2)}) copy-start(bf16[128,4096]{1,0:T(8,128)(2,1)} %refs_1_.4) | copy-start | bytes 3145732
  1.9 1.7 %copy-start.4 = (bf16[128,4096]{1,0:T(8,128)(2,1)S(1)}, bf16[128,4096]{1,0:T(8,128)(2,1)}, u32[]{:S(2)}) copy-start(bf16[128,4096]{1,0:T(8,128)(2,1)} %refs_6_.1) | copy-start | bytes 3145732
  1.9 3.7 %collective-permute-start.1 = (f32[128,2048]{1,0:T(8,128)S(1)}, f32[128,2048]{1,0:T(8,128)S(1)}, u32[]{:S(2)}, u32[]{:S(2)}) collective-permute-start(f32[128,2048]{1,0:T(8,128)S(1)} %dynamic-slice_convert_fusion.2), channel_id=1, source_target_pairs={{0,1},{1,0},{2,3},{3,2},{4,5},{5,4},{6,7},{7,6},{8,9},{9,8},{10,11... | collective-permute-start | bytes 3145736 | tf_op jit(solution)/shard_map/ppermute | solution.py:486
  3.5 3.7 %collective-permute-start = (f32[128,2048]{1,0:T(8,128)S(1)}, f32[128,2048]{1,0:T(8,128)S(1)}, u32[]{:S(2)}, u32[]{:S(2)}) collective-permute-start(f32[128,2048]{1,0:T(8,128)S(1)} %dynamic-slice_convert_fusion.3), channel_id=1, source_target_pairs={{0,1},{1,0},{2,3},{3,2},{4,5},{5,4},{6,7},{7,6},{8,9},{9,8},{10,11... | collective-permute-start | bytes 3145736 | tf_op jit(solution)/shard_map/ppermute | solution.py:486
  4.6 22.4 %collective-permute-start.3 = (f32[128,2048]{1,0:T(8,128)}, f32[128,2048]{1,0:T(8,128)}, u32[]{:S(2)}, u32[]{:S(2)}) collective-permute-start(f32[128,2048]{1,0:T(8,128)} %dynamic-slice_convert_fusion), channel_id=1, source_target_pairs={{0,1},{1,0},{2,3},{3,2},{4,5},{5,4},{6,7},{7,6},{8,9},{9,8},{10,11... | collective-permute-start | bytes 3145736 | tf_op jit(solution)/shard_map/ppermute | solution.py:486
  11.2 28.6 %all-to-all-start = ((f32[64,1,4224]{2,1,0:T(1,128)}), f32[64,1,4224]{2,1,0:T(1,128)S(1)}, u32[]{:S(2)}, u32[]{:S(2)}) async-start(f32[64,1,4224]{2,1,0:T(1,128)} %bitcast.26), calls=%async_computation | async-start | bytes 2162688 | tf_op jit(solution)/shard_map/all_to_all | solution.py:474
  23.6 3.4 %collective-permute-start.2 = (f32[128,2048]{1,0:T(8,128)S(1)}, f32[128,2048]{1,0:T(8,128)}, u32[]{:S(2)}, u32[]{:S(2)}) collective-permute-start(f32[128,2048]{1,0:T(8,128)S(1)} %dynamic-slice_convert_fusion.1), channel_id=1, source_target_pairs={{0,1},{1,0},{2,3},{3,2},{4,5},{5,4},{6,7},{7,6},{8,9},{9,8},{10,11... | collective-permute-start | bytes 3145736 | tf_op jit(solution)/shard_map/ppermute | solution.py:486
  40.9 22.1 %all-to-all-start.1 = ((f32[64,1,4224]{2,1,0:T(1,128)}), f32[64,1,4224]{2,1,0:T(1,128)S(1)}, u32[]{:S(2)}, u32[]{:S(2)}) async-start(f32[64,1,4224]{2,1,0:T(1,128)} %bitcast.24), calls=%async_computation.1 | async-start | bytes 2162688 | tf_op jit(solution)/shard_map/all_to_all | solution.py:474
  63.1 6.1 %copy-start = (f32[64,1,4224]{2,1,0:T(1,128)}, f32[64,1,4224]{2,1,0:T(1,128)S(1)}, u32[]{:S(2)}) copy-start(f32[64,1,4224]{2,1,0:T(1,128)S(1)} %all-to-all-done.1) | copy-start | bytes 3244036
  69.1 22.7 %all-to-all-start.2 = ((f32[64,1,4224]{2,1,0:T(1,128)}), f32[64,1,4224]{2,1,0:T(1,128)S(1)}, u32[]{:S(2)}, u32[]{:S(2)}) async-start(f32[64,1,4224]{2,1,0:T(1,128)} %bitcast.27), calls=%async_computation.2 | async-start | bytes 2162688 | tf_op jit(solution)/shard_map/all_to_all | solution.py:474
  92.9 20.6 %all-to-all-start.3 = ((f32[64,1,4224]{2,1,0:T(1,128)}), f32[64,1,4224]{2,1,0:T(1,128)S(1)}, u32[]{:S(2)}, u32[]{:S(2)}) async-start(f32[64,1,4224]{2,1,0:T(1,128)} %bitcast.23), calls=%async_computation.3 | async-start | bytes 2162688 | tf_op jit(solution)/shard_map/all_to_all | solution.py:474
  97.6 5.9 %collective-permute-start.4 = (f32[128,2048]{1,0:T(8,128)}, f32[128,2048]{1,0:T(8,128)S(1)}, u32[]{:S(2)}, u32[]{:S(2)}) collective-permute-start(f32[128,2048]{1,0:T(8,128)} %get-tuple-element.60), channel_id=1, source_target_pairs={{0,1},{1,0},{2,3},{3,2},{4,5},{5,4},{6,7},{7,6},{8,9},{9,8},{10,11... | collective-permute-start | bytes 3145736 | tf_op jit(solution)/shard_map/ppermute | solution.py:486
  101.0 12.6 %collective-permute-start.5 = (f32[8,128]{1,0:T(8,128)S(1)}, f32[8,128]{1,0:T(8,128)S(1)}, u32[]{:S(2)}, u32[]{:S(2)}) collective-permute-start(f32[8,128]{1,0:T(8,128)S(1)} %get-tuple-element.64.refs_6_), channel_id=1, source_target_pairs={{0,1},{1,0},{2,3},{3,2},{4,5},{5,4},{6,7},{7,6},{8,9},{9,8},{10,11... | collective-permute-start | bytes 12296 | tf_op jit(solution)/shard_map/ppermute | solution.py:486
  103.5 1.0 copy-start.1
  118.1 5.2 %copy-start.2 = (f32[128,2048]{1,0:T(8,128)S(1)}, f32[128,2048]{1,0:T(8,128)}, u32[]{:S(2)}) copy-start(f32[128,2048]{1,0:T(8,128)} %copy-done.1) | copy-start | bytes 3145732
  118.1 20.6 %all-to-all-start.4 = ((f32[64,1,4224]{2,1,0:T(1,128)}), f32[64,1,4224]{2,1,0:T(1,128)S(1)}, u32[]{:S(2)}, u32[]{:S(2)}) async-start(f32[64,1,4224]{2,1,0:T(1,128)} %bitcast.22), calls=%async_computation.4 | async-start | bytes 2162688 | tf_op jit(solution)/shard_map/all_to_all | solution.py:474
  159.1 7.9 %collective-permute-start.6 = (f32[4,2,264,128]{3,2,1,0:T(8,128)S(1)}, f32[4,2,264,128]{3,2,1,0:T(8,128)S(1)}, u32[]{:S(2)}, u32[]{:S(2)}) collective-permute-start(f32[4,2,264,128]{3,2,1,0:T(8,128)S(1)} %bitcast.19), channel_id=1, source_target_pairs={{0,1},{1,0},{2,3},{3,2},{4,5},{5,4},{6,7},{7,6},{8,9},{9,8},{10,11... | collective-permute-start | bytes 3244040 | tf_op jit(solution)/shard_map/ppermute | solution.py:486

commit v6 on v5

--- a/solution.py
+++ b/solution.py
@@ -19,7 +19,7 @@
 WIDTH = 128
 PIECE = 33
 PAIRS = HALF // 2
-GROUPS = ((8, 8), (12, 4))
+GROUPS = ((8, 8), (4, 4, 4, 4))
 PROWS = 2 * 4 * PIECE
 
 NN = ((1,), (0,))
@@ -181,7 +181,7 @@
         yield
         y = (num_ref[h] + carried) * inv
         y_own[:, columns(h)] = y[:ROWS].astype(BF16)
-        y_send[:, columns(h)] = y[ROWS:]
+        y_send[:, columns(h)] = y[ROWS:].astype(BF16)
         err = y - tf[h].astype(F32)
         loss_ref[...] += jnp.sum((err * err).reshape(TOK // 8, 8, WIDTH), axis=0)
         dnum = (scale * err) * inv
@@ -531,9 +531,9 @@
         out_kernel, "outs",
         [(pre, None), (num, None), (phiq, features[1]), (phiqb, natural[1]), (den, row[1]),
          (tf, natural[1])],
-        [(sds((ROWS, half), BF16), cols), (sds((ROWS, half)), cols), natural, row, payload,
+        [(sds((ROWS, half), BF16), cols), (sds((ROWS, half), BF16), cols), natural, row, payload,
          lossy],
-        groups=((6, 10), (12, 4)),
+        groups=((6, 10), (4, 4, 4, 2, 2)),
     )
     loss_other = swap(loss)
     gathered = exchange(send)
@@ -546,7 +546,7 @@
     gathered, dphik, query_sent, y_send = lax.optimization_barrier(
         (gathered, dphik, query_sent, y_send)
     )
-    y_other = swap(y_send)
+    y_other = swap(y_send.astype(F32))
     suf, y_other = lax.optimization_barrier((exchange(scan(core, gathered, True)), y_other))
     send, = call(
         last_kernel, "last", core,

time: 170 us -> 169 us (level)
  transfers between devices with their start and end apart: 12 -> 12, of which waited for: 8 -> 8; matrix products, arithmetic and copies ran while one was open for 2% -> 2% of each run, Pallas kernels for 16% -> 15%
where the time goes in v6:
time: 169 us; the launch traced here: 168 us
  waiting for transfers between devices  55.4 us (33%)
  starting transfers between devices  45 us (27%)
  Pallas kernels  40.1 us (24%)
  blocking collectives  19.2 us (11%)
  other arithmetic  5.26 us (3%)
  between operations  2.65 us (2%)
    all_to_all x5, waiting for transfers between devices, exchange(): lax.all_to_all(x.reshape(NCHIP, 1, PIECE * WIDTH), CHIPS, 0, 0, tiled=True)  51.6 us
    pallas_call x12, Pallas kernels, raw_call(): pl.pallas_call(body, in_specs=[pl.BlockSpec(memory_space=pltpu.SMEM)] + [...  40.1 us
    all_to_all x5, starting transfers between devices, exchange(): lax.all_to_all(x.reshape(NCHIP, 1, PIECE * WIDTH), CHIPS, 0, 0, tiled=True)  32.7 us
    all_to_all x1, blocking collectives, exchange(): lax.all_to_all(x.reshape(NCHIP, 1, PIECE * WIDTH), CHIPS, 0, 0, tiled=True)  19.2 us
    ppermute x7, starting transfers between devices, swap(): return lax.ppermute(x, 'c', [(0, 1), (1, 0)])  12.3 us
    ppermute x7, waiting for transfers between devices, swap(): return lax.ppermute(x, 'c', [(0, 1), (1, 0)])  3.79 us
    convert_element_type x4, other arithmetic, others(): return swap(part.astype(F32))  3.52 us
  transfers between devices with their start and end apart: 12, of which 8 were waited for; matrix products, arithmetic and copies ran while one was open for 2% of the time, Pallas kernels for 15%

profile of v6, /device:TPU:1, one launch (start us, length us, event | category | flops | bytes accessed | tf_op | source)
XLA Modules:
  0.0 168.5 jit_solution(7017135445534464878)
XLA Ops:
  0.6 1.2 dynamic-slice_convert_fusion.2
  1.9 1.5 collective-permute-start.1
  3.6 1.1 dynamic-slice_convert_fusion
  5.6 1.5 collective-permute-done.refs_2_
  7.1 3.9 %keys.1 = (bf16[16,128,256]{2,1,0:T(8,128)(2,1)}, f32[8,264,128]{2,1,0:T(8,128)}) custom-call(s32[1]{0:T(128)} %bitcast.refs_0_.core_ref, bf16[128,4096]{1,0:T(8,128)(2,1)} %refs_1_.4, f32[128,2048]{1,0:T(8,128)S(1)} %collective-permute-done.refs_2_, bf16[128,4096]{1,0:T(8,128)(2,1)} %refs_3_.4, f32[128,2048]{1,0:T(8,128)S(1)} %collective-permute-done.1.refs_4_, ...), custom_call_target="tpu_custom_call" | custom-call | tf_op jit(solution)/shard_map/keys/pallas_call | solution.py:433
  11.1 11.3 %all-to-all-start = ((f32[64,1,4224]{2,1,0:T(1,128)}), f32[64,1,4224]{2,1,0:T(1,128)S(1)}, u32[]{:S(2)}, u32[]{:S(2)}) async-start(f32[64,1,4224]{2,1,0:T(1,128)} %bitcast.26), calls=%async_computation | async-start | bytes 2162688 | tf_op jit(solution)/shard_map/all_to_all | solution.py:474
  22.4 1.1 dynamic-slice_convert_fusion.1
  24.2 2.5 %pack.1 = (bf16[16,256,128]{2,1,0:T(8,128)(2,1)}, bf16[16,256,128]{2,1,0:T(8,128)(2,1)}) custom-call(s32[1]{0:T(128)} %bitcast.refs_0_.core_ref, bf16[128,4096]{1,0:T(8,128)(2,1)} %refs_1_.4, f32[128,2048]{1,0:T(8,128)S(1)} %collective-permute-done.refs_2_, bf16[128,4096]{1,0:T(8,128)(2,1)} %refs_3_.4, f32[128,2048]{1,0:T(8,128)S(1)} %collective-permute-done.1.refs_4_), custom_call_target="tpu_custom_call" | custom-call | tf_op jit(solution)/shard_map/pack/pallas_call | solution.py:433
  26.8 12.9 %all-to-all-done = f32[64,1,4224]{2,1,0:T(1,128)S(1)} async-done(((f32[64,1,4224]{2,1,0:T(1,128)}), f32[64,1,4224]{2,1,0:T(1,128)S(1)}, u32[]{:S(2)}, u32[]{:S(2)}) %all-to-all-start) | async-done | bytes 1081376 | tf_op jit(solution)/shard_map/all_to_all | solution.py:474
  39.7 1.1 scan.2
  40.8 5.7 %all-to-all-start.1 = ((f32[64,1,4224]{2,1,0:T(1,128)}), f32[64,1,4224]{2,1,0:T(1,128)S(1)}, u32[]{:S(2)}, u32[]{:S(2)}) async-start(f32[64,1,4224]{2,1,0:T(1,128)} %bitcast.24), calls=%async_computation.1 | async-start | bytes 2162688 | tf_op jit(solution)/shard_map/all_to_all | solution.py:474
  46.5 6.2 %scores.1 = (bf16[16,256,128]{2,1,0:T(8,128)(2,1)}, f32[16,128,256]{2,1,0:T(8,128)}, bf16[16,256,128]{2,1,0:T(8,128)(2,1)}, bf16[16,256,128]{2,1,0:T(8,128)(2,1)...) custom-call(s32[1]{0:T(128)} %bitcast.refs_0_.core_ref, bf16[128,4096]{1,0:T(8,128)(2,1)} %refs_1_.5, ...), custom_call_target="tpu_custom_call" | custom-call | tf_op jit(solution)/shard_map/scores/pallas_call | solution.py:433
  52.6 10.3 %all-to-all-done.1 = f32[64,1,4224]{2,1,0:T(1,128)S(1)} async-done(((f32[64,1,4224]{2,1,0:T(1,128)}), f32[64,1,4224]{2,1,0:T(1,128)S(1)}, u32[]{:S(2)}, u32[]{:S(2)}) %all-to-all-start.1) | async-done | bytes 1081376 | tf_op jit(solution)/shard_map/all_to_all | solution.py:474
  62.9 5.4 %outs.1 = (bf16[128,2048]{1,0:T(8,128)(2,1)}, bf16[128,2048]{1,0:T(8,128)(2,1)}, bf16[16,256,128]{2,1,0:T(8,128)(2,1)}, f32[16,8,256]{2,1,0:T(8,128)}, f32[8,264,128]{2,1,0:T(8,128)}, /*index=5*/f32[8,128]{1,0:T(8,128)S(1)}) custom-call(s32[1]{0:T(128)} %bitcast.refs_0_.core_ref, f32[8,264,128]{2,1,0:T(8,128)S(1)} %bitcast.13, ...), custom_call_target="tpu_custom_call" | custom-call | tf_op jit(solution)/shard_map/outs/pallas_call | solution.py:433
  68.4 5.9 %all-to-all-start.2 = ((f32[64,1,4224]{2,1,0:T(1,128)}), f32[64,1,4224]{2,1,0:T(1,128)S(1)}, u32[]{:S(2)}, u32[]{:S(2)}) async-start(f32[64,1,4224]{2,1,0:T(1,128)} %bitcast.27), calls=%async_computation.2 | async-start | bytes 2162688 | tf_op jit(solution)/shard_map/all_to_all | solution.py:474
  74.3 10.0 %grids.1 = (f32[4,2,264,128]{3,2,1,0:T(8,128)}, f32[16,128,256]{2,1,0:T(8,128)S(1)}) custom-call(s32[1]{0:T(128)} %bitcast.refs_0_.core_ref, bf16[16,256,128]{2,1,0:T(8,128)(2,1)} %get-tuple-element.53.refs_1_, bf16[16,256,128]{2,1,0:T(8,128)(2,1)} %get-tuple-element.45.refs_5_.refs_2_, f32[16,8,256]{2,1,0:T(8,128)} %get-tuple-element.54.refs_3_, ...), custom_call_target="tpu_custom_call" | custom-call | tf_op jit(solution)/shard_map/grids/pallas_call | solution.py:433
  84.3 6.8 %all-to-all-done.2 = f32[64,1,4224]{2,1,0:T(1,128)S(1)} async-done(((f32[64,1,4224]{2,1,0:T(1,128)}), f32[64,1,4224]{2,1,0:T(1,128)S(1)}, u32[]{:S(2)}, u32[]{:S(2)}) %all-to-all-start.2) | async-done | bytes 1081376 | tf_op jit(solution)/shard_map/all_to_all | solution.py:474
  91.1 1.1 scan.3
  92.2 4.7 %all-to-all-start.3 = ((f32[64,1,4224]{2,1,0:T(1,128)}), f32[64,1,4224]{2,1,0:T(1,128)S(1)}, u32[]{:S(2)}, u32[]{:S(2)}) async-start(f32[64,1,4224]{2,1,0:T(1,128)} %bitcast.23), calls=%async_computation.3 | async-start | bytes 2162688 | tf_op jit(solution)/shard_map/all_to_all | solution.py:474
  96.8 1.1 convert_element_type.19
  98.0 3.4 %collective-permute-start.4 = (f32[128,2048]{1,0:T(8,128)S(1)}, f32[128,2048]{1,0:T(8,128)S(1)}, u32[]{:S(2)}, u32[]{:S(2)}) collective-permute-start(f32[128,2048]{1,0:T(8,128)S(1)} %convert_element_type.19), channel_id=1, source_target_pairs={{0,1},{1,0},{2,3},{3,2},{4,5},{5,4},{6,7},{7,6},{8,9},{9,8},{10,11... | collective-permute-start | bytes 3145736 | tf_op jit(solution)/shard_map/ppermute | solution.py:486
  101.4 2.2 %collective-permute-done.4.refs_2_ = f32[128,2048]{1,0:T(8,128)S(1)} collective-permute-done((f32[128,2048]{1,0:T(8,128)S(1)}, f32[128,2048]{1,0:T(8,128)S(1)}, u32[]{:S(2)}, u32[]{:S(2)}) %collective-permute-start.4) | collective-permute-done | bytes 1048608 | tf_op jit(solution)/shard_map/ppermute | solution.py:486
  104.6 8.2 %all-to-all-done.3 = f32[64,1,4224]{2,1,0:T(1,128)S(1)} async-done(((f32[64,1,4224]{2,1,0:T(1,128)}), f32[64,1,4224]{2,1,0:T(1,128)S(1)}, u32[]{:S(2)}, u32[]{:S(2)}) %all-to-all-start.3) | async-done | bytes 1081376 | tf_op jit(solution)/shard_map/all_to_all | solution.py:474
  112.8 4.6 %last.1 = f32[4,2,264,128]{3,2,1,0:T(8,128)} custom-call(s32[1]{0:T(128)} %bitcast.refs_0_.core_ref, f32[8,264,128]{2,1,0:T(8,128)S(1)} %bitcast.15, bf16[16,256,128]{2,1,0:T(8,128)(2,1)} %get-tuple-element.45.refs_5_.refs_2_, bf16[16,128,256]{2,1,0:T(8,128)(2,1)} %get-tuple-element.44.refs_4_.refs_5_.refs_3_, ...), custom_call_target="tpu_custom_call", output_to_operand_aliasing={{}: (8, {})} | custom-call | tf_op jit(solution)/shard_map/last/pallas_call | solution.py:433
  117.4 5.2 %all-to-all-start.4 = ((f32[64,1,4224]{2,1,0:T(1,128)}), f32[64,1,4224]{2,1,0:T(1,128)S(1)}, u32[]{:S(2)}, u32[]{:S(2)}) async-start(f32[64,1,4224]{2,1,0:T(1,128)} %bitcast.22), calls=%async_computation.4 | async-start | bytes 2162688 | tf_op jit(solution)/shard_map/all_to_all | solution.py:474
  122.6 2.0 %merge.1 = bf16[128,4096]{1,0:T(8,128)(2,1)} custom-call(s32[1]{0:T(128)} %bitcast.refs_0_.core_ref, bf16[128,2048]{1,0:T(8,128)(2,1)} %get-tuple-element.66.refs_1_, f32[128,2048]{1,0:T(8,128)S(1)} %copy-done.2), custom_call_target="tpu_custom_call" | custom-call | tf_op jit(solution)/shard_map/merge/pallas_call | solution.py:433
  124.6 13.4 %all-to-all-done.4 = f32[64,1,4224]{2,1,0:T(1,128)S(1)} async-done(((f32[64,1,4224]{2,1,0:T(1,128)}), f32[64,1,4224]{2,1,0:T(1,128)S(1)}, u32[]{:S(2)}, u32[]{:S(2)}) %all-to-all-start.4) | async-done | bytes 1081376 | tf_op jit(solution)/shard_map/all_to_all | solution.py:474
  138.0 1.2 sum.1
  139.2 19.2 %all_to_all.30 = f32[64,1,4224]{2,1,0:T(1,128)S(1)} all-to-all(f32[64,1,4224]{2,1,0:T(1,128)} %bitcast.25), channel_id=1, replica_groups=mesh['x'=4,'z'=4,'y'=4,'c'=2] {'x','z','y'}, dimensions={0} | all-to-all | bytes 2162688 | tf_op jit(solution)/shard_map/all_to_all | solution.py:474
  158.3 5.6 %collective-permute-start.6 = (f32[4,2,264,128]{3,2,1,0:T(8,128)S(1)}, f32[4,2,264,128]{3,2,1,0:T(8,128)S(1)}, u32[]{:S(2)}, u32[]{:S(2)}) collective-permute-start(f32[4,2,264,128]{3,2,1,0:T(8,128)S(1)} %bitcast.19), channel_id=1, source_target_pairs={{0,1},{1,0},{2,3},{3,2},{4,5},{5,4},{6,7},{7,6},{8,9},{9,8},{10,11... | collective-permute-start | bytes 3244040 | tf_op jit(solution)/shard_map/ppermute | solution.py:486
  163.9 1.1 unpack_mine.1
  166.3 1.1 unpack.1
  (21 shorter events, 3.6 us)
Async XLA Ops:
  0.6 2.7 %copy-start.3 = (bf16[128,4096]{1,0:T(8,128)(2,1)S(1)}, bf16[128,4096]{1,0:T(8,128)(2,1)}, u32[]{:S(2)}) copy-start(bf16[128,4096]{1,0:T(8,128)(2,1)} %refs_1_.4) | copy-start | bytes 3145732
  1.9 1.7 %copy-start.4 = (bf16[128,4096]{1,0:T(8,128)(2,1)S(1)}, bf16[128,4096]{1,0:T(8,128)(2,1)}, u32[]{:S(2)}) copy-start(bf16[128,4096]{1,0:T(8,128)(2,1)} %refs_6_.1) | copy-start | bytes 3145732
  1.9 3.7 %collective-permute-start.1 = (f32[128,2048]{1,0:T(8,128)S(1)}, f32[128,2048]{1,0:T(8,128)S(1)}, u32[]{:S(2)}, u32[]{:S(2)}) collective-permute-start(f32[128,2048]{1,0:T(8,128)S(1)} %dynamic-slice_convert_fusion.2), channel_id=1, source_target_pairs={{0,1},{1,0},{2,3},{3,2},{4,5},{5,4},{6,7},{7,6},{8,9},{9,8},{10,11... | collective-permute-start | bytes 3145736 | tf_op jit(solution)/shard_map/ppermute | solution.py:486
  3.5 3.7 %collective-permute-start = (f32[128,2048]{1,0:T(8,128)S(1)}, f32[128,2048]{1,0:T(8,128)S(1)}, u32[]{:S(2)}, u32[]{:S(2)}) collective-permute-start(f32[128,2048]{1,0:T(8,128)S(1)} %dynamic-slice_convert_fusion.3), channel_id=1, source_target_pairs={{0,1},{1,0},{2,3},{3,2},{4,5},{5,4},{6,7},{7,6},{8,9},{9,8},{10,11... | collective-permute-start | bytes 3145736 | tf_op jit(solution)/shard_map/ppermute | solution.py:486
  4.6 22.1 %collective-permute-start.3 = (f32[128,2048]{1,0:T(8,128)}, f32[128,2048]{1,0:T(8,128)}, u32[]{:S(2)}, u32[]{:S(2)}) collective-permute-start(f32[128,2048]{1,0:T(8,128)} %dynamic-slice_convert_fusion), channel_id=1, source_target_pairs={{0,1},{1,0},{2,3},{3,2},{4,5},{5,4},{6,7},{7,6},{8,9},{9,8},{10,11... | collective-permute-start | bytes 3145736 | tf_op jit(solution)/shard_map/ppermute | solution.py:486
  11.1 28.6 %all-to-all-start = ((f32[64,1,4224]{2,1,0:T(1,128)}), f32[64,1,4224]{2,1,0:T(1,128)S(1)}, u32[]{:S(2)}, u32[]{:S(2)}) async-start(f32[64,1,4224]{2,1,0:T(1,128)} %bitcast.26), calls=%async_computation | async-start | bytes 2162688 | tf_op jit(solution)/shard_map/all_to_all | solution.py:474
  23.5 3.3 %collective-permute-start.2 = (f32[128,2048]{1,0:T(8,128)S(1)}, f32[128,2048]{1,0:T(8,128)}, u32[]{:S(2)}, u32[]{:S(2)}) collective-permute-start(f32[128,2048]{1,0:T(8,128)S(1)} %dynamic-slice_convert_fusion.1), channel_id=1, source_target_pairs={{0,1},{1,0},{2,3},{3,2},{4,5},{5,4},{6,7},{7,6},{8,9},{9,8},{10,11... | collective-permute-start | bytes 3145736 | tf_op jit(solution)/shard_map/ppermute | solution.py:486
  40.8 22.1 %all-to-all-start.1 = ((f32[64,1,4224]{2,1,0:T(1,128)}), f32[64,1,4224]{2,1,0:T(1,128)S(1)}, u32[]{:S(2)}, u32[]{:S(2)}) async-start(f32[64,1,4224]{2,1,0:T(1,128)} %bitcast.24), calls=%async_computation.1 | async-start | bytes 2162688 | tf_op jit(solution)/shard_map/all_to_all | solution.py:474
  62.9 5.5 %copy-start = (f32[64,1,4224]{2,1,0:T(1,128)}, f32[64,1,4224]{2,1,0:T(1,128)S(1)}, u32[]{:S(2)}) copy-start(f32[64,1,4224]{2,1,0:T(1,128)S(1)} %all-to-all-done.1) | copy-start | bytes 3244036
  68.4 22.7 %all-to-all-start.2 = ((f32[64,1,4224]{2,1,0:T(1,128)}), f32[64,1,4224]{2,1,0:T(1,128)S(1)}, u32[]{:S(2)}, u32[]{:S(2)}) async-start(f32[64,1,4224]{2,1,0:T(1,128)} %bitcast.27), calls=%async_computation.2 | async-start | bytes 2162688 | tf_op jit(solution)/shard_map/all_to_all | solution.py:474
  92.2 20.6 %all-to-all-start.3 = ((f32[64,1,4224]{2,1,0:T(1,128)}), f32[64,1,4224]{2,1,0:T(1,128)S(1)}, u32[]{:S(2)}, u32[]{:S(2)}) async-start(f32[64,1,4224]{2,1,0:T(1,128)} %bitcast.23), calls=%async_computation.3 | async-start | bytes 2162688 | tf_op jit(solution)/shard_map/all_to_all | solution.py:474
  98.0 5.6 %collective-permute-start.4 = (f32[128,2048]{1,0:T(8,128)S(1)}, f32[128,2048]{1,0:T(8,128)S(1)}, u32[]{:S(2)}, u32[]{:S(2)}) collective-permute-start(f32[128,2048]{1,0:T(8,128)S(1)} %convert_element_type.19), channel_id=1, source_target_pairs={{0,1},{1,0},{2,3},{3,2},{4,5},{5,4},{6,7},{7,6},{8,9},{9,8},{10,11... | collective-permute-start | bytes 3145736 | tf_op jit(solution)/shard_map/ppermute | solution.py:486
  101.3 11.5 %collective-permute-start.5 = (f32[8,128]{1,0:T(8,128)S(1)}, f32[8,128]{1,0:T(8,128)S(1)}, u32[]{:S(2)}, u32[]{:S(2)}) collective-permute-start(f32[8,128]{1,0:T(8,128)S(1)} %get-tuple-element.64.refs_6_), channel_id=1, source_target_pairs={{0,1},{1,0},{2,3},{3,2},{4,5},{5,4},{6,7},{7,6},{8,9},{9,8},{10,11... | collective-permute-start | bytes 12296 | tf_op jit(solution)/shard_map/ppermute | solution.py:486
  103.6 1.0 copy-start.1
  117.4 5.2 %copy-start.2 = (f32[128,2048]{1,0:T(8,128)S(1)}, f32[128,2048]{1,0:T(8,128)}, u32[]{:S(2)}) copy-start(f32[128,2048]{1,0:T(8,128)} %copy-done.1) | copy-start | bytes 3145732
  117.4 20.6 %all-to-all-start.4 = ((f32[64,1,4224]{2,1,0:T(1,128)}), f32[64,1,4224]{2,1,0:T(1,128)S(1)}, u32[]{:S(2)}, u32[]{:S(2)}) async-start(f32[64,1,4224]{2,1,0:T(1,128)} %bitcast.22), calls=%async_computation.4 | async-start | bytes 2162688 | tf_op jit(solution)/shard_map/all_to_all | solution.py:474
  158.3 7.9 %collective-permute-start.6 = (f32[4,2,264,128]{3,2,1,0:T(8,128)S(1)}, f32[4,2,264,128]{3,2,1,0:T(8,128)S(1)}, u32[]{:S(2)}, u32[]{:S(2)}) collective-permute-start(f32[4,2,264,128]{3,2,1,0:T(8,128)S(1)} %bitcast.19), channel_id=1, source_target_pairs={{0,1},{1,0},{2,3},{3,2},{4,5},{5,4},{6,7},{7,6},{8,9},{9,8},{10,11... | collective-permute-start | bytes 3244040 | tf_op jit(solution)/shard_map/ppermute | solution.py:486

commit v7 on v6

--- a/solution.py
+++ b/solution.py
@@ -533,7 +533,7 @@
          (tf, natural[1])],
         [(sds((ROWS, half), BF16), cols), (sds((ROWS, half), BF16), cols), natural, row, payload,
          lossy],
-        groups=((6, 10), (4, 4, 4, 2, 2)),
+        groups=((4, 4, 8), (4, 4, 4, 2, 2)),
     )
     loss_other = swap(loss)
     gathered = exchange(send)
@@ -552,7 +552,7 @@
         last_kernel, "last", core,
         [(suf, None), (vf, natural[1]), (phik, halved[1]), (kf, natural[1]), (dphik, None),
          (loss, None), (loss_other, None), (query_sent, pltpu.HBM)],
-        [GRADS], [(0, quads_block(1))], aliases=[(8, 0)],
+        [GRADS], [(0, quads_block(1))], aliases=[(8, 0)], groups=((4, 4, 8), (4, 4, 4, 4)),
     )
     attn, = call(
         merge_kernel, "merge", core, [(y_own, cols), (y_other, None)],

time: 169 us -> 169 us (level)
  no operation moved by 1% of the time
where the time goes in v7:
time: 169 us; the launch traced here: 168 us
  waiting for transfers between devices  55.4 us (33%)
  starting transfers between devices  45 us (27%)
  Pallas kernels  39.9 us (24%)
  blocking collectives  19.2 us (11%)
  other arithmetic  5.26 us (3%)
  between operations  2.65 us (2%)
    all_to_all x5, waiting for transfers between devices, exchange(): lax.all_to_all(x.reshape(NCHIP, 1, PIECE * WIDTH), CHIPS, 0, 0, tiled=True)  51.6 us
    pallas_call x12, Pallas kernels, raw_call(): pl.pallas_call(body, in_specs=[pl.BlockSpec(memory_space=pltpu.SMEM)] + [...  39.9 us
    all_to_all x5, starting transfers between devices, exchange(): lax.all_to_all(x.reshape(NCHIP, 1, PIECE * WIDTH), CHIPS, 0, 0, tiled=True)  32.7 us
    all_to_all x1, blocking collectives, exchange(): lax.all_to_all(x.reshape(NCHIP, 1, PIECE * WIDTH), CHIPS, 0, 0, tiled=True)  19.2 us
    ppermute x7, starting transfers between devices, swap(): return lax.ppermute(x, 'c', [(0, 1), (1, 0)])  12.3 us
    ppermute x7, waiting for transfers between devices, swap(): return lax.ppermute(x, 'c', [(0, 1), (1, 0)])  3.79 us
    convert_element_type x4, other arithmetic, others(): return swap(part.astype(F32))  3.52 us
  transfers between devices with their start and end apart: 12, of which 8 were waited for; matrix products, arithmetic and copies ran while one was open for 2% of the time, Pallas kernels for 15%

profile of v7, /device:TPU:1, one launch (start us, length us, event | category | flops | bytes accessed | tf_op | source)
XLA Modules:
  0.0 168.3 jit_solution(10680437572478593739)
XLA Ops:
  0.6 1.2 dynamic-slice_convert_fusion.2
  1.9 1.5 collective-permute-start.1
  3.6 1.1 dynamic-slice_convert_fusion
  5.6 1.5 collective-permute-done.refs_2_
  7.1 3.9 %keys.1 = (bf16[16,128,256]{2,1,0:T(8,128)(2,1)}, f32[8,264,128]{2,1,0:T(8,128)}) custom-call(s32[1]{0:T(128)} %bitcast.refs_0_.core_ref, bf16[128,4096]{1,0:T(8,128)(2,1)} %refs_1_.4, f32[128,2048]{1,0:T(8,128)S(1)} %collective-permute-done.refs_2_, bf16[128,4096]{1,0:T(8,128)(2,1)} %refs_3_.4, f32[128,2048]{1,0:T(8,128)S(1)} %collective-permute-done.1.refs_4_, ...), custom_call_target="tpu_custom_call" | custom-call | tf_op jit(solution)/shard_map/keys/pallas_call | solution.py:433
  11.1 11.3 %all-to-all-start = ((f32[64,1,4224]{2,1,0:T(1,128)}), f32[64,1,4224]{2,1,0:T(1,128)S(1)}, u32[]{:S(2)}, u32[]{:S(2)}) async-start(f32[64,1,4224]{2,1,0:T(1,128)} %bitcast.26), calls=%async_computation | async-start | bytes 2162688 | tf_op jit(solution)/shard_map/all_to_all | solution.py:474
  22.4 1.1 dynamic-slice_convert_fusion.1
  24.2 2.5 %pack.1 = (bf16[16,256,128]{2,1,0:T(8,128)(2,1)}, bf16[16,256,128]{2,1,0:T(8,128)(2,1)}) custom-call(s32[1]{0:T(128)} %bitcast.refs_0_.core_ref, bf16[128,4096]{1,0:T(8,128)(2,1)} %refs_1_.4, f32[128,2048]{1,0:T(8,128)S(1)} %collective-permute-done.refs_2_, bf16[128,4096]{1,0:T(8,128)(2,1)} %refs_3_.4, f32[128,2048]{1,0:T(8,128)S(1)} %collective-permute-done.1.refs_4_), custom_call_target="tpu_custom_call" | custom-call | tf_op jit(solution)/shard_map/pack/pallas_call | solution.py:433
  26.8 12.9 %all-to-all-done = f32[64,1,4224]{2,1,0:T(1,128)S(1)} async-done(((f32[64,1,4224]{2,1,0:T(1,128)}), f32[64,1,4224]{2,1,0:T(1,128)S(1)}, u32[]{:S(2)}, u32[]{:S(2)}) %all-to-all-start) | async-done | bytes 1081376 | tf_op jit(solution)/shard_map/all_to_all | solution.py:474
  39.7 1.1 scan.2
  40.8 5.7 %all-to-all-start.1 = ((f32[64,1,4224]{2,1,0:T(1,128)}), f32[64,1,4224]{2,1,0:T(1,128)S(1)}, u32[]{:S(2)}, u32[]{:S(2)}) async-start(f32[64,1,4224]{2,1,0:T(1,128)} %bitcast.24), calls=%async_computation.1 | async-start | bytes 2162688 | tf_op jit(solution)/shard_map/all_to_all | solution.py:474
  46.5 6.2 %scores.1 = (bf16[16,256,128]{2,1,0:T(8,128)(2,1)}, f32[16,128,256]{2,1,0:T(8,128)}, bf16[16,256,128]{2,1,0:T(8,128)(2,1)}, bf16[16,256,128]{2,1,0:T(8,128)(2,1)...) custom-call(s32[1]{0:T(128)} %bitcast.refs_0_.core_ref, bf16[128,4096]{1,0:T(8,128)(2,1)} %refs_1_.5, ...), custom_call_target="tpu_custom_call" | custom-call | tf_op jit(solution)/shard_map/scores/pallas_call | solution.py:433
  52.6 10.3 %all-to-all-done.1 = f32[64,1,4224]{2,1,0:T(1,128)S(1)} async-done(((f32[64,1,4224]{2,1,0:T(1,128)}), f32[64,1,4224]{2,1,0:T(1,128)S(1)}, u32[]{:S(2)}, u32[]{:S(2)}) %all-to-all-start.1) | async-done | bytes 1081376 | tf_op jit(solution)/shard_map/all_to_all | solution.py:474
  62.9 5.3 %outs.1 = (bf16[128,2048]{1,0:T(8,128)(2,1)}, bf16[128,2048]{1,0:T(8,128)(2,1)}, bf16[16,256,128]{2,1,0:T(8,128)(2,1)}, f32[16,8,256]{2,1,0:T(8,128)}, f32[8,264,128]{2,1,0:T(8,128)}, /*index=5*/f32[8,128]{1,0:T(8,128)S(1)}) custom-call(s32[1]{0:T(128)} %bitcast.refs_0_.core_ref, f32[8,264,128]{2,1,0:T(8,128)S(1)} %bitcast.13, ...), custom_call_target="tpu_custom_call" | custom-call | tf_op jit(solution)/shard_map/outs/pallas_call | solution.py:433
  68.3 5.9 %all-to-all-start.2 = ((f32[64,1,4224]{2,1,0:T(1,128)}), f32[64,1,4224]{2,1,0:T(1,128)S(1)}, u32[]{:S(2)}, u32[]{:S(2)}) async-start(f32[64,1,4224]{2,1,0:T(1,128)} %bitcast.27), calls=%async_computation.2 | async-start | bytes 2162688 | tf_op jit(solution)/shard_map/all_to_all | solution.py:474
  74.2 10.0 %grids.1 = (f32[4,2,264,128]{3,2,1,0:T(8,128)}, f32[16,128,256]{2,1,0:T(8,128)S(1)}) custom-call(s32[1]{0:T(128)} %bitcast.refs_0_.core_ref, bf16[16,256,128]{2,1,0:T(8,128)(2,1)} %get-tuple-element.53.refs_1_, bf16[16,256,128]{2,1,0:T(8,128)(2,1)} %get-tuple-element.45.refs_5_.refs_2_, f32[16,8,256]{2,1,0:T(8,128)} %get-tuple-element.54.refs_3_, ...), custom_call_target="tpu_custom_call" | custom-call | tf_op jit(solution)/shard_map/grids/pallas_call | solution.py:433
  84.2 6.8 %all-to-all-done.2 = f32[64,1,4224]{2,1,0:T(1,128)S(1)} async-done(((f32[64,1,4224]{2,1,0:T(1,128)}), f32[64,1,4224]{2,1,0:T(1,128)S(1)}, u32[]{:S(2)}, u32[]{:S(2)}) %all-to-all-start.2) | async-done | bytes 1081376 | tf_op jit(solution)/shard_map/all_to_all | solution.py:474
  91.0 1.1 scan.3
  92.1 4.7 %all-to-all-start.3 = ((f32[64,1,4224]{2,1,0:T(1,128)}), f32[64,1,4224]{2,1,0:T(1,128)S(1)}, u32[]{:S(2)}, u32[]{:S(2)}) async-start(f32[64,1,4224]{2,1,0:T(1,128)} %bitcast.23), calls=%async_computation.3 | async-start | bytes 2162688 | tf_op jit(solution)/shard_map/all_to_all | solution.py:474
  96.7 1.1 convert_element_type.19
  97.9 3.4 %collective-permute-start.4 = (f32[128,2048]{1,0:T(8,128)S(1)}, f32[128,2048]{1,0:T(8,128)S(1)}, u32[]{:S(2)}, u32[]{:S(2)}) collective-permute-start(f32[128,2048]{1,0:T(8,128)S(1)} %convert_element_type.19), channel_id=1, source_target_pairs={{0,1},{1,0},{2,3},{3,2},{4,5},{5,4},{6,7},{7,6},{8,9},{9,8},{10,11... | collective-permute-start | bytes 3145736 | tf_op jit(solution)/shard_map/ppermute | solution.py:486
  101.3 2.2 %collective-permute-done.4.refs_2_ = f32[128,2048]{1,0:T(8,128)S(1)} collective-permute-done((f32[128,2048]{1,0:T(8,128)S(1)}, f32[128,2048]{1,0:T(8,128)S(1)}, u32[]{:S(2)}, u32[]{:S(2)}) %collective-permute-start.4) | collective-permute-done | bytes 1048608 | tf_op jit(solution)/shard_map/ppermute | solution.py:486
  104.5 8.2 %all-to-all-done.3 = f32[64,1,4224]{2,1,0:T(1,128)S(1)} async-done(((f32[64,1,4224]{2,1,0:T(1,128)}), f32[64,1,4224]{2,1,0:T(1,128)S(1)}, u32[]{:S(2)}, u32[]{:S(2)}) %all-to-all-start.3) | async-done | bytes 1081376 | tf_op jit(solution)/shard_map/all_to_all | solution.py:474
  112.7 4.5 %last.1 = f32[4,2,264,128]{3,2,1,0:T(8,128)} custom-call(s32[1]{0:T(128)} %bitcast.refs_0_.core_ref, f32[8,264,128]{2,1,0:T(8,128)S(1)} %bitcast.15, bf16[16,256,128]{2,1,0:T(8,128)(2,1)} %get-tuple-element.45.refs_5_.refs_2_, bf16[16,128,256]{2,1,0:T(8,128)(2,1)} %get-tuple-element.44.refs_4_.refs_5_.refs_3_, ...), custom_call_target="tpu_custom_call", output_to_operand_aliasing={{}: (8, {})} | custom-call | tf_op jit(solution)/shard_map/last/pallas_call | solution.py:433
  117.2 5.2 %all-to-all-start.4 = ((f32[64,1,4224]{2,1,0:T(1,128)}), f32[64,1,4224]{2,1,0:T(1,128)S(1)}, u32[]{:S(2)}, u32[]{:S(2)}) async-start(f32[64,1,4224]{2,1,0:T(1,128)} %bitcast.22), calls=%async_computation.4 | async-start | bytes 2162688 | tf_op jit(solution)/shard_map/all_to_all | solution.py:474
  122.4 2.0 %merge.1 = bf16[128,4096]{1,0:T(8,128)(2,1)} custom-call(s32[1]{0:T(128)} %bitcast.refs_0_.core_ref, bf16[128,2048]{1,0:T(8,128)(2,1)} %get-tuple-element.66.refs_1_, f32[128,2048]{1,0:T(8,128)S(1)} %copy-done.2), custom_call_target="tpu_custom_call" | custom-call | tf_op jit(solution)/shard_map/merge/pallas_call | solution.py:433
  124.5 13.4 %all-to-all-done.4 = f32[64,1,4224]{2,1,0:T(1,128)S(1)} async-done(((f32[64,1,4224]{2,1,0:T(1,128)}), f32[64,1,4224]{2,1,0:T(1,128)S(1)}, u32[]{:S(2)}, u32[]{:S(2)}) %all-to-all-start.4) | async-done | bytes 1081376 | tf_op jit(solution)/shard_map/all_to_all | solution.py:474
  137.8 1.2 sum.1
  139.0 19.2 %all_to_all.30 = f32[64,1,4224]{2,1,0:T(1,128)S(1)} all-to-all(f32[64,1,4224]{2,1,0:T(1,128)} %bitcast.25), channel_id=1, replica_groups=mesh['x'=4,'z'=4,'y'=4,'c'=2] {'x','z','y'}, dimensions={0} | all-to-all | bytes 2162688 | tf_op jit(solution)/shard_map/all_to_all | solution.py:474
  158.2 5.6 %collective-permute-start.6 = (f32[4,2,264,128]{3,2,1,0:T(8,128)S(1)}, f32[4,2,264,128]{3,2,1,0:T(8,128)S(1)}, u32[]{:S(2)}, u32[]{:S(2)}) collective-permute-start(f32[4,2,264,128]{3,2,1,0:T(8,128)S(1)} %bitcast.19), channel_id=1, source_target_pairs={{0,1},{1,0},{2,3},{3,2},{4,5},{5,4},{6,7},{7,6},{8,9},{9,8},{10,11... | collective-permute-start | bytes 3244040 | tf_op jit(solution)/shard_map/ppermute | solution.py:486
  163.8 1.1 unpack_mine.1
  166.1 1.1 unpack.1
  (21 shorter events, 3.6 us)
Async XLA Ops:
  0.6 2.7 %copy-start.3 = (bf16[128,4096]{1,0:T(8,128)(2,1)S(1)}, bf16[128,4096]{1,0:T(8,128)(2,1)}, u32[]{:S(2)}) copy-start(bf16[128,4096]{1,0:T(8,128)(2,1)} %refs_1_.4) | copy-start | bytes 3145732
  1.9 1.7 %copy-start.4 = (bf16[128,4096]{1,0:T(8,128)(2,1)S(1)}, bf16[128,4096]{1,0:T(8,128)(2,1)}, u32[]{:S(2)}) copy-start(bf16[128,4096]{1,0:T(8,128)(2,1)} %refs_6_.1) | copy-start | bytes 3145732
  1.9 3.7 %collective-permute-start.1 = (f32[128,2048]{1,0:T(8,128)S(1)}, f32[128,2048]{1,0:T(8,128)S(1)}, u32[]{:S(2)}, u32[]{:S(2)}) collective-permute-start(f32[128,2048]{1,0:T(8,128)S(1)} %dynamic-slice_convert_fusion.2), channel_id=1, source_target_pairs={{0,1},{1,0},{2,3},{3,2},{4,5},{5,4},{6,7},{7,6},{8,9},{9,8},{10,11... | collective-permute-start | bytes 3145736 | tf_op jit(solution)/shard_map/ppermute | solution.py:486
  3.5 3.7 %collective-permute-start = (f32[128,2048]{1,0:T(8,128)S(1)}, f32[128,2048]{1,0:T(8,128)S(1)}, u32[]{:S(2)}, u32[]{:S(2)}) collective-permute-start(f32[128,2048]{1,0:T(8,128)S(1)} %dynamic-slice_convert_fusion.3), channel_id=1, source_target_pairs={{0,1},{1,0},{2,3},{3,2},{4,5},{5,4},{6,7},{7,6},{8,9},{9,8},{10,11... | collective-permute-start | bytes 3145736 | tf_op jit(solution)/shard_map/ppermute | solution.py:486
  4.6 22.1 %collective-permute-start.3 = (f32[128,2048]{1,0:T(8,128)}, f32[128,2048]{1,0:T(8,128)}, u32[]{:S(2)}, u32[]{:S(2)}) collective-permute-start(f32[128,2048]{1,0:T(8,128)} %dynamic-slice_convert_fusion), channel_id=1, source_target_pairs={{0,1},{1,0},{2,3},{3,2},{4,5},{5,4},{6,7},{7,6},{8,9},{9,8},{10,11... | collective-permute-start | bytes 3145736 | tf_op jit(solution)/shard_map/ppermute | solution.py:486
  11.1 28.6 %all-to-all-start = ((f32[64,1,4224]{2,1,0:T(1,128)}), f32[64,1,4224]{2,1,0:T(1,128)S(1)}, u32[]{:S(2)}, u32[]{:S(2)}) async-start(f32[64,1,4224]{2,1,0:T(1,128)} %bitcast.26), calls=%async_computation | async-start | bytes 2162688 | tf_op jit(solution)/shard_map/all_to_all | solution.py:474
  23.5 3.3 %collective-permute-start.2 = (f32[128,2048]{1,0:T(8,128)S(1)}, f32[128,2048]{1,0:T(8,128)}, u32[]{:S(2)}, u32[]{:S(2)}) collective-permute-start(f32[128,2048]{1,0:T(8,128)S(1)} %dynamic-slice_convert_fusion.1), channel_id=1, source_target_pairs={{0,1},{1,0},{2,3},{3,2},{4,5},{5,4},{6,7},{7,6},{8,9},{9,8},{10,11... | collective-permute-start | bytes 3145736 | tf_op jit(solution)/shard_map/ppermute | solution.py:486
  40.8 22.1 %all-to-all-start.1 = ((f32[64,1,4224]{2,1,0:T(1,128)}), f32[64,1,4224]{2,1,0:T(1,128)S(1)}, u32[]{:S(2)}, u32[]{:S(2)}) async-start(f32[64,1,4224]{2,1,0:T(1,128)} %bitcast.24), calls=%async_computation.1 | async-start | bytes 2162688 | tf_op jit(solution)/shard_map/all_to_all | solution.py:474
  62.9 5.3 %copy-start = (f32[64,1,4224]{2,1,0:T(1,128)}, f32[64,1,4224]{2,1,0:T(1,128)S(1)}, u32[]{:S(2)}) copy-start(f32[64,1,4224]{2,1,0:T(1,128)S(1)} %all-to-all-done.1) | copy-start | bytes 3244036
  68.3 22.7 %all-to-all-start.2 = ((f32[64,1,4224]{2,1,0:T(1,128)}), f32[64,1,4224]{2,1,0:T(1,128)S(1)}, u32[]{:S(2)}, u32[]{:S(2)}) async-start(f32[64,1,4224]{2,1,0:T(1,128)} %bitcast.27), calls=%async_computation.2 | async-start | bytes 2162688 | tf_op jit(solution)/shard_map/all_to_all | solution.py:474
  92.1 20.6 %all-to-all-start.3 = ((f32[64,1,4224]{2,1,0:T(1,128)}), f32[64,1,4224]{2,1,0:T(1,128)S(1)}, u32[]{:S(2)}, u32[]{:S(2)}) async-start(f32[64,1,4224]{2,1,0:T(1,128)} %bitcast.23), calls=%async_computation.3 | async-start | bytes 2162688 | tf_op jit(solution)/shard_map/all_to_all | solution.py:474
  97.9 5.6 %collective-permute-start.4 = (f32[128,2048]{1,0:T(8,128)S(1)}, f32[128,2048]{1,0:T(8,128)S(1)}, u32[]{:S(2)}, u32[]{:S(2)}) collective-permute-start(f32[128,2048]{1,0:T(8,128)S(1)} %convert_element_type.19), channel_id=1, source_target_pairs={{0,1},{1,0},{2,3},{3,2},{4,5},{5,4},{6,7},{7,6},{8,9},{9,8},{10,11... | collective-permute-start | bytes 3145736 | tf_op jit(solution)/shard_map/ppermute | solution.py:486
  101.2 11.5 %collective-permute-start.5 = (f32[8,128]{1,0:T(8,128)S(1)}, f32[8,128]{1,0:T(8,128)S(1)}, u32[]{:S(2)}, u32[]{:S(2)}) collective-permute-start(f32[8,128]{1,0:T(8,128)S(1)} %get-tuple-element.64.refs_6_), channel_id=1, source_target_pairs={{0,1},{1,0},{2,3},{3,2},{4,5},{5,4},{6,7},{7,6},{8,9},{9,8},{10,11... | collective-permute-start | bytes 12296 | tf_op jit(solution)/shard_map/ppermute | solution.py:486
  103.5 1.0 copy-start.1
  117.2 5.2 %copy-start.2 = (f32[128,2048]{1,0:T(8,128)S(1)}, f32[128,2048]{1,0:T(8,128)}, u32[]{:S(2)}) copy-start(f32[128,2048]{1,0:T(8,128)} %copy-done.1) | copy-start | bytes 3145732
  117.2 20.6 %all-to-all-start.4 = ((f32[64,1,4224]{2,1,0:T(1,128)}), f32[64,1,4224]{2,1,0:T(1,128)S(1)}, u32[]{:S(2)}, u32[]{:S(2)}) async-start(f32[64,1,4224]{2,1,0:T(1,128)} %bitcast.22), calls=%async_computation.4 | async-start | bytes 2162688 | tf_op jit(solution)/shard_map/all_to_all | solution.py:474
  158.2 7.9 %collective-permute-start.6 = (f32[4,2,264,128]{3,2,1,0:T(8,128)S(1)}, f32[4,2,264,128]{3,2,1,0:T(8,128)S(1)}, u32[]{:S(2)}, u32[]{:S(2)}) collective-permute-start(f32[4,2,264,128]{3,2,1,0:T(8,128)S(1)} %bitcast.19), channel_id=1, source_target_pairs={{0,1},{1,0},{2,3},{3,2},{4,5},{5,4},{6,7},{7,6},{8,9},{9,8},{10,11... | collective-permute-start | bytes 3244040 | tf_op jit(solution)/shard_map/ppermute | solution.py:486
